TPU v7x, 256 devices: a whole 4x4x8 slice. The times are simulated.
256 devices in a mesh: dp: 4 (over x), expert: 64 (over z, y, core).
Axes of the slice: x: 4, y: 4, z: 8, core: 2. Of those that a mesh axis runs over, the one named last changes fastest.
Arguments:
- tokens: bfloat16 [4096, 4096], P(('dp', 'expert')), may hold values from -6 to 6
- expert_ids: int32 [4096, 8], P(('dp', 'expert')), may hold values from 0 to 127, all different within a row
- scores: float32 [4096, 8], P(('dp', 'expert')), may hold values from 0.05 to 1
- up_weight: bfloat16 [128, 4096, 1024], P('expert', 'dp'), may hold values from -0.09375 to 0.09375
- down_weight: bfloat16 [128, 1024, 4096], P('expert', None, 'dp'), may hold values from -0.1875 to 0.1875
- swap_slot: int32 [64], replicated, may hold values from 0 to 2, as said below
Outputs:
- combined: bfloat16 [4096, 4096], P(('dp', 'expert'))
Inputs may be any that keep to these rules, and one draw needn't show every extreme that they name: `swap_slot`: the value 2 means that the index gives no slot; indices i and (i + 32) mod 64 both give a slot below 2 or both have 2.
All inputs are finite; a program needn't handle non-finite values.
Results may differ from a plain program's by a relative error of at most 0.0058.
Values may be sent and summed in bfloat16 or wider, within the bound.
No kernel may reach another device: no remote copies, remote signals or barrier semaphores. Data moves between devices by JAX's collectives and lax.ppermute only.
A program may use at most 64 MiB of HBM per device.

v0:
```python
import jax
import jax.numpy as jnp
from jax import lax
from jax.sharding import PartitionSpec as P

CAP_SLOTS = 2
HOLD_CAP = 3


def shifted(value, axis, steps):
    count = lax.axis_size(axis)
    pairs = [(source, (source + steps) % count) for source in range(count)]
    return lax.ppermute(value, axis, pairs)


def rank_among(keys):
    positions = jnp.arange(keys.shape[0], dtype=jnp.int32)
    earlier = positions[None, :] < positions[:, None]
    return jnp.sum(jnp.where((keys[:, None] == keys[None, :]) & earlier, 1, 0), axis=1)


def body(tokens, expert_ids, scores, up_weight, down_weight, swap_slot):
    holders = lax.axis_size("expert")
    groups = lax.axis_size("dp")
    device_pos = lax.axis_index("expert")
    half_way = holders // 2
    slot_count = up_weight.shape[0]
    experts_all = jnp.arange(slot_count * holders, dtype=jnp.int32)
    home_device = experts_all // slot_count
    home_slot = experts_all % slot_count
    partner = (home_device + half_way) % holders
    relocated = swap_slot[home_device] == home_slot
    holder = jnp.where(relocated, partner, home_device)
    landing = jnp.where(relocated, swap_slot[partner], home_slot)
    tok_rows, chosen = expert_ids.shape
    assign_count = tok_rows * chosen
    flat_ids = expert_ids.reshape(assign_count)
    matches = flat_ids[:, None] == experts_all[None, :]
    target = jnp.sum(jnp.where(matches, holder[None, :], 0), axis=1)
    local_slot = jnp.sum(jnp.where(matches, landing[None, :], 0), axis=1)
    holder_rank = rank_among(target)
    expert_rank = rank_among(flat_ids)
    kept_mask = (holder_rank < HOLD_CAP) & (expert_rank < CAP_SLOTS)
    slot_rows = slot_count * CAP_SLOTS
    buffer_rows = holders * slot_rows
    destination = (target * slot_count + local_slot) * CAP_SLOTS + expert_rank
    placing = (
        jnp.arange(buffer_rows, dtype=jnp.int32)[:, None] == destination[None, :]
    ) & kept_mask[None, :]
    repeated = jnp.repeat(tokens, chosen, axis=0)
    outgoing = jnp.dot(
        placing.astype(jnp.bfloat16), repeated, preferred_element_type=jnp.float32
    ).astype(jnp.bfloat16)
    model_width = tokens.shape[1]
    send_rows = outgoing.reshape(1, holders, slot_rows, model_width)
    given_slot = swap_slot[device_pos]
    pick_slot = jnp.minimum(given_slot, slot_count - 1)
    up_block = lax.dynamic_index_in_dim(up_weight, pick_slot, 0, keepdims=False)
    down_block = lax.dynamic_index_in_dim(down_weight, pick_slot, 0, keepdims=False)
    got_up, got_down = shifted((up_block, down_block), "expert", half_way)
    taken = jnp.arange(slot_count, dtype=jnp.int32) == given_slot
    up_new = jnp.where(taken[:, None, None], got_up[None], up_weight)
    down_new = jnp.where(taken[:, None, None], got_down[None], down_weight)
    rows_mid = lax.all_to_all(send_rows, "expert", split_axis=1, concat_axis=1, tiled=True)
    arrived = lax.all_to_all(rows_mid, "dp", split_axis=3, concat_axis=0, tiled=True)
    slice_width = model_width // groups
    slot_total = groups * holders * CAP_SLOTS
    by_slot = arrived.reshape(groups, holders, slot_count, CAP_SLOTS, slice_width)
    by_slot = by_slot.transpose(2, 0, 1, 3, 4).reshape(slot_count, slot_total, slice_width)
    hidden_width = up_weight.shape[2]
    terms = jnp.einsum("srd,sdh->hsr", by_slot, up_new, preferred_element_type=jnp.float32)
    shares = lax.psum_scatter(
        terms.reshape(lax.axis_size("dp") * (hidden_width // groups), slot_count * slot_total),
        "dp",
        scatter_dimension=0,
        tiled=True,
    )
    hidden_part = jax.nn.silu(shares).astype(jnp.bfloat16)
    portion = lax.all_gather(hidden_part, "dp", axis=0, tiled=True)
    grouped = portion.reshape(portion.shape[0], slot_count, slot_total)
    result = jnp.einsum("hsr,shc->src", grouped, down_new, preferred_element_type=jnp.float32)
    expert_out = result.astype(jnp.bfloat16).reshape(
        slot_count, groups, holders, CAP_SLOTS, slice_width
    )
    expert_out = expert_out.transpose(1, 2, 0, 3, 4).reshape(
        groups, holders, slot_rows, slice_width
    )
    joined = lax.all_to_all(expert_out, "dp", split_axis=0, concat_axis=3, tiled=True)
    returned = lax.all_to_all(joined, "expert", split_axis=1, concat_axis=1, tiled=True)
    returned_rows = returned.reshape(buffer_rows, model_width)
    per_assign = jnp.dot(
        placing.T.astype(jnp.bfloat16), returned_rows, preferred_element_type=jnp.float32
    )
    gate_share = 2.5 * scores / jnp.sum(scores, axis=1, keepdims=True)
    weight = jnp.where(kept_mask, gate_share.reshape(assign_count), 0.0)
    combined = jnp.sum(
        (weight[:, None] * per_assign).reshape(tok_rows, chosen, model_width), axis=1
    )
    return combined.astype(jnp.bfloat16)


def solution(mesh):
    return jax.shard_map(
        body,
        mesh=mesh,
        in_specs=(
            P(("dp", "expert"), None),
            P(("dp", "expert"), None),
            P(("dp", "expert"), None),
            P("expert", "dp", None),
            P("expert", None, "dp"),
            P(),
        ),
        out_specs=P(("dp", "expert"), None),
        check_vma=False,
    )
```

profile of v0, /device:TPU:8, one launch (start us, length us, event | category | flops | bytes accessed | tf_op | source)
XLA Modules:
  0.0 483.0 jit_solution(4672439073876705274)
XLA Ops:
  6.5 0.0 copy-start
  6.6 1.6 gather_fusion
  8.2 1.6 gather_fusion.1
  9.8 0.8 copy.32
  10.6 0.1 eq.79
  10.7 0.2 select_reduce_fusion.3
  10.9 0.2 select_reduce_fusion.2
  11.0 0.7 reduce_sum.57
  11.8 0.7 multiply_divide_fusion
  12.5 0.1 copy.33
  12.5 0.1 reshape.206
  12.7 0.0 copy-done
  12.7 0.7 convolution_convert_fusion
  13.4 2.2 reshape.208
  15.6 0.0 copy-start.2
  15.6 12.2 %all-to-all-start = ((bf16[1,64,4,4096]{3,2,0,1:T(4,128)(2,1)}), bf16[1,64,4,4096]{3,2,0,1:T(4,128)(2,1)S(1)}, u32[]{:S(2)}, u32[]{:S(2)}) async-start(bf16[1,64,4,4096]{3,2,0,1:T(4,128)(2,1)} %bitcast.42), calls=%async_computation | async-start | bytes 4194304 | tf_op jit(solution)/shard_map/all_to_all | solution.py:64
  27.8 0.0 copy-done.2
  27.9 0.6 dynamic_slice.10
  29.1 3.1 dynamic-slice_bitcast_fusion.1
  32.2 5.5 %collective-permute-start = (bf16[1024,1024]{1,0:T(8,128)(2,1)}, bf16[1024,1024]{1,0:T(8,128)(2,1)}, u32[]{:S(2)}, u32[]{:S(2)}) collective-permute-start(bf16[1024,1024]{1,0:T(8,128)(2,1)} %dynamic-slice_bitcast_fusion.1), channel_id=1, source_target_pairs={{0,32},{1,33},{2,34},{3,35},{4,36},{5,37},{6,38},{7,39},{8,40},{9,... | collective-permute-start | bytes 6291464 | tf_op jit(solution)/shard_map/ppermute | solution.py:13
  37.7 41.2 %all-to-all-done = bf16[1,64,4,4096]{3,2,0,1:T(4,128)(2,1)S(1)} async-done(((bf16[1,64,4,4096]{3,2,0,1:T(4,128)(2,1)}), bf16[1,64,4,4096]{3,2,0,1:T(4,128)(2,1)S(1)}, u32[]{:S(2)}, u32[]{:S(2)}) %all-to-all-start) | async-done | bytes 2097184 | tf_op jit(solution)/shard_map/all_to_all | solution.py:64
  78.9 5.1 %copy.35 = bf16[1,64,4,4096]{1,2,0,3:T(4,128)(2,1)} copy(bf16[1,64,4,4096]{3,2,0,1:T(4,128)(2,1)S(1)} %all-to-all-done) | data formatting | bytes 4194304 | tf_op jit(solution)/shard_map/all_to_all | solution.py:64
  84.0 5.9 %reshape.234 = bf16[4,2,131072]{2,1,0:T(2,128)(2,1)} reshape(bf16[4096,1,4,64]{3,2,1,0:T(4,128)(2,1)} %bitcast.39) | data formatting | bytes 4194304
  89.9 4.3 all-to-all-start.1
  94.2 0.0 reduce-scatter.2.cloned.1.call-start
  94.2 0.6 iota_compare_fusion.3
  94.8 24.2 %all-to-all-done.1 = bf16[4,2,131072]{2,1,0:T(2,128)(2,1)S(1)} async-done(((bf16[4,2,131072]{2,1,0:T(2,128)(2,1)}), bf16[4,2,131072]{2,1,0:T(2,128)(2,1)S(1)}, u32[]{:S(2)}, u32[]{:S(2)}) %all-to-all-start.1) | async-done | bytes 2097184 | tf_op jit(solution)/shard_map/all_to_all | solution.py:65
  119.1 4.0 reshape.235
  123.1 6.4 %copy.42 = bf16[1,64,4,4,1024]{4,3,1,2,0:T(4,128)(2,1)S(1)} copy(bf16[1,64,4,4,1024]{1,2,4,3,0:T(4,128)(2,1)} %bitcast.40) | data formatting | bytes 4194304 | tf_op jit(solution)/shard_map/all_to_all | solution.py:65
  129.5 0.6 copy.37
  130.1 2.2 copy.38
  132.3 2.3 reshape.210
  134.6 34.5 %collective-permute-done = bf16[1024,1024]{1,0:T(8,128)(2,1)} collective-permute-done((bf16[1024,1024]{1,0:T(8,128)(2,1)}, bf16[1024,1024]{1,0:T(8,128)(2,1)}, u32[]{:S(2)}, u32[]{:S(2)}) %collective-permute-start) | collective-permute-done | bytes 2097184 | tf_op jit(solution)/shard_map/ppermute | solution.py:13
  169.1 8.0 %fusion.3 = f32[2,1024,512]{1,2,0:T(8,128)} fusion(bf16[2,512,1024]{2,1,0:T(8,128)(2,1)} %reshape.210, bf16[2,1024,1024]{2,1,0:T(8,128)(2,1)} %param.9, pred[2]{0:T(512)(128)(4,1)S(1)} %iota_compare_fusion.3, bf16[1024,1024]{1,0:T(8,128)(2,1)} %collective-permute-done), kind=kOutput, calls=%fused_computation.7 | convolution fusion | flops 2149580800 | bytes 12582914 | tf_op jit(solution)/shard_map/srd,sdh->hsr/dot_general | solution.py:71
  177.1 0.0 reduce-scatter.2.cloned.1.call-update
  177.1 0.0 all-gather.2.cloned.1.call-start
  177.1 89.3 %reduce-scatter.2.cloned.1.call-done = f32[256,1024]{0,1:T(8,128)} async-done(((f32[1024,1024]{0,1:T(8,128)}), f32[256,1024]{0,1:T(8,128)}) %reduce-scatter.2.cloned.1.call-update) | async-done | bytes 1048592 | tf_op jit(solution)/shard_map/reduce_scatter | solution.py:72
  266.4 2.3 multiply_convert_fusion
  268.7 0.0 all-gather.2.cloned.1.call-update
  268.7 1.8 dynamic-slice_bitcast_fusion
  270.5 6.0 %collective-permute-start.1 = (bf16[1024,1024]{1,0:T(8,128)(2,1)S(1)}, bf16[1024,1024]{1,0:T(8,128)(2,1)S(1)}, u32[]{:S(2)}, u32[]{:S(2)}) collective-permute-start(bf16[1024,1024]{1,0:T(8,128)(2,1)S(1)} %dynamic-slice_bitcast_fusion), channel_id=1, source_target_pairs={{0,32},{1,33},{2,34},{3,35},{4,36},{5,37},{6,38},{7,39},{8,40},{9,... | collective-permute-start | bytes 6291464 | tf_op jit(solution)/shard_map/ppermute | solution.py:13
  276.5 90.7 %collective-permute-done.1 = bf16[1024,1024]{1,0:T(8,128)(2,1)S(1)} collective-permute-done((bf16[1024,1024]{1,0:T(8,128)(2,1)S(1)}, bf16[1024,1024]{1,0:T(8,128)(2,1)S(1)}, u32[]{:S(2)}, u32[]{:S(2)}) %collective-permute-start.1) | collective-permute-done | bytes 2097184 | tf_op jit(solution)/shard_map/ppermute | solution.py:13
  367.3 0.0 all-gather.2.cloned.1.call-done
  367.3 6.5 %fusion.9 = bf16[2,512,1024]{2,1,0:T(8,128)(2,1)} fusion(bf16[1024,2,512]{0,2,1:T(8,128)(2,1)} %bitcast.47, bf16[2,1024,1024]{2,1,0:T(8,128)(2,1)} %param.10, pred[2]{0:T(512)(128)(4,1)S(1)} %iota_compare_fusion.3, bf16[1024,1024]{1,0:T(8,128)(2,1)S(1)} %collective-permute-done.1), kind=kOutput, calls=%fused_computation.15 | convolution fusion | flops 2150629376 | bytes 10485762 | tf_op jit(solution)/shard_map/hsr,shc->src/dot_general | solution.py:81
  373.8 2.7 reshape.213
  376.6 0.6 copy.39
  377.2 19.9 %all_to_all.43 = bf16[4,64,4,1024]{3,1,2,0:T(8,128)(2,1)S(1)} all-to-all(bf16[4,64,4,1024]{3,1,2,0:T(8,128)(2,1)S(1)} %bitcast.44), channel_id=1, replica_groups=mesh['dp'=4,'expert'=64] {'dp'}, dimensions={0} | all-to-all | bytes 4194304 | tf_op jit(solution)/shard_map/all_to_all | solution.py:88
  397.1 1.6 copy.43
  398.8 2.8 reshape.233
  401.6 69.3 %all_to_all.44 = bf16[1,64,4,4096]{3,2,0,1:T(4,128)(2,1)S(1)} all-to-all(bf16[1,64,4,4096]{3,2,0,1:T(4,128)(2,1)} %reshape.233), channel_id=1, replica_groups=mesh['dp'=4,'expert'=64] {'expert'}, dimensions={1} | all-to-all | bytes 4194304 | tf_op jit(solution)/shard_map/all_to_all | solution.py:89
  470.9 0.0 copy-start.1
  470.9 2.1 reshape.215
  473.0 3.2 fusion.12
  476.2 0.0 copy-done.1
  (6 shorter events, 0.0 us)
Async XLA Ops:
  6.5 6.1 %copy-start = (bf16[16,4096]{1,0:T(8,128)(2,1)S(1)}, bf16[16,4096]{1,0:T(8,128)(2,1)}, u32[]{:S(2)}) copy-start(bf16[16,4096]{1,0:T(8,128)(2,1)} %param.6) | copy-start | bytes 393220
  15.6 12.2 %copy-start.2 = (s32[64]{0:T(128)S(1)}, s32[64]{0:T(128)}, u32[]{:S(2)}) copy-start(s32[64]{0:T(128)} %param.11) | copy-start | bytes 772
  15.6 63.3 %all-to-all-start = ((bf16[1,64,4,4096]{3,2,0,1:T(4,128)(2,1)}), bf16[1,64,4,4096]{3,2,0,1:T(4,128)(2,1)S(1)}, u32[]{:S(2)}, u32[]{:S(2)}) async-start(bf16[1,64,4,4096]{3,2,0,1:T(4,128)(2,1)} %bitcast.42), calls=%async_computation | async-start | bytes 4194304 | tf_op jit(solution)/shard_map/all_to_all | solution.py:64
  32.2 136.9 %collective-permute-start = (bf16[1024,1024]{1,0:T(8,128)(2,1)}, bf16[1024,1024]{1,0:T(8,128)(2,1)}, u32[]{:S(2)}, u32[]{:S(2)}) collective-permute-start(bf16[1024,1024]{1,0:T(8,128)(2,1)} %dynamic-slice_bitcast_fusion.1), channel_id=1, source_target_pairs={{0,32},{1,33},{2,34},{3,35},{4,36},{5,37},{6,38},{7,39},{8,40},{9,... | collective-permute-start | bytes 6291464 | tf_op jit(solution)/shard_map/ppermute | solution.py:13
  89.9 29.2 %all-to-all-start.1 = ((bf16[4,2,131072]{2,1,0:T(2,128)(2,1)}), bf16[4,2,131072]{2,1,0:T(2,128)(2,1)S(1)}, u32[]{:S(2)}, u32[]{:S(2)}) async-start(bf16[4,2,131072]{2,1,0:T(2,128)(2,1)} %reshape.234), calls=%async_computation.1 | async-start | bytes 4194304 | tf_op jit(solution)/shard_map/all_to_all | solution.py:65
  94.2 172.2 %reduce-scatter.2.cloned.1.call-start = ((), (), s32[]{:S(2)}) async-start(), calls=%async_computation.5 | async-start | bytes 5242880 | tf_op jit(solution)/shard_map/reduce_scatter | solution.py:72
  177.1 190.2 %all-gather.2.cloned.1.call-start = ((), (), s32[]{:S(2)}) async-start(), calls=%async_computation.6 | async-start | bytes 2621440 | tf_op jit(solution)/shard_map/all_gather | solution.py:79
  270.5 96.7 %collective-permute-start.1 = (bf16[1024,1024]{1,0:T(8,128)(2,1)S(1)}, bf16[1024,1024]{1,0:T(8,128)(2,1)S(1)}, u32[]{:S(2)}, u32[]{:S(2)}) collective-permute-start(bf16[1024,1024]{1,0:T(8,128)(2,1)S(1)} %dynamic-slice_bitcast_fusion), channel_id=1, source_target_pairs={{0,32},{1,33},{2,34},{3,35},{4,36},{5,37},{6,38},{7,39},{8,40},{9,... | collective-permute-start | bytes 6291464 | tf_op jit(solution)/shard_map/ppermute | solution.py:13
  470.9 5.2 %copy-start.1 = (bf16[16,4096]{1,0:T(8,128)(2,1)S(1)}, bf16[16,4096]{1,0:T(8,128)(2,1)}, u32[]{:S(2)}) copy-start(bf16[16,4096]{1,0:T(8,128)(2,1)} %param.6) | copy-start | bytes 393220
Sparse Core Ops, SparseCore 0:
  177.2 89.1 reduce-scatter.1
  268.9 36.2 all-gather.1
where the time goes:
time: 484 us; the launch traced here: 483 us
  waiting for transfers between devices  280 us (58%)
  blocking collectives  89.3 us (18%)
  local copies, waits for them, and re-layouts  48.3 us (10%)
  starting transfers between devices  28 us (6%)
  matrix products  18.4 us (4%)
  between operations  14.2 us (3%)
    ppermute x2, waiting for transfers between devices, shifted(): return lax.ppermute(value, axis, pairs)  125 us
    reduce_scatter x1, waiting for transfers between devices, body(): lax.psum_scatter(terms.reshape(lax.axis_size('dp') * (hidden_width // gro...  89.3 us
    all_to_all x1, blocking collectives, body(): lax.all_to_all(joined, 'expert', split_axis=1, concat_axis=1, tiled=True)  69.3 us
    all_to_all x1, waiting for transfers between devices, body(): lax.all_to_all(send_rows, 'expert', split_axis=1, concat_axis=1, tiled=True)  41.2 us
    all_to_all x1, waiting for transfers between devices, body(): lax.all_to_all(rows_mid, 'dp', split_axis=3, concat_axis=0, tiled=True)  24.2 us
    all_to_all x1, blocking collectives, body(): lax.all_to_all(expert_out, 'dp', split_axis=0, concat_axis=3, tiled=True)  19.9 us
    all_to_all x1, starting transfers between devices, body(): lax.all_to_all(send_rows, 'expert', split_axis=1, concat_axis=1, tiled=True)  12.2 us
    ppermute x2, starting transfers between devices, shifted(): return lax.ppermute(value, axis, pairs)  11.5 us
  transfers between devices with their start and end apart: 6, of which 5 were waited for; matrix products, arithmetic and copies ran while one was open for 7% of the time, Pallas kernels for 0%

commit v1 on v0

v1 whole, which is shorter than its diff:
```python
import jax
import jax.numpy as jnp
from jax import lax
from jax.sharding import Mesh, PartitionSpec as P

CAP_SLOTS = 2
HOLD_CAP = 3
BF = jnp.bfloat16
F32 = jnp.float32


def slot_weights(expert_ids, scores, swap_slot, experts):
    tok_rows, chosen = expert_ids.shape
    holders = swap_slot.shape[0]
    per_dev = experts // holders
    ids = jnp.arange(experts, dtype=jnp.int32)
    home = ids // per_dev
    swap_of = jnp.broadcast_to(swap_slot[:, None], (holders, per_dev)).reshape(experts)
    holder = jnp.where(swap_of == ids % per_dev, (home + holders // 2) % holders, home)
    picks = expert_ids[:, :, None] == ids[None, None, :]
    order = jnp.arange(1, chosen + 1, dtype=jnp.int32)[None, :, None]
    place = jnp.sum(jnp.where(picks, order, 0), axis=1)
    gate = 2.5 * scores / jnp.sum(scores, axis=1, keepdims=True)
    share = jnp.sum(jnp.where(picks, gate[:, :, None], 0.0), axis=1)
    picked = place > 0
    same = holder[:, None] == holder[None, :]
    mate = same & (ids[:, None] != ids[None, :])
    before = jnp.tril(jnp.ones((tok_rows, tok_rows), F32), -1)
    ones = picked.astype(F32)
    in_rows = jnp.dot(ones, same.astype(F32))
    mate_place = jnp.dot(place.astype(F32), mate.astype(F32))
    earlier = (mate_place > 0) & (mate_place < place.astype(F32))
    holder_rank = jnp.dot(before, in_rows) + earlier.astype(F32)
    expert_rank = jnp.dot(before, ones)
    kept = picked & (holder_rank < HOLD_CAP)
    return [jnp.where(kept & (expert_rank == rank), share, 0.0) for rank in range(CAP_SLOTS)]


def body(tokens, expert_ids, scores, up_weight, down_weight, swap_slot):
    groups = lax.axis_size("dp")
    planes = lax.axis_size("z")
    cells = lax.axis_size("yc")
    tok_rows, width = tokens.shape
    per_dev = up_weight.shape[0]
    experts = planes * cells * per_dev
    part_width = width // groups
    blocks = groups * planes
    plane_experts = cells * per_dev
    weights = slot_weights(expert_ids, scores, swap_slot, experts)
    high = [lax.reduce_precision(w, 8, 7) for w in weights]
    low = [w - h for w, h in zip(weights, high)]
    meta = jnp.stack(high + low, axis=1).astype(BF)
    meta = meta.reshape(tok_rows, 2 * CAP_SLOTS, planes, plane_experts).transpose(2, 0, 1, 3)
    meta_used = 2 * CAP_SLOTS * plane_experts
    meta = meta.reshape(planes, tok_rows, meta_used)
    meta_cols = -(-meta_used // 128) * 128
    meta = jnp.pad(meta, ((0, 0), (0, 0), (0, meta_cols - meta_used)))
    feats = tokens.reshape(tok_rows, groups, part_width).transpose(1, 0, 2)
    payload = jnp.concatenate(
        [
            jnp.broadcast_to(feats[:, None], (groups, planes, tok_rows, part_width)),
            jnp.broadcast_to(meta[None], (groups, planes, tok_rows, meta_cols)),
        ],
        axis=-1,
    ).reshape(blocks, tok_rows, part_width + meta_cols)
    spread = lax.all_to_all(payload, ("dp", "z"), 0, 0, tiled=True)
    spread = spread.reshape(blocks * tok_rows, part_width + meta_cols)
    tok = spread[:, :part_width]
    info = spread[:, part_width:]
    cell_rows = CAP_SLOTS * blocks
    slots = cells * cell_rows
    slot = jnp.arange(slots, dtype=jnp.int32)
    slot_cell = slot // cell_rows
    slot_rank = (slot % cell_rows) // blocks
    slot_block = slot % blocks
    own = (jnp.arange(blocks * tok_rows, dtype=jnp.int32) // tok_rows)[:, None] == slot_block[None, :]
    columns = jnp.arange(meta_cols, dtype=jnp.int32)[:, None]
    total = jnp.zeros((blocks * tok_rows, part_width), F32)
    for s in range(per_dev):
        source = slot_rank * plane_experts + slot_cell * per_dev + s
        pick_high = (columns == source[None, :]).astype(BF)
        pick_low = (columns == source[None, :] + CAP_SLOTS * plane_experts).astype(BF)
        spread_high = jnp.where(own, jnp.dot(info, pick_high, preferred_element_type=F32), 0.0).astype(BF)
        spread_low = jnp.where(own, jnp.dot(info, pick_low, preferred_element_type=F32), 0.0).astype(BF)
        rows = lax.dot_general(
            (spread_high > 0).astype(BF), tok, (((0,), (0,)), ((), ())), preferred_element_type=F32
        ).astype(BF)
        arrived = lax.all_to_all(rows.reshape(cells, cell_rows, part_width), "yc", 0, 0, tiled=True)
        arrived = arrived.reshape(slots, part_width)
        terms = jnp.dot(arrived, up_weight[s], preferred_element_type=F32).astype(BF)
        hidden_width = terms.shape[1]
        shares = lax.all_to_all(terms.reshape(groups, slots // groups, hidden_width), "dp", 0, 0, tiled=True)
        hidden = jax.nn.silu(jnp.sum(shares.astype(F32), axis=0)).astype(BF)
        copies = jnp.broadcast_to(hidden[None], (groups,) + hidden.shape)
        whole = lax.all_to_all(copies, "dp", 0, 0, tiled=True).reshape(slots, hidden_width)
        result = jnp.dot(whole, down_weight[s], preferred_element_type=F32).astype(BF)
        back = lax.all_to_all(result.reshape(cells, cell_rows, part_width), "yc", 0, 0, tiled=True)
        back = back.reshape(slots, part_width)
        total = total + jnp.dot(spread_high, back, preferred_element_type=F32)
        total = total + jnp.dot(spread_low, back, preferred_element_type=F32)
    sums = total.astype(BF).reshape(blocks, tok_rows, part_width)
    parts = lax.all_to_all(sums, ("dp", "z"), 0, 0, tiled=True)
    parts = jnp.sum(parts.reshape(groups, planes, tok_rows, part_width).astype(F32), axis=1)
    return parts.astype(BF).transpose(1, 0, 2).reshape(tok_rows, width)


def solution(mesh):
    groups, holders = mesh.devices.shape
    cells = 8 if holders % 8 == 0 else holders
    grid = Mesh(mesh.devices.reshape(groups, holders // cells, cells), ("dp", "z", "yc"))
    every = ("dp", "z", "yc")
    return jax.shard_map(
        body,
        mesh=grid,
        in_specs=(
            P(every, None),
            P(every, None),
            P(every, None),
            P(("z", "yc"), "dp", None),
            P(("z", "yc"), None, "dp"),
            P(),
        ),
        out_specs=P(every, None),
        check_vma=False,
    )
```

time: 484 us -> 246 us (0.51)
  waiting for transfers between devices: 280 us -> 120 us
  blocking collectives: 89.3 us -> 33.2 us
  local copies, waits for them, and re-layouts: 48.3 us -> 8.32 us
  starting transfers between devices: 28 us -> 45 us
  matrix products: 18.4 us -> 33 us
  between operations: 14.2 us -> 0.28 us
    ppermute x2 -> x0, waiting for transfers between devices: 125 us -> none  [shifted(): return lax.ppermute(value, axis, pairs)]
    reduce_scatter x1 -> x0, waiting for transfers between devices: 89.3 us -> none  [body(): lax.psum_scatter(terms.reshape(lax.axis_size('dp') * (hidden_width // gro...]
    all_to_all x2 -> x1, blocking collectives: 89.3 us -> 33.2 us  [body(): parts = lax.all_to_all(sums, ('dp', 'z'), 0, 0, tiled=True)]
    all_to_all x2 -> x9, waiting for transfers between devices: 65.5 us -> 120 us  [the longest x1 31.3 us: body(): spread = lax.all_to_all(payload, ('dp', 'z'), 0, 0, tiled=True)]
    all_to_all x2 -> x9, starting transfers between devices: 16.5 us -> 45 us  [the longest x1 11.3 us: body(): spread = lax.all_to_all(payload, ('dp', 'z'), 0, 0, tiled=True)]
    all_to_all x5 -> x0, local copies, waits for them, and re-layouts: 16.6 us -> none  [the longest x2 7.05 us: body(): lax.all_to_all(rows_mid, 'dp', split_axis=3, concat_axis=0, tiled=True)]
    dot_general x4 -> x15, matrix products: 18.4 us -> 33 us  [the longest x2 8.02 us: body(): jnp.dot(arrived, up_weight[s], preferred_element_type=F32).astype(BF)]
    ppermute x2 -> x0, starting transfers between devices: 11.5 us -> none  [shifted(): return lax.ppermute(value, axis, pairs)]
  transfers between devices with their start and end apart: 6 -> 9, of which waited for: 5 -> 9; matrix products, arithmetic and copies ran while one was open for 7% -> 10% of each run, Pallas kernels for 0% -> 0%
where the time goes in v1:
time: 246 us; the launch traced here: 244 us
  waiting for transfers between devices  120 us (49%)
  starting transfers between devices  45 us (18%)
  blocking collectives  33.2 us (13%)
  matrix products  33 us (13%)
  local copies, waits for them, and re-layouts  8.32 us (3%)
  other arithmetic  4.01 us (2%)
    all_to_all x1, blocking collectives, body(): parts = lax.all_to_all(sums, ('dp', 'z'), 0, 0, tiled=True)  33.2 us
    all_to_all x1, waiting for transfers between devices, body(): spread = lax.all_to_all(payload, ('dp', 'z'), 0, 0, tiled=True)  31.3 us
    all_to_all x2, waiting for transfers between devices, body(): lax.all_to_all(terms.reshape(groups, slots // groups, hidden_width), 'dp'...  24.7 us
    all_to_all x2, waiting for transfers between devices, body(): lax.all_to_all(rows.reshape(cells, cell_rows, part_width), 'yc', 0, 0, ti...  23 us
    all_to_all x2, waiting for transfers between devices, body(): lax.all_to_all(copies, 'dp', 0, 0, tiled=True).reshape(slots, hidden_width)  21.4 us
    all_to_all x2, waiting for transfers between devices, body(): lax.all_to_all(result.reshape(cells, cell_rows, part_width), 'yc', 0, 0,...  19.8 us
    all_to_all x1, starting transfers between devices, body(): spread = lax.all_to_all(payload, ('dp', 'z'), 0, 0, tiled=True)  11.3 us
    all_to_all x2, starting transfers between devices, body(): lax.all_to_all(rows.reshape(cells, cell_rows, part_width), 'yc', 0, 0, ti...  9.84 us
  transfers between devices with their start and end apart: 9, of which 9 were waited for; matrix products, arithmetic and copies ran while one was open for 10% of the time, Pallas kernels for 0%

profile of v1, /device:TPU:8, one launch (start us, length us, event | category | flops | bytes accessed | tf_op | source)
XLA Modules:
  0.0 244.2 jit_solution(12116939273398473342)
XLA Ops:
  0.0 0.8 copy.33
  0.8 0.7 broadcast_in_dim.55
  1.5 0.1 reshape.255
  1.6 0.1 select_reduce_fusion.1
  1.8 0.2 fusion.63
  2.0 0.2 fusion.70
  2.1 0.7 reduce_sum.58
  2.9 0.7 multiply_divide_fusion
  3.5 0.1 copy.34
  3.6 0.1 select_reduce_fusion
  3.7 0.3 reduce-precision_convert_fusion.1
  4.1 0.1 stack.15
  4.2 0.1 copy.35
  4.2 0.1 stack.16
  4.3 0.1 copy.36
  4.4 0.1 stack.17
  4.5 0.1 copy.37
  4.5 0.1 stack.18
  4.7 0.4 maximum_bitcast_fusion
  5.1 0.1 reshape.256
  5.2 1.0 reshape.254
  6.3 0.1 broadcast_in_dim.50
  6.4 1.1 pad_maximum_fusion
  7.5 11.3 %all-to-all-start = ((bf16[32,16,1152]{2,1,0:T(8,128)(2,1)}), bf16[32,16,1152]{2,1,0:T(8,128)(2,1)S(1)}, u32[]{:S(2)}, u32[]{:S(2)}) async-start(bf16[32,16,1152]{2,1,0:T(8,128)(2,1)} %bitcast.2), calls=%async_computation | async-start | bytes 2359296 | tf_op jit(solution)/shard_map/all_to_all | solution.py:66
  18.9 31.3 %all-to-all-done = bf16[32,16,1152]{2,1,0:T(8,128)(2,1)S(1)} async-done(((bf16[32,16,1152]{2,1,0:T(8,128)(2,1)}), bf16[32,16,1152]{2,1,0:T(8,128)(2,1)S(1)}, u32[]{:S(2)}, u32[]{:S(2)}) %all-to-all-start) | async-done | bytes 1179680 | tf_op jit(solution)/shard_map/all_to_all | solution.py:66
  50.2 0.3 fusion.24
  50.5 0.9 copy-done.3
  51.4 1.7 convolution_convert_fusion.1
  53.1 4.9 %all-to-all-start.1 = ((bf16[8,64,1024]{2,1,0:T(8,128)(2,1)}), bf16[8,64,1024]{2,1,0:T(8,128)(2,1)S(1)}, u32[]{:S(2)}, u32[]{:S(2)}) async-start(bf16[8,64,1024]{2,1,0:T(8,128)(2,1)} %bitcast.4), calls=%async_computation.1 | async-start | bytes 2097152 | tf_op jit(solution)/shard_map/all_to_all | solution.py:88
  58.0 0.3 fusion.26
  58.4 1.8 convolution_convert_fusion
  60.1 12.3 %all-to-all-done.1 = bf16[8,64,1024]{2,1,0:T(8,128)(2,1)S(1)} async-done(((bf16[8,64,1024]{2,1,0:T(8,128)(2,1)}), bf16[8,64,1024]{2,1,0:T(8,128)(2,1)S(1)}, u32[]{:S(2)}, u32[]{:S(2)}) %all-to-all-start.1) | async-done | bytes 1048608 | tf_op jit(solution)/shard_map/all_to_all | solution.py:88
  72.5 4.9 %all-to-all-start.5 = ((bf16[8,64,1024]{2,1,0:T(8,128)(2,1)}), bf16[8,64,1024]{2,1,0:T(8,128)(2,1)S(1)}, u32[]{:S(2)}, u32[]{:S(2)}) async-start(bf16[8,64,1024]{2,1,0:T(8,128)(2,1)} %bitcast.72), calls=%async_computation.5 | async-start | bytes 2097152 | tf_op jit(solution)/shard_map/all_to_all | solution.py:88
  77.4 3.8 %fusion.12 = bf16[512,1024]{1,0:T(8,128)(2,1)} fusion(bf16[512,1024]{1,0:T(8,128)(2,1)S(1)} %bitcast.65, bf16[2,1024,1024]{2,1,0:T(8,128)(2,1)} %param.9), kind=kOutput, calls=%fused_computation.19 | convolution fusion | flops 1074266112 | bytes 4194304 | tf_op jit(solution)/shard_map/dot_general | solution.py:90
  81.2 10.7 %all-to-all-done.5 = bf16[8,64,1024]{2,1,0:T(8,128)(2,1)S(1)} async-done(((bf16[8,64,1024]{2,1,0:T(8,128)(2,1)}), bf16[8,64,1024]{2,1,0:T(8,128)(2,1)S(1)}, u32[]{:S(2)}, u32[]{:S(2)}) %all-to-all-start.5) | async-done | bytes 1048608 | tf_op jit(solution)/shard_map/all_to_all | solution.py:88
  91.9 1.0 copy-done.2
  92.9 3.5 %all-to-all-start.2 = ((bf16[4,128,1024]{2,1,0:T(8,128)(2,1)}), bf16[4,128,1024]{2,1,0:T(8,128)(2,1)S(1)}, u32[]{:S(2)}, u32[]{:S(2)}) async-start(bf16[4,128,1024]{2,1,0:T(8,128)(2,1)} %bitcast.70), calls=%async_computation.2 | async-start | bytes 2097152 | tf_op jit(solution)/shard_map/all_to_all | solution.py:92
  96.4 4.2 %fusion.18 = bf16[512,1024]{1,0:T(8,128)(2,1)} fusion(bf16[512,1024]{1,0:T(8,128)(2,1)} %bitcast.67, bf16[2,1024,1024]{2,1,0:T(8,128)(2,1)} %param.9), kind=kOutput, calls=%fused_computation.21 | convolution fusion | flops 1074266112 | bytes 4194304 | tf_op jit(solution)/shard_map/dot_general | solution.py:90
  100.6 10.8 %all-to-all-done.2 = bf16[4,128,1024]{2,1,0:T(8,128)(2,1)S(1)} async-done(((bf16[4,128,1024]{2,1,0:T(8,128)(2,1)}), bf16[4,128,1024]{2,1,0:T(8,128)(2,1)S(1)}, u32[]{:S(2)}, u32[]{:S(2)}) %all-to-all-start.2) | async-done | bytes 1048608 | tf_op jit(solution)/shard_map/all_to_all | solution.py:92
  111.5 3.5 %all-to-all-start.6 = ((bf16[4,128,1024]{2,1,0:T(8,128)(2,1)}), bf16[4,128,1024]{2,1,0:T(8,128)(2,1)S(1)}, u32[]{:S(2)}, u32[]{:S(2)}) async-start(bf16[4,128,1024]{2,1,0:T(8,128)(2,1)} %bitcast.69), calls=%async_computation.6 | async-start | bytes 2097152 | tf_op jit(solution)/shard_map/all_to_all | solution.py:92
  115.0 0.2 convert_reduce_fusion.1
  115.2 0.1 multiply_convert_fusion.1
  115.4 13.8 %all-to-all-done.6 = bf16[4,128,1024]{2,1,0:T(8,128)(2,1)S(1)} async-done(((bf16[4,128,1024]{2,1,0:T(8,128)(2,1)}), bf16[4,128,1024]{2,1,0:T(8,128)(2,1)S(1)}, u32[]{:S(2)}, u32[]{:S(2)}) %all-to-all-start.6) | async-done | bytes 1048608 | tf_op jit(solution)/shard_map/all_to_all | solution.py:92
  129.2 1.1 broadcast_in_dim.97
  130.3 3.5 %all-to-all-start.3 = ((bf16[4,128,1024]{2,1,0:T(8,128)(2,1)}), bf16[4,128,1024]{2,1,0:T(8,128)(2,1)S(1)}, u32[]{:S(2)}, u32[]{:S(2)}) async-start(bf16[4,128,1024]{2,1,0:T(8,128)(2,1)} %broadcast_in_dim.97), calls=%async_computation.3 | async-start | bytes 2097152 | tf_op jit(solution)/shard_map/all_to_all | solution.py:95
  133.8 0.2 convert_reduce_fusion
  134.0 0.1 multiply_convert_fusion
  134.2 13.0 %all-to-all-done.3 = bf16[4,128,1024]{2,1,0:T(8,128)(2,1)S(1)} async-done(((bf16[4,128,1024]{2,1,0:T(8,128)(2,1)}), bf16[4,128,1024]{2,1,0:T(8,128)(2,1)S(1)}, u32[]{:S(2)}, u32[]{:S(2)}) %all-to-all-start.3) | async-done | bytes 1048608 | tf_op jit(solution)/shard_map/all_to_all | solution.py:95
  147.2 1.2 broadcast_in_dim.98
  148.3 3.5 %all-to-all-start.7 = ((bf16[4,128,1024]{2,1,0:T(8,128)(2,1)}), bf16[4,128,1024]{2,1,0:T(8,128)(2,1)S(1)}, u32[]{:S(2)}, u32[]{:S(2)}) async-start(bf16[4,128,1024]{2,1,0:T(8,128)(2,1)} %broadcast_in_dim.98), calls=%async_computation.7 | async-start | bytes 2097152 | tf_op jit(solution)/shard_map/all_to_all | solution.py:95
  151.8 3.8 %fusion.15 = bf16[512,1024]{1,0:T(8,128)(2,1)} fusion(bf16[512,1024]{1,0:T(8,128)(2,1)S(1)} %bitcast.64, bf16[2,1024,1024]{2,1,0:T(8,128)(2,1)} %param.10), kind=kOutput, calls=%fused_computation.20 | convolution fusion | flops 1074266112 | bytes 4194304 | tf_op jit(solution)/shard_map/dot_general | solution.py:96
  155.7 8.4 %all-to-all-done.7 = bf16[4,128,1024]{2,1,0:T(8,128)(2,1)S(1)} async-done(((bf16[4,128,1024]{2,1,0:T(8,128)(2,1)}), bf16[4,128,1024]{2,1,0:T(8,128)(2,1)S(1)}, u32[]{:S(2)}, u32[]{:S(2)}) %all-to-all-start.7) | async-done | bytes 1048608 | tf_op jit(solution)/shard_map/all_to_all | solution.py:95
  164.0 4.9 %all-to-all-start.4 = ((bf16[8,64,1024]{2,1,0:T(8,128)(2,1)}), bf16[8,64,1024]{2,1,0:T(8,128)(2,1)S(1)}, u32[]{:S(2)}, u32[]{:S(2)}) async-start(bf16[8,64,1024]{2,1,0:T(8,128)(2,1)} %bitcast.71), calls=%async_computation.4 | async-start | bytes 2097152 | tf_op jit(solution)/shard_map/all_to_all | solution.py:97
  168.9 3.8 %fusion.21 = bf16[512,1024]{1,0:T(8,128)(2,1)} fusion(bf16[512,1024]{1,0:T(8,128)(2,1)S(1)} %bitcast.68, bf16[2,1024,1024]{2,1,0:T(8,128)(2,1)} %param.10), kind=kOutput, calls=%fused_computation.22 | convolution fusion | flops 1074266112 | bytes 4194304 | tf_op jit(solution)/shard_map/dot_general | solution.py:96
  172.8 10.7 %all-to-all-done.4 = bf16[8,64,1024]{2,1,0:T(8,128)(2,1)S(1)} async-done(((bf16[8,64,1024]{2,1,0:T(8,128)(2,1)}), bf16[8,64,1024]{2,1,0:T(8,128)(2,1)S(1)}, u32[]{:S(2)}, u32[]{:S(2)}) %all-to-all-start.4) | async-done | bytes 1048608 | tf_op jit(solution)/shard_map/all_to_all | solution.py:97
  183.5 4.9 %all-to-all-start.8 = ((bf16[8,64,1024]{2,1,0:T(8,128)(2,1)}), bf16[8,64,1024]{2,1,0:T(8,128)(2,1)S(1)}, u32[]{:S(2)}, u32[]{:S(2)}) async-start(bf16[8,64,1024]{2,1,0:T(8,128)(2,1)} %bitcast.66), calls=%async_computation.8 | async-start | bytes 2097152 | tf_op jit(solution)/shard_map/all_to_all | solution.py:97
  188.4 2.2 fusion.28
  190.6 3.1 %fusion.114 = f32[512,1024]{1,0:T(8,128)} fusion(bf16[512,512]{1,0:T(8,128)(2,1)} %copy-done.3, bf16[512,1024]{1,0:T(8,128)(2,1)S(1)} %bitcast.56), kind=kOutput, calls=%fused_computation.152 | convolution fusion | flops 536870912 | bytes 3670016 | tf_op jit(solution)/shard_map/dot_general | solution.py:99
  193.7 9.2 %all-to-all-done.8 = bf16[8,64,1024]{2,1,0:T(8,128)(2,1)S(1)} async-done(((bf16[8,64,1024]{2,1,0:T(8,128)(2,1)}), bf16[8,64,1024]{2,1,0:T(8,128)(2,1)S(1)}, u32[]{:S(2)}, u32[]{:S(2)}) %all-to-all-start.8) | async-done | bytes 1048608 | tf_op jit(solution)/shard_map/all_to_all | solution.py:97
  202.9 3.1 %fusion.115 = f32[512,1024]{1,0:T(8,128)} fusion(bf16[512,512]{1,0:T(8,128)(2,1)} %copy-done.4, bf16[512,1024]{1,0:T(8,128)(2,1)S(1)} %bitcast.53), kind=kOutput, calls=%fused_computation.153 | convolution fusion | flops 536870912 | bytes 3670016 | tf_op jit(solution)/shard_map/dot_general | solution.py:99
  205.9 4.1 %add_convert_fusion = bf16[512,1024]{1,0:T(8,128)(2,1)} fusion(f32[512,1024]{1,0:T(8,128)} %fusion.115, f32[512,1024]{1,0:T(8,128)S(1)} %copy-done, f32[512,1024]{1,0:T(8,128)} %fusion.28, bf16[512,1024]{1,0:T(8,128)(2,1)S(1)} %bitcast.54, s32[512]{0:T(512)S(1)} %get-tuple-element.9, s32[512]{0:T(512)S(1)} %get-tuple-element.10, ...), kind=kOutput, calls=%fused_computation.8 | convolution fusion | flops 606928896 | bytes 8525824 | tf_op jit(solution)/shard_map/dot_general | solution.py:100
  210.1 33.2 %all_to_all.50 = bf16[32,16,1024]{2,1,0:T(8,128)(2,1)S(1)} all-to-all(bf16[32,16,1024]{2,1,0:T(8,128)(2,1)} %bitcast.57), channel_id=1, replica_groups=mesh['dp'=4,'z'=8,'yc'=8] {'dp','z'}, dimensions={0} | all-to-all | bytes 2097152 | tf_op jit(solution)/shard_map/all_to_all | solution.py:102
  243.3 0.2 bitcast_reduce_fusion
  243.5 0.7 copy.40
  (20 shorter events, 0.2 us)
Async XLA Ops:
  7.5 42.7 %all-to-all-start = ((bf16[32,16,1152]{2,1,0:T(8,128)(2,1)}), bf16[32,16,1152]{2,1,0:T(8,128)(2,1)S(1)}, u32[]{:S(2)}, u32[]{:S(2)}) async-start(bf16[32,16,1152]{2,1,0:T(8,128)(2,1)} %bitcast.2), calls=%async_computation | async-start | bytes 2359296 | tf_op jit(solution)/shard_map/all_to_all | solution.py:66
  50.2 138.2 %copy-start.1 = (bf16[32,16,1152]{2,1,0:T(8,128)(2,1)}, bf16[32,16,1152]{2,1,0:T(8,128)(2,1)S(1)}, u32[]{:S(2)}) copy-start(bf16[32,16,1152]{2,1,0:T(8,128)(2,1)S(1)} %all-to-all-done) | copy-start | bytes 3538948
  50.5 0.9 copy-start.3
  53.1 19.4 %all-to-all-start.1 = ((bf16[8,64,1024]{2,1,0:T(8,128)(2,1)}), bf16[8,64,1024]{2,1,0:T(8,128)(2,1)S(1)}, u32[]{:S(2)}, u32[]{:S(2)}) async-start(bf16[8,64,1024]{2,1,0:T(8,128)(2,1)} %bitcast.4), calls=%async_computation.1 | async-start | bytes 2097152 | tf_op jit(solution)/shard_map/all_to_all | solution.py:88
  58.3 14.1 %copy-start.4 = (bf16[512,512]{1,0:T(8,128)(2,1)}, bf16[512,512]{1,0:T(8,128)(2,1)S(1)}, u32[]{:S(2)}) copy-start(bf16[512,512]{1,0:T(8,128)(2,1)S(1)} %fusion.26) | copy-start | bytes 1572868
  72.5 19.4 %all-to-all-start.5 = ((bf16[8,64,1024]{2,1,0:T(8,128)(2,1)}), bf16[8,64,1024]{2,1,0:T(8,128)(2,1)S(1)}, u32[]{:S(2)}, u32[]{:S(2)}) async-start(bf16[8,64,1024]{2,1,0:T(8,128)(2,1)} %bitcast.72), calls=%async_computation.5 | async-start | bytes 2097152 | tf_op jit(solution)/shard_map/all_to_all | solution.py:88
  91.9 1.0 copy-start.2
  92.9 18.6 %all-to-all-start.2 = ((bf16[4,128,1024]{2,1,0:T(8,128)(2,1)}), bf16[4,128,1024]{2,1,0:T(8,128)(2,1)S(1)}, u32[]{:S(2)}, u32[]{:S(2)}) async-start(bf16[4,128,1024]{2,1,0:T(8,128)(2,1)} %bitcast.70), calls=%async_computation.2 | async-start | bytes 2097152 | tf_op jit(solution)/shard_map/all_to_all | solution.py:92
  111.5 17.7 %all-to-all-start.6 = ((bf16[4,128,1024]{2,1,0:T(8,128)(2,1)}), bf16[4,128,1024]{2,1,0:T(8,128)(2,1)S(1)}, u32[]{:S(2)}, u32[]{:S(2)}) async-start(bf16[4,128,1024]{2,1,0:T(8,128)(2,1)} %bitcast.69), calls=%async_computation.6 | async-start | bytes 2097152 | tf_op jit(solution)/shard_map/all_to_all | solution.py:92
  130.3 16.9 %all-to-all-start.3 = ((bf16[4,128,1024]{2,1,0:T(8,128)(2,1)}), bf16[4,128,1024]{2,1,0:T(8,128)(2,1)S(1)}, u32[]{:S(2)}, u32[]{:S(2)}) async-start(bf16[4,128,1024]{2,1,0:T(8,128)(2,1)} %broadcast_in_dim.97), calls=%async_computation.3 | async-start | bytes 2097152 | tf_op jit(solution)/shard_map/all_to_all | solution.py:95
  148.3 15.7 %all-to-all-start.7 = ((bf16[4,128,1024]{2,1,0:T(8,128)(2,1)}), bf16[4,128,1024]{2,1,0:T(8,128)(2,1)S(1)}, u32[]{:S(2)}, u32[]{:S(2)}) async-start(bf16[4,128,1024]{2,1,0:T(8,128)(2,1)} %broadcast_in_dim.98), calls=%async_computation.7 | async-start | bytes 2097152 | tf_op jit(solution)/shard_map/all_to_all | solution.py:95
  164.0 19.4 %all-to-all-start.4 = ((bf16[8,64,1024]{2,1,0:T(8,128)(2,1)}), bf16[8,64,1024]{2,1,0:T(8,128)(2,1)S(1)}, u32[]{:S(2)}, u32[]{:S(2)}) async-start(bf16[8,64,1024]{2,1,0:T(8,128)(2,1)} %bitcast.71), calls=%async_computation.4 | async-start | bytes 2097152 | tf_op jit(solution)/shard_map/all_to_all | solution.py:97
  183.5 19.4 %all-to-all-start.8 = ((bf16[8,64,1024]{2,1,0:T(8,128)(2,1)}), bf16[8,64,1024]{2,1,0:T(8,128)(2,1)S(1)}, u32[]{:S(2)}, u32[]{:S(2)}) async-start(bf16[8,64,1024]{2,1,0:T(8,128)(2,1)} %bitcast.66), calls=%async_computation.8 | async-start | bytes 2097152 | tf_op jit(solution)/shard_map/all_to_all | solution.py:97
  193.7 12.2 %copy-start = (f32[512,1024]{1,0:T(8,128)S(1)}, f32[512,1024]{1,0:T(8,128)}, u32[]{:S(2)}) copy-start(f32[512,1024]{1,0:T(8,128)} %fusion.114) | copy-start | bytes 6291460

commit v2 on v1

v2 whole, which is shorter than its diff:
```python
import functools

import jax
import jax.numpy as jnp
from jax import lax
from jax.experimental import pallas as pl
from jax.experimental.pallas import tpu as pltpu
from jax.sharding import Mesh, PartitionSpec as P

CAP_SLOTS = 2
HOLD_CAP = 3
META_COLS = 128
TILE = 512
VMEM_LIMIT = 16 << 20
BF = jnp.bfloat16
F32 = jnp.float32
I32 = jnp.int32


def iota(shape, dim):
    return lax.broadcasted_iota(I32, shape, dim)


def shift(value, axis, steps):
    count = lax.axis_size(axis)
    return lax.ppermute(value, axis, [(source, (source + steps) % count) for source in range(count)])


def local_call(kernel, inputs, outputs, scalars=(), hbm=(), scratch=(), flops=0):
    moved = sum(a.size * a.dtype.itemsize for a in [*hbm, *inputs, *outputs])
    vmem = pl.BlockSpec(memory_space=pltpu.VMEM)
    return pl.pallas_call(
        kernel,
        in_specs=[pl.BlockSpec(memory_space=pltpu.SMEM)] * len(scalars)
        + [pl.BlockSpec(memory_space=pltpu.HBM)] * len(hbm)
        + [vmem] * len(inputs),
        out_specs=[vmem] * len(outputs),
        out_shape=outputs,
        scratch_shapes=list(scratch),
        cost_estimate=pl.CostEstimate(flops=flops, bytes_accessed=moved, transcendentals=0),
        compiler_params=pltpu.CompilerParams(vmem_limit_bytes=VMEM_LIMIT),
    )(*scalars, *hbm, *inputs)


def turn(value, count):
    eye = (iota((count, count), 0) == iota((count, count), 1)).astype(F32)
    return lax.dot_general(eye, value, (((1,), (1,)), ((), ())), preferred_element_type=F32)


def route_kernel(tokens_hbm, ids_hbm, scores_hbm, swap_hbm, out_ref, ids_ref, scores_ref, swap_ref, sems):
    chosen, rows = ids_ref.shape
    holders = swap_ref.shape[1]
    groups = out_ref.shape[0]
    width = tokens_hbm.shape[1] // groups
    experts = META_COLS
    per_dev = experts // holders
    small = [
        pltpu.make_async_copy(source, target, sems.at[n])
        for n, (source, target) in enumerate(
            ((ids_hbm, ids_ref), (scores_hbm, scores_ref), (swap_hbm, swap_ref))
        )
    ]
    large = [
        pltpu.make_async_copy(
            tokens_hbm.at[:, pl.ds(g * width, width)], out_ref.at[g, :, pl.ds(0, width)], sems.at[3 + g]
        )
        for g in range(groups)
    ]
    for copy in small + large:
        copy.start()
    for copy in small:
        copy.wait()
    ids = turn(ids_ref[...].astype(F32), rows)
    lane = iota((rows, experts), 1)
    hits = [lane.astype(F32) == ids[:, k : k + 1] for k in range(chosen)]
    place = jnp.zeros((rows, experts), F32)
    for k, hit in enumerate(hits):
        place = jnp.where(hit, float(k + 1), place)
    expert = iota((1, experts), 1)
    home = expert // per_dev
    spread = (iota((holders, experts), 1) // per_dev == iota((holders, experts), 0)).astype(F32)
    swap_of = jnp.dot(jnp.broadcast_to(swap_ref[...].astype(F32), (8, holders)), spread, preferred_element_type=F32)
    moved = swap_of[0:1] == (expert % per_dev).astype(F32)
    partner = jnp.where(home + holders // 2 >= holders, home - holders // 2, home + holders // 2)
    holder = jnp.where(moved, partner, home).astype(F32)
    across = jnp.broadcast_to(holder, (experts, experts))
    same = across == across.T
    mate = same & (iota((experts, experts), 0) != iota((experts, experts), 1))
    before = (iota((rows, rows), 1) < iota((rows, rows), 0)).astype(F32)
    ones = (place > 0).astype(F32)
    in_rows = jnp.dot(ones, same.astype(F32), preferred_element_type=F32)
    mate_place = jnp.dot(place, mate.astype(F32), preferred_element_type=F32)
    earlier = ((mate_place > 0) & (mate_place < place)).astype(F32)
    holder_rank = jnp.dot(before, in_rows, preferred_element_type=F32) + earlier
    expert_rank = jnp.dot(before, ones, preferred_element_type=F32)
    kept = (holder_rank < HOLD_CAP) & (expert_rank < CAP_SLOTS)
    code = jnp.where(kept, (CAP_SLOTS * lane).astype(F32) + expert_rank, -1.0)
    scores = scores_ref[...]
    gate = 2.5 * scores / jnp.sum(scores, axis=0, keepdims=True)
    gate_high = gate.astype(BF).astype(F32)
    high = turn(gate_high, rows)
    low = turn((gate - gate_high).astype(BF).astype(F32), rows)
    meta = jnp.zeros((rows, META_COLS), F32)
    for k, hit in enumerate(hits):
        code_k = jnp.sum(jnp.where(hit, code, 0.0), axis=1, keepdims=True)
        meta = jnp.where(lane == k, code_k, meta)
        meta = jnp.where(lane == chosen + k, high[:, k : k + 1], meta)
        meta = jnp.where(lane == 2 * chosen + k, low[:, k : k + 1], meta)
    meta = meta.astype(BF)
    for g in range(groups):
        out_ref[g, :, width:] = meta
    for copy in large:
        copy.wait()


def slot_code(me_ref, index, cells, per_dev, blocks, turn_way):
    unit = blocks * CAP_SLOTS
    cell = index // (per_dev * unit)
    if turn_way:
        cell = me_ref[2] + turn_way * cell
        cell = jnp.where(cell >= cells, cell - cells, jnp.where(cell < 0, cell + cells, cell))
    expert = (me_ref[1] * cells + cell) * per_dev + (index // unit) % per_dev
    return (expert * CAP_SLOTS + index % CAP_SLOTS) + 256 * ((index % unit) // CAP_SLOTS)


def gather_kernel(cells, per_dev, chosen, block_rows, pieces_in, ways, me_ref, *refs):
    pieces, outs = refs[:pieces_in], refs[pieces_in:-2]
    high_ref, low_ref = refs[-2:]
    width = outs[0].shape[1]
    slots = sum(out.shape[0] for out in outs)
    blocks = pieces_in * pieces[0].shape[0] // block_rows
    tok = jnp.concatenate([p[:, :width] for p in pieces], axis=0)
    info = jnp.concatenate([p[:, width:] for p in pieces], axis=0).astype(F32)
    count = tok.shape[0]
    mine = 256.0 * (iota((count, META_COLS), 0) // block_rows).astype(F32)
    keyed = jnp.where(info < 0, -1.0, info + mine)
    turned = keyed.T
    wanted = slot_code(me_ref, iota((slots, 1), 0), cells, per_dev, blocks, ways[0]).astype(F32)
    pick = jnp.zeros((slots, count), F32)
    for k in range(chosen):
        pick = jnp.where(turned[k : k + 1, :] == wanted, 1.0, pick)
    rows = jnp.dot(pick.astype(BF), tok, preferred_element_type=F32).astype(BF)
    each = slots // len(outs)
    for n, out in enumerate(outs):
        out[...] = rows[n * each : (n + 1) * each]
    wanted = slot_code(me_ref, iota((1, slots), 1), cells, per_dev, blocks, ways[1]).astype(F32)
    high = jnp.zeros((count, slots), F32)
    low = jnp.zeros((count, slots), F32)
    for k in range(chosen):
        hit = keyed[:, k : k + 1] == wanted
        high = jnp.where(hit, info[:, chosen + k : chosen + k + 1], high)
        low = jnp.where(hit, info[:, 2 * chosen + k : 2 * chosen + k + 1], low)
    high_ref[...] = high.astype(BF)
    low_ref[...] = low.astype(BF)


def up_kernel(arrivals, me_ref, weight_ref, *refs):
    sources, outs = refs[:arrivals], refs[arrivals:-1]
    rows_ref = refs[-1]
    groups = len(outs)
    cells, per_dev, unit, width = rows_ref.shape
    if arrivals == 1:
        rows_ref = sources[0]
    else:
        for n, source in enumerate(sources):
            rows_ref[n] = source[...].reshape(per_dev, unit, width)
    span = cells // groups
    half = span * unit
    for s in range(per_dev):
        parts = []
        for k in range(groups):
            start = lax.rem(me_ref[0] + groups - k, groups) * span
            parts.append(rows_ref[pl.ds(start, span), s].reshape(half, width))
        rows = jnp.concatenate(parts, axis=0)

        def columns(j, _):
            cols = pl.ds(pl.multiple_of(j * TILE, TILE), TILE)
            result = jnp.dot(rows, weight_ref[s, :, cols], preferred_element_type=F32)
            for k, out in enumerate(outs):
                out[s * half : (s + 1) * half, cols] = result[k * half : (k + 1) * half].astype(out.dtype)
            return 0

        lax.fori_loop(0, weight_ref.shape[2] // TILE, columns, 0)


def down_kernel(groups, arrival_way, me_ref, weight_ref, *refs):
    pieces, outs = refs[:groups], refs[groups:-1]
    rows_ref = refs[-1]
    cells, per_dev, unit, _ = rows_ref.shape
    target = outs[0] if len(outs) == 1 else rows_ref
    span = cells // groups
    half = span * unit
    for s in range(per_dev):
        rows = jnp.concatenate([piece[s * half : (s + 1) * half, :] for piece in pieces], axis=0)

        def columns(j, _):
            cols = pl.ds(pl.multiple_of(j * TILE, TILE), TILE)
            result = jnp.dot(rows, weight_ref[s, :, cols], preferred_element_type=F32).astype(BF)
            for k in range(groups):
                start = lax.rem(me_ref[0] + groups - k, groups) * span
                for n in range(span):
                    index = start + n
                    if arrival_way:
                        index = lax.rem(me_ref[2] + cells - index, cells)
                    else:
                        index = lax.rem(index + cells - me_ref[2], cells)
                    first = k * half + n * unit
                    target[index, s, :, cols] = result[first : first + unit]
            return 0

        lax.fori_loop(0, weight_ref.shape[2] // TILE, columns, 0)
    if len(outs) > 1:
        for n, out in enumerate(outs):
            out[...] = rows_ref[n].reshape(out.shape)


def combine_kernel(arrivals, high_ref, low_ref, *refs):
    sources, outs = refs[:arrivals], refs[arrivals:]
    rows = jnp.concatenate([source[...] for source in sources], axis=0)
    total = jnp.dot(high_ref[...], rows, preferred_element_type=F32)
    total = total + jnp.dot(low_ref[...], rows, preferred_element_type=F32)
    count = outs[0].shape[0]
    for n, out in enumerate(outs):
        out[...] = total[n * count : (n + 1) * count].astype(out.dtype)


def layer(tokens, expert_ids, scores, up_weight, down_weight, swap_slot):
    groups = lax.axis_size("dp")
    planes = lax.axis_size("z")
    cells = lax.axis_size("yc")
    tok_rows, width = tokens.shape
    chosen = expert_ids.shape[1]
    per_dev, part_width, hidden_width = up_weight.shape
    full = part_width + META_COLS
    dp_rows = groups * tok_rows
    me = jnp.stack([lax.axis_index("dp"), lax.axis_index("z"), lax.axis_index("yc")]).astype(I32)

    payload = local_call(
        route_kernel,
        [],
        [jax.ShapeDtypeStruct((groups, tok_rows, full), BF)],
        hbm=[tokens, expert_ids.T, scores.T, swap_slot.reshape(1, -1)],
        scratch=[
            pltpu.VMEM((chosen, tok_rows), I32),
            pltpu.VMEM((chosen, tok_rows), F32),
            pltpu.VMEM((1, swap_slot.shape[0]), I32),
            pltpu.SemaphoreType.DMA((3 + groups,)),
        ],
    )[0]
    own = lax.all_to_all(payload, "dp", 0, 0, tiled=True).reshape(dp_rows, full)
    half = planes // 2
    near = {0: own}
    for offset in (1, -1, half):
        near[offset] = shift(own, "z", offset)
    far = {
        2: shift(near[1], "z", 1),
        -2: shift(near[-1], "z", -1),
        3: shift(near[half], "z", -1),
        -3: shift(near[half], "z", 1),
    }
    unit = len(near) * groups * CAP_SLOTS
    slots = cells * per_dev * unit
    rows_shape = (cells, per_dev, unit, part_width)
    count = slots // groups

    cell_rows = per_dev * unit
    scratch = [pltpu.VMEM(rows_shape, BF)]

    chunks = []
    for n, chunk in enumerate((near, far)):
        tokens_in = [chunk[offset] for offset in chunk]
        one = jax.ShapeDtypeStruct((cell_rows, part_width), BF)
        whole = jax.ShapeDtypeStruct((slots, part_width), BF)
        weights = [jax.ShapeDtypeStruct((len(chunk) * dp_rows, slots), BF)] * 2
        *rows, high, low = local_call(
            functools.partial(
                gather_kernel, cells, per_dev, chosen, tok_rows, len(chunk), (0, -1) if n else (1, 0)
            ),
            tokens_in,
            ([whole] if n else [one] * cells) + weights,
            scalars=(me,),
        )
        if n:
            arrived = lax.all_to_all(rows[0].reshape(cells, cell_rows, part_width), "yc", 0, 0, tiled=True)
            arrived = [arrived.reshape(rows_shape)]
        else:
            arrived = [rows[0]] + [shift(rows[k], "yc", k) for k in range(1, cells)]
        sent = local_call(
            functools.partial(up_kernel, len(arrived)),
            [up_weight] + arrived,
            [jax.ShapeDtypeStruct((count, hidden_width), BF if k else F32) for k in range(groups)],
            scalars=(me,),
            scratch=scratch,
            flops=2 * slots * part_width * hidden_width,
        )
        chunks.append((list(chunk), high, low, sent))
    pieces = []
    for _, _, _, sent in chunks:
        partial = sent[0]
        for k in range(1, groups):
            partial = partial + shift(sent[k], "dp", -k).astype(F32)
        hidden = jax.nn.silu(partial).astype(BF)
        pieces.append([hidden] + [shift(hidden, "dp", k) for k in range(1, groups)])
    total = None
    for n, (offsets, high, low, sent) in enumerate(chunks):
        hidden = pieces[n]
        result = local_call(
            functools.partial(down_kernel, groups, n == 0),
            [down_weight] + hidden,
            [one] * cells if n else [jax.ShapeDtypeStruct(rows_shape, BF)],
            scalars=(me,),
            scratch=scratch,
            flops=2 * slots * part_width * hidden_width,
        )
        if n:
            back = [result[0]] + [shift(result[k], "yc", k) for k in range(1, cells)]
        else:
            back = lax.all_to_all(result[0].reshape(cells, cell_rows, part_width), "yc", 0, 0, tiled=True)
            back = [back.reshape(slots, part_width)]
        sums = local_call(
            functools.partial(combine_kernel, len(back)),
            [high, low] + back,
            [jax.ShapeDtypeStruct((dp_rows, part_width), BF if offset else F32) for offset in offsets],
            flops=4 * slots * part_width * len(offsets) * dp_rows,
        )
        for offset, value in zip(offsets, sums):
            if offset:
                value = shift(value, "z", -offset).astype(F32)
            total = value if total is None else total + value
    parts = total.astype(BF).reshape(groups, tok_rows, part_width)
    parts = lax.all_to_all(parts, "dp", 0, 0, tiled=True)
    return parts.transpose(1, 0, 2).reshape(tok_rows, width)


def solution(mesh):
    groups, holders = mesh.devices.shape
    planes = 8
    grid = Mesh(mesh.devices.reshape(groups, planes, holders // planes), ("dp", "z", "yc"))
    every = ("dp", "z", "yc")
    return jax.shard_map(
        layer,
        mesh=grid,
        in_specs=(
            P(every, None),
            P(every, None),
            P(every, None),
            P(("z", "yc"), "dp", None),
            P(("z", "yc"), None, "dp"),
            P(),
        ),
        out_specs=P(every, None),
        check_vma=False,
    )
```

time: 246 us -> 181 us (0.74)
  waiting for transfers between devices: 120 us -> 59.5 us
  matrix products: 33 us -> 0 us
  starting transfers between devices: 45 us -> 67.4 us
  Pallas kernels: 0 us -> 19.8 us
  blocking collectives: 33.2 us -> 18.7 us
  local copies, waits for them, and re-layouts: 8.32 us -> 10.9 us
    all_to_all x9 -> x2, waiting for transfers between devices: 120 us -> 0.01 us  [the longest x1 0.01 us: layer(): lax.all_to_all(result[0].reshape(cells, cell_rows, part_width), 'yc', 0,...]
    ppermute x0 -> x40, waiting for transfers between devices: none -> 59.4 us  [shift(): lax.ppermute(value, axis, [(source, (source + steps) % count) for source...]
    ppermute x0 -> x40, starting transfers between devices: none -> 58.1 us  [shift(): lax.ppermute(value, axis, [(source, (source + steps) % count) for source...]
    all_to_all x9 -> x2, starting transfers between devices: 45 us -> 9.28 us  [the longest x1 4.99 us: layer(): lax.all_to_all(rows[0].reshape(cells, cell_rows, part_width), 'yc', 0, 0,...]
    dot_general x15 -> x0, matrix products: 33 us -> none  [the longest x2 8.02 us: body(): jnp.dot(arrived, up_weight[s], preferred_element_type=F32).astype(BF)]
    pallas_call x0 -> x9, Pallas kernels: none -> 19.8 us  [local_call(): pl.pallas_call(kernel, in_specs=[pl.BlockSpec(memory_space=pltpu.SMEM)] *...]
    all_to_all x1 -> x2, blocking collectives: 33.2 us -> 18.7 us  [the longest x1 10.2 us: layer(): own = lax.all_to_all(payload, 'dp', 0, 0, tiled=True).reshape(dp_rows, full)]
    unnamed x11 -> x20, local copies, waits for them, and re-layouts: 2.62 us -> 10.2 us
  transfers between devices with their start and end apart: 9 -> 42, of which waited for: 9 -> 15; matrix products, arithmetic and copies ran while one was open for 10% -> 1% of each run, Pallas kernels for 0% -> 10%
where the time goes in v2:
time: 181 us; the launch traced here: 178 us
  starting transfers between devices  67.4 us (37%)
  waiting for transfers between devices  59.5 us (33%)
  Pallas kernels  19.8 us (11%)
  blocking collectives  18.7 us (10%)
  local copies, waits for them, and re-layouts  10.9 us (6%)
  other arithmetic  1.81 us (1%)
    ppermute x40, waiting for transfers between devices, shift(): lax.ppermute(value, axis, [(source, (source + steps) % count) for source...  59.4 us
    ppermute x40, starting transfers between devices, shift(): lax.ppermute(value, axis, [(source, (source + steps) % count) for source...  58.1 us
    pallas_call x9, Pallas kernels, local_call(): pl.pallas_call(kernel, in_specs=[pl.BlockSpec(memory_space=pltpu.SMEM)] *...  19.8 us
    unnamed x20, local copies, waits for them, and re-layouts  10.2 us
    all_to_all x1, blocking collectives, layer(): own = lax.all_to_all(payload, 'dp', 0, 0, tiled=True).reshape(dp_rows, full)  10.2 us
    all_to_all x1, blocking collectives, layer(): parts = lax.all_to_all(parts, 'dp', 0, 0, tiled=True)  8.52 us
    all_to_all x1, starting transfers between devices, layer(): lax.all_to_all(rows[0].reshape(cells, cell_rows, part_width), 'yc', 0, 0,...  4.99 us
    all_to_all x1, starting transfers between devices, layer(): lax.all_to_all(result[0].reshape(cells, cell_rows, part_width), 'yc', 0,...  4.29 us
  transfers between devices with their start and end apart: 42, of which 15 were waited for; matrix products, arithmetic and copies ran while one was open for 1% of the time, Pallas kernels for 10%

profile of v2, /device:TPU:8, one launch (start us, length us, event | category | flops | bytes accessed | tf_op | source)
XLA Modules:
  0.0 178.2 jit_solution(8131558020928033590)
XLA Ops:
  0.0 0.9 copy-done.4
  0.9 0.7 copy-done.5
  2.9 0.8 shard_map.64
  3.7 10.2 %all_to_all.20 = bf16[4,16,1152]{2,1,0:T(8,128)(2,1)S(1)} all-to-all(bf16[4,16,1152]{2,1,0:T(8,128)(2,1)S(1)} %shard_map.64), channel_id=1, replica_groups=mesh['dp'=4,'z'=8,'yc'=8] {'dp'}, dimensions={0} | all-to-all | bytes 294912 | tf_op jit(solution)/shard_map/all_to_all | solution.py:250
  13.9 7.2 %collective-permute-start.2 = (bf16[64,1152]{1,0:T(8,128)(2,1)S(1)}, bf16[64,1152]{1,0:T(8,128)(2,1)S(1)}, u32[]{:S(2)}, u32[]{:S(2)}) collective-permute-start(bf16[64,1152]{1,0:T(8,128)(2,1)S(1)} %bitcast.17), channel_id=1, source_target_pairs={{0,32},{8,40},{16,48},{24,56},{32,0},{40,8},{48,16},{56,24},{1,33}... | collective-permute-start | bytes 442376 | tf_op jit(solution)/shard_map/ppermute | solution.py:26
  21.2 1.9 %collective-permute-start = (bf16[64,1152]{1,0:T(8,128)(2,1)S(1)}, bf16[64,1152]{1,0:T(8,128)(2,1)S(1)}, u32[]{:S(2)}, u32[]{:S(2)}) collective-permute-start(bf16[64,1152]{1,0:T(8,128)(2,1)S(1)} %bitcast.19), channel_id=1, source_target_pairs={{0,8},{8,16},{16,24},{24,32},{32,40},{40,48},{48,56},{56,0},{1,9},... | collective-permute-start | bytes 442376 | tf_op jit(solution)/shard_map/ppermute | solution.py:26
  23.2 3.6 %collective-permute-done.2.refs_3_ = bf16[64,1152]{1,0:T(8,128)(2,1)S(1)} collective-permute-done((bf16[64,1152]{1,0:T(8,128)(2,1)S(1)}, bf16[64,1152]{1,0:T(8,128)(2,1)S(1)}, u32[]{:S(2)}, u32[]{:S(2)}) %collective-permute-start.2) | collective-permute-done | bytes 147488 | tf_op jit(solution)/shard_map/ppermute | solution.py:26
  26.8 3.8 %collective-permute-done.1.refs_2_ = bf16[64,1152]{1,0:T(8,128)(2,1)S(1)} collective-permute-done((bf16[64,1152]{1,0:T(8,128)(2,1)S(1)}, bf16[64,1152]{1,0:T(8,128)(2,1)S(1)}, u32[]{:S(2)}, u32[]{:S(2)}) %collective-permute-start.1) | collective-permute-done | bytes 147488 | tf_op jit(solution)/shard_map/ppermute | solution.py:26
  30.6 2.0 %shard_map.65 = (bf16[64,1024]{1,0:T(8,128)(2,1)S(1)}, bf16[64,1024]{1,0:T(8,128)(2,1)S(1)}, bf16[64,1024]{1,0:T(8,128)(2,1)S(1)}, bf16[64,1024]{1,0:T(8,128)(2,...) custom-call(s32[3]{0:T(128)S(1)} %pad_add_fusion.me_ref, ...), custom_call_target="tpu_custom_call" | custom-call | bytes 2162688 | tf_op jit(solution)/shard_map/pallas_call | solution.py:32
  32.9 3.0 %collective-permute-start.21 = (bf16[64,1152]{1,0:T(8,128)(2,1)S(1)}, bf16[64,1152]{1,0:T(8,128)(2,1)S(1)}, u32[]{:S(2)}, u32[]{:S(2)}) collective-permute-start(bf16[64,1152]{1,0:T(8,128)(2,1)S(1)} %collective-permute-done.2.refs_3_), channel_id=1, source_target_pairs={{0,56},{8,0},{16,8},{24,16},{32,24},{40,32},{48,40},{56,48},{1,57}... | collective-permute-start | bytes 442376 | tf_op jit(solution)/shard_map/ppermute | solution.py:26
  35.9 1.0 collective-permute-start.20
  36.9 1.1 collective-permute-start.19
  37.9 1.6 collective-permute-start.4
  39.5 4.3 %collective-permute-done.4.refs_2_ = bf16[64,1024]{1,0:T(8,128)(2,1)S(1)} collective-permute-done((bf16[64,1024]{1,0:T(8,128)(2,1)S(1)}, bf16[64,1024]{1,0:T(8,128)(2,1)S(1)}, u32[]{:S(2)}, u32[]{:S(2)}) %collective-permute-start.4) | collective-permute-done | bytes 131104 | tf_op jit(solution)/shard_map/ppermute | solution.py:26
  44.0 2.5 %collective-permute-start.6 = (bf16[64,1024]{1,0:T(8,128)(2,1)S(1)}, bf16[64,1024]{1,0:T(8,128)(2,1)S(1)}, u32[]{:S(2)}, u32[]{:S(2)}) collective-permute-start(bf16[64,1024]{1,0:T(8,128)(2,1)S(1)} %get-tuple-element.48), channel_id=1, source_target_pairs={{0,4},{1,5},{2,6},{3,7},{4,0},{5,1},{6,2},{7,3},{8,12},{9,13},{10,... | collective-permute-start | bytes 393224 | tf_op jit(solution)/shard_map/ppermute | solution.py:26
  46.5 1.6 collective-permute-start.7
  48.2 2.0 %collective-permute-start.8 = (bf16[64,1024]{1,0:T(8,128)(2,1)S(1)}, bf16[64,1024]{1,0:T(8,128)(2,1)S(1)}, u32[]{:S(2)}, u32[]{:S(2)}) collective-permute-start(bf16[64,1024]{1,0:T(8,128)(2,1)S(1)} %get-tuple-element.50), channel_id=1, source_target_pairs={{0,6},{1,7},{2,0},{3,1},{4,2},{5,3},{6,4},{7,5},{8,14},{9,15},{10,... | collective-permute-start | bytes 393224 | tf_op jit(solution)/shard_map/ppermute | solution.py:26
  50.2 2.5 %shard_map.69 = (bf16[512,1024]{1,0:T(8,128)(2,1)}, bf16[256,512]{1,0:T(8,128)(2,1)S(1)}, bf16[256,512]{1,0:T(8,128)(2,1)S(1)}) custom-call(s32[3]{0:T(128)S(1)} %pad_add_fusion.me_ref, bf16[64,1152]{1,0:T(8,128)(2,1)S(1)} %collective-permute-done.19.refs_0_, bf16[64,1152]{1,0:T(8,128)(2,1)S(1)} %collective-permute-done.20.refs_1_, ...), custom_call_target="tpu_custom_call" | custom-call | bytes 2162688 | tf_op jit(solution)/shard_map/pallas_call | solution.py:32
  52.7 0.7 copy-done.8
  53.4 5.0 %all-to-all-start.2 = ((bf16[8,64,1024]{2,1,0:T(8,128)(2,1)}), bf16[8,64,1024]{2,1,0:T(8,128)(2,1)S(1)}, u32[]{:S(2)}, u32[]{:S(2)}) async-start(bf16[8,64,1024]{2,1,0:T(8,128)(2,1)} %bitcast.9), calls=%async_computation.2 | async-start | bytes 2097152 | tf_op jit(solution)/shard_map/all_to_all | solution.py:284
  58.5 2.2 %copy-done = bf16[2,1024,1024]{2,1,0:T(8,128)(2,1)S(1)} copy-done((bf16[2,1024,1024]{2,1,0:T(8,128)(2,1)S(1)}, bf16[2,1024,1024]{2,1,0:T(8,128)(2,1)}, u32[]{:S(2)}) %copy-start) | copy-done | bytes 4194328
  60.7 2.4 %shard_map.66 = (f32[128,1024]{1,0:T(8,128)S(1)}, bf16[128,1024]{1,0:T(8,128)(2,1)S(1)}, bf16[128,1024]{1,0:T(8,128)(2,1)S(1)}, bf16[128,1024]{1,0:T(8,128)(2,1)S(1)}) custom-call(s32[3]{0:T(128)S(1)} %pad_add_fusion.me_ref, bf16[2,1024,1024]{2,1,0:T(8,128)(2,1)S(1)} %copy-done, bf16[64,1024]{1,0:T(8,128)(2,1)S(1)} %get-tuple-element.44.refs_0_, ...), custom_call_target="tpu_custom_call" | custom-call | flops 1073741824 | bytes 6553600 | tf_op jit(solution)/shard_map/pallas_call | solution.py:32
  63.1 1.2 collective-permute-start.10
  64.4 1.5 collective-permute-start.11
  66.0 6.3 %collective-permute-done.10 = bf16[128,1024]{1,0:T(8,128)(2,1)S(1)} collective-permute-done((bf16[128,1024]{1,0:T(8,128)(2,1)S(1)}, bf16[128,1024]{1,0:T(8,128)(2,1)S(1)}, u32[]{:S(2)}, u32[]{:S(2)}) %collective-permute-start.10) | collective-permute-done | bytes 262176 | tf_op jit(solution)/shard_map/ppermute | solution.py:26
  72.4 2.7 %collective-permute-done.11 = bf16[128,1024]{1,0:T(8,128)(2,1)S(1)} collective-permute-done((bf16[128,1024]{1,0:T(8,128)(2,1)S(1)}, bf16[128,1024]{1,0:T(8,128)(2,1)S(1)}, u32[]{:S(2)}, u32[]{:S(2)}) %collective-permute-start.11) | collective-permute-done | bytes 262176 | tf_op jit(solution)/shard_map/ppermute | solution.py:26
  75.1 5.2 %collective-permute-done.12 = bf16[128,1024]{1,0:T(8,128)(2,1)S(1)} collective-permute-done((bf16[128,1024]{1,0:T(8,128)(2,1)S(1)}, bf16[128,1024]{1,0:T(8,128)(2,1)S(1)}, u32[]{:S(2)}, u32[]{:S(2)}) %collective-permute-start.12) | collective-permute-done | bytes 262176 | tf_op jit(solution)/shard_map/ppermute | solution.py:26
  81.2 1.5 collective-permute-start.14
  82.7 0.8 collective-permute-start.13
  83.5 2.2 %copy-done.1 = bf16[2,1024,1024]{2,1,0:T(8,128)(2,1)S(1)} copy-done((bf16[2,1024,1024]{2,1,0:T(8,128)(2,1)S(1)}, bf16[2,1024,1024]{2,1,0:T(8,128)(2,1)}, u32[]{:S(2)}) %copy-start.1) | copy-done | bytes 4194328
  85.7 3.2 %shard_map.70 = (f32[128,1024]{1,0:T(8,128)S(1)}, bf16[128,1024]{1,0:T(8,128)(2,1)}, bf16[128,1024]{1,0:T(8,128)(2,1)}, bf16[128,1024]{1,0:T(8,128)(2,1)}) custom-call(s32[3]{0:T(128)S(1)} %pad_add_fusion.me_ref, bf16[2,1024,1024]{2,1,0:T(8,128)(2,1)S(1)} %copy-done.1, bf16[8,2,32,1024]{3,2,1,0:T(8,128)(2,1)S(1)} %bitcast.15), custom_call_target="tpu_custom_call" | custom-call | flops 1073741824 | bytes 6553600 | tf_op jit(solution)/shard_map/pallas_call | solution.py:32
  88.9 2.4 %collective-permute-start.23 = (bf16[128,1024]{1,0:T(8,128)(2,1)}, bf16[128,1024]{1,0:T(8,128)(2,1)}, u32[]{:S(2)}, u32[]{:S(2)}) collective-permute-start(bf16[128,1024]{1,0:T(8,128)(2,1)} %get-tuple-element.64), channel_id=1, source_target_pairs={{0,192},{64,0},{128,64},{192,128},{1,193},{65,1},{129,65},{193,129... | collective-permute-start | bytes 786440 | tf_op jit(solution)/shard_map/ppermute | solution.py:26
  91.4 0.9 collective-permute-start.24
  92.2 1.4 collective-permute-start.25
  93.7 4.0 %collective-permute-done.13.refs_1_ = bf16[128,1024]{1,0:T(8,128)(2,1)S(1)} collective-permute-done((bf16[128,1024]{1,0:T(8,128)(2,1)S(1)}, bf16[128,1024]{1,0:T(8,128)(2,1)S(1)}, u32[]{:S(2)}, u32[]{:S(2)}) %collective-permute-start.13) | collective-permute-done | bytes 262176 | tf_op jit(solution)/shard_map/ppermute | solution.py:26
  97.6 3.4 %shard_map.67 = bf16[8,2,32,1024]{3,2,1,0:T(8,128)(2,1)} custom-call(s32[3]{0:T(128)S(1)} %pad_add_fusion.me_ref, bf16[2,1024,1024]{2,1,0:T(8,128)(2,1)S(1)} %copy-done.2, bf16[128,1024]{1,0:T(8,128)(2,1)S(1)} %multiply_convert_fusion.1.refs_0_, bf16[128,1024]{1,0:T(8,128)(2,1)S(1)} %collective-permute-done.13.refs_1_, ...), custom_call_target="tpu_custom_call" | custom-call | flops 1073741824 | bytes 6291456 | tf_op jit(solution)/shard_map/pallas_call | solution.py:32
  101.0 4.3 %all-to-all-start.1 = ((bf16[8,64,1024]{2,1,0:T(8,128)(2,1)}), bf16[8,64,1024]{2,1,0:T(8,128)(2,1)S(1)}, u32[]{:S(2)}, u32[]{:S(2)}) async-start(bf16[8,64,1024]{2,1,0:T(8,128)(2,1)} %bitcast.7), calls=%async_computation.1 | async-start | bytes 2097152 | tf_op jit(solution)/shard_map/all_to_all | solution.py:318
  105.3 2.1 %collective-permute-done.25 = bf16[128,1024]{1,0:T(8,128)(2,1)} collective-permute-done((bf16[128,1024]{1,0:T(8,128)(2,1)}, bf16[128,1024]{1,0:T(8,128)(2,1)}, u32[]{:S(2)}, u32[]{:S(2)}) %collective-permute-start.25) | collective-permute-done | bytes 262176 | tf_op jit(solution)/shard_map/ppermute | solution.py:26
  107.4 1.4 multiply_convert_fusion.refs_0_
  108.8 1.2 collective-permute-start.28
  110.0 1.0 collective-permute-start.27
  111.0 0.8 collective-permute-start.26
  111.8 6.3 %collective-permute-done.28.refs_3_ = bf16[128,1024]{1,0:T(8,128)(2,1)S(1)} collective-permute-done((bf16[128,1024]{1,0:T(8,128)(2,1)S(1)}, bf16[128,1024]{1,0:T(8,128)(2,1)S(1)}, u32[]{:S(2)}, u32[]{:S(2)}) %collective-permute-start.28) | collective-permute-done | bytes 262176 | tf_op jit(solution)/shard_map/ppermute | solution.py:26
  118.1 2.7 %collective-permute-done.27.refs_2_ = bf16[128,1024]{1,0:T(8,128)(2,1)S(1)} collective-permute-done((bf16[128,1024]{1,0:T(8,128)(2,1)S(1)}, bf16[128,1024]{1,0:T(8,128)(2,1)S(1)}, u32[]{:S(2)}, u32[]{:S(2)}) %collective-permute-start.27) | collective-permute-done | bytes 262176 | tf_op jit(solution)/shard_map/ppermute | solution.py:26
  120.7 3.6 %collective-permute-done.26.refs_1_ = bf16[128,1024]{1,0:T(8,128)(2,1)S(1)} collective-permute-done((bf16[128,1024]{1,0:T(8,128)(2,1)S(1)}, bf16[128,1024]{1,0:T(8,128)(2,1)S(1)}, u32[]{:S(2)}, u32[]{:S(2)}) %collective-permute-start.26) | collective-permute-done | bytes 262176 | tf_op jit(solution)/shard_map/ppermute | solution.py:26
  124.3 2.2 %copy-done.3 = bf16[2,1024,1024]{2,1,0:T(8,128)(2,1)S(1)} copy-done((bf16[2,1024,1024]{2,1,0:T(8,128)(2,1)S(1)}, bf16[2,1024,1024]{2,1,0:T(8,128)(2,1)}, u32[]{:S(2)}) %copy-start.3) | copy-done | bytes 4194328
  126.5 3.1 %shard_map.71 = (bf16[64,1024]{1,0:T(8,128)(2,1)S(1)}, bf16[64,1024]{1,0:T(8,128)(2,1)S(1)}, bf16[64,1024]{1,0:T(8,128)(2,1)S(1)}, bf16[64,1024]{1,0:T(8,128)(2,...) custom-call(s32[3]{0:T(128)S(1)} %pad_add_fusion.me_ref, ...), custom_call_target="tpu_custom_call" | custom-call | flops 1073741824 | bytes 6291456 | tf_op jit(solution)/shard_map/pallas_call | solution.py:32
  130.3 1.8 %collective-permute-start.31 = (bf16[64,1024]{1,0:T(8,128)(2,1)}, bf16[64,1024]{1,0:T(8,128)(2,1)S(1)}, u32[]{:S(2)}, u32[]{:S(2)}) collective-permute-start(bf16[64,1024]{1,0:T(8,128)(2,1)} %get-tuple-element.70), channel_id=1, source_target_pairs={{0,3},{1,4},{2,5},{3,6},{4,7},{5,0},{6,1},{7,2},{8,11},{9,12},{10,... | collective-permute-start | bytes 393224 | tf_op jit(solution)/shard_map/ppermute | solution.py:26
  132.1 1.7 collective-permute-start.32
  133.8 1.2 collective-permute-start.33
  135.1 2.0 %collective-permute-start.34 = (bf16[64,1024]{1,0:T(8,128)(2,1)S(1)}, bf16[64,1024]{1,0:T(8,128)(2,1)S(1)}, u32[]{:S(2)}, u32[]{:S(2)}) collective-permute-start(bf16[64,1024]{1,0:T(8,128)(2,1)S(1)} %get-tuple-element.73), channel_id=1, source_target_pairs={{0,6},{1,7},{2,0},{3,1},{4,2},{5,3},{6,4},{7,5},{8,14},{9,15},{10,... | collective-permute-start | bytes 393224 | tf_op jit(solution)/shard_map/ppermute | solution.py:26
  137.1 1.6 collective-permute-start.35
  138.7 0.7 shard_map.68
  139.4 2.2 %collective-permute-start.16 = (bf16[64,1024]{1,0:T(8,128)(2,1)S(1)}, bf16[64,1024]{1,0:T(8,128)(2,1)S(1)}, u32[]{:S(2)}, u32[]{:S(2)}) collective-permute-start(bf16[64,1024]{1,0:T(8,128)(2,1)S(1)} %get-tuple-element.57), channel_id=1, source_target_pairs={{0,56},{8,0},{16,8},{24,16},{32,24},{40,32},{48,40},{56,48},{1,57}... | collective-permute-start | bytes 393224 | tf_op jit(solution)/shard_map/ppermute | solution.py:26
  141.6 1.8 %collective-permute-done.33.refs_5_ = bf16[64,1024]{1,0:T(8,128)(2,1)S(1)} collective-permute-done((bf16[64,1024]{1,0:T(8,128)(2,1)S(1)}, bf16[64,1024]{1,0:T(8,128)(2,1)S(1)}, u32[]{:S(2)}, u32[]{:S(2)}) %collective-permute-start.33) | collective-permute-done | bytes 131104 | tf_op jit(solution)/shard_map/ppermute | solution.py:26
  143.4 4.0 %collective-permute-start.18 = (bf16[64,1024]{1,0:T(8,128)(2,1)S(1)}, bf16[64,1024]{1,0:T(8,128)(2,1)S(1)}, u32[]{:S(2)}, u32[]{:S(2)}) collective-permute-start(bf16[64,1024]{1,0:T(8,128)(2,1)S(1)} %get-tuple-element.59), channel_id=1, source_target_pairs={{0,32},{8,40},{16,48},{24,56},{32,0},{40,8},{48,16},{56,24},{1,33}... | collective-permute-start | bytes 393224 | tf_op jit(solution)/shard_map/ppermute | solution.py:26
  147.4 1.6 shard_map.72
  149.1 2.9 %collective-permute-start.37 = (bf16[64,1024]{1,0:T(8,128)(2,1)S(1)}, bf16[64,1024]{1,0:T(8,128)(2,1)S(1)}, u32[]{:S(2)}, u32[]{:S(2)}) collective-permute-start(bf16[64,1024]{1,0:T(8,128)(2,1)S(1)} %get-tuple-element.76), channel_id=1, source_target_pairs={{0,16},{8,24},{16,32},{24,40},{32,48},{40,56},{48,0},{56,8},{1,17}... | collective-permute-start | bytes 393224 | tf_op jit(solution)/shard_map/ppermute | solution.py:26
  152.1 1.2 collective-permute-start.38
  153.3 2.6 %collective-permute-start.39 = (bf16[64,1024]{1,0:T(8,128)(2,1)S(1)}, bf16[64,1024]{1,0:T(8,128)(2,1)S(1)}, u32[]{:S(2)}, u32[]{:S(2)}) collective-permute-start(bf16[64,1024]{1,0:T(8,128)(2,1)S(1)} %get-tuple-element.78), channel_id=1, source_target_pairs={{0,24},{8,32},{16,40},{24,48},{32,56},{40,0},{48,8},{56,16},{1,25}... | collective-permute-start | bytes 393224 | tf_op jit(solution)/shard_map/ppermute | solution.py:26
  155.9 6.3 %collective-permute-done.36 = bf16[64,1024]{1,0:T(8,128)(2,1)S(1)} collective-permute-done((bf16[64,1024]{1,0:T(8,128)(2,1)S(1)}, bf16[64,1024]{1,0:T(8,128)(2,1)S(1)}, u32[]{:S(2)}, u32[]{:S(2)}) %collective-permute-start.36) | collective-permute-done | bytes 131104 | tf_op jit(solution)/shard_map/ppermute | solution.py:26
  162.2 5.3 %collective-permute-done.38 = bf16[64,1024]{1,0:T(8,128)(2,1)S(1)} collective-permute-done((bf16[64,1024]{1,0:T(8,128)(2,1)S(1)}, bf16[64,1024]{1,0:T(8,128)(2,1)S(1)}, u32[]{:S(2)}, u32[]{:S(2)}) %collective-permute-start.38) | collective-permute-done | bytes 131104 | tf_op jit(solution)/shard_map/ppermute | solution.py:26
  167.5 1.4 collective-permute-done.39
  169.0 8.5 %all_to_all.21 = bf16[4,16,1024]{2,1,0:T(8,128)(2,1)S(1)} all-to-all(bf16[4,16,1024]{2,1,0:T(8,128)(2,1)S(1)} %bitcast.24), channel_id=1, replica_groups=mesh['dp'=4,'z'=8,'yc'=8] {'dp'}, dimensions={0} | all-to-all | bytes 262144 | tf_op jit(solution)/shard_map/all_to_all | solution.py:331
  (56 shorter events, 4.9 us)
Async XLA Ops:
  0.0 0.9 copy-start.4
  0.9 0.7 copy-start.5
  1.6 0.7 copy-start.6
  2.3 0.7 copy-start.7
  13.9 12.9 %collective-permute-start.2 = (bf16[64,1152]{1,0:T(8,128)(2,1)S(1)}, bf16[64,1152]{1,0:T(8,128)(2,1)S(1)}, u32[]{:S(2)}, u32[]{:S(2)}) collective-permute-start(bf16[64,1152]{1,0:T(8,128)(2,1)S(1)} %bitcast.17), channel_id=1, source_target_pairs={{0,32},{8,40},{16,48},{24,56},{32,0},{40,8},{48,16},{56,24},{1,33}... | collective-permute-start | bytes 442376 | tf_op jit(solution)/shard_map/ppermute | solution.py:26
  21.1 9.5 %collective-permute-start.1 = (bf16[64,1152]{1,0:T(8,128)(2,1)S(1)}, bf16[64,1152]{1,0:T(8,128)(2,1)S(1)}, u32[]{:S(2)}, u32[]{:S(2)}) collective-permute-start(bf16[64,1152]{1,0:T(8,128)(2,1)S(1)} %bitcast.18), channel_id=1, source_target_pairs={{0,56},{8,0},{16,8},{24,16},{32,24},{40,32},{48,40},{56,48},{1,57}... | collective-permute-start | bytes 442376 | tf_op jit(solution)/shard_map/ppermute | solution.py:26
  21.2 9.4 %collective-permute-start = (bf16[64,1152]{1,0:T(8,128)(2,1)S(1)}, bf16[64,1152]{1,0:T(8,128)(2,1)S(1)}, u32[]{:S(2)}, u32[]{:S(2)}) collective-permute-start(bf16[64,1152]{1,0:T(8,128)(2,1)S(1)} %bitcast.19), channel_id=1, source_target_pairs={{0,8},{8,16},{16,24},{24,32},{32,40},{40,48},{48,56},{56,0},{1,9},... | collective-permute-start | bytes 442376 | tf_op jit(solution)/shard_map/ppermute | solution.py:26
  32.6 5.4 %collective-permute-start.3 = (bf16[64,1024]{1,0:T(8,128)(2,1)S(1)}, bf16[64,1024]{1,0:T(8,128)(2,1)S(1)}, u32[]{:S(2)}, u32[]{:S(2)}) collective-permute-start(bf16[64,1024]{1,0:T(8,128)(2,1)S(1)} %get-tuple-element.45), channel_id=1, source_target_pairs={{0,1},{1,2},{2,3},{3,4},{4,5},{5,6},{6,7},{7,0},{8,9},{9,10},{10,1... | collective-permute-start | bytes 393224 | tf_op jit(solution)/shard_map/ppermute | solution.py:26
  32.6 11.5 %collective-permute-start.22 = (bf16[64,1152]{1,0:T(8,128)(2,1)S(1)}, bf16[64,1152]{1,0:T(8,128)(2,1)S(1)}, u32[]{:S(2)}, u32[]{:S(2)}) collective-permute-start(bf16[64,1152]{1,0:T(8,128)(2,1)S(1)} %collective-permute-done.2.refs_3_), channel_id=1, source_target_pairs={{0,8},{8,16},{16,24},{24,32},{32,40},{40,48},{48,56},{56,0},{1,9},... | collective-permute-start | bytes 442376 | tf_op jit(solution)/shard_map/ppermute | solution.py:26
  32.9 13.6 %collective-permute-start.21 = (bf16[64,1152]{1,0:T(8,128)(2,1)S(1)}, bf16[64,1152]{1,0:T(8,128)(2,1)S(1)}, u32[]{:S(2)}, u32[]{:S(2)}) collective-permute-start(bf16[64,1152]{1,0:T(8,128)(2,1)S(1)} %collective-permute-done.2.refs_3_), channel_id=1, source_target_pairs={{0,56},{8,0},{16,8},{24,16},{32,24},{40,32},{48,40},{56,48},{1,57}... | collective-permute-start | bytes 442376 | tf_op jit(solution)/shard_map/ppermute | solution.py:26
  35.9 12.3 %collective-permute-start.20 = (bf16[64,1152]{1,0:T(8,128)(2,1)S(1)}, bf16[64,1152]{1,0:T(8,128)(2,1)S(1)}, u32[]{:S(2)}, u32[]{:S(2)}) collective-permute-start(bf16[64,1152]{1,0:T(8,128)(2,1)S(1)} %collective-permute-done.1.refs_2_), channel_id=1, source_target_pairs={{0,56},{8,0},{16,8},{24,16},{32,24},{40,32},{48,40},{56,48},{1,57}... | collective-permute-start | bytes 442376 | tf_op jit(solution)/shard_map/ppermute | solution.py:26
  36.9 13.3 %collective-permute-start.19 = (bf16[64,1152]{1,0:T(8,128)(2,1)S(1)}, bf16[64,1152]{1,0:T(8,128)(2,1)S(1)}, u32[]{:S(2)}, u32[]{:S(2)}) collective-permute-start(bf16[64,1152]{1,0:T(8,128)(2,1)S(1)} %collective-permute-done.refs_1_), channel_id=1, source_target_pairs={{0,8},{8,16},{16,24},{24,32},{32,40},{40,48},{48,56},{56,0},{1,9},... | collective-permute-start | bytes 442376 | tf_op jit(solution)/shard_map/ppermute | solution.py:26
  37.9 5.9 %collective-permute-start.4 = (bf16[64,1024]{1,0:T(8,128)(2,1)S(1)}, bf16[64,1024]{1,0:T(8,128)(2,1)S(1)}, u32[]{:S(2)}, u32[]{:S(2)}) collective-permute-start(bf16[64,1024]{1,0:T(8,128)(2,1)S(1)} %get-tuple-element.46), channel_id=1, source_target_pairs={{0,2},{1,3},{2,4},{3,5},{4,6},{5,7},{6,0},{7,1},{8,10},{9,11},{10,... | collective-permute-start | bytes 393224 | tf_op jit(solution)/shard_map/ppermute | solution.py:26
  43.8 14.6 %collective-permute-start.5 = (bf16[64,1024]{1,0:T(8,128)(2,1)S(1)}, bf16[64,1024]{1,0:T(8,128)(2,1)S(1)}, u32[]{:S(2)}, u32[]{:S(2)}) collective-permute-start(bf16[64,1024]{1,0:T(8,128)(2,1)S(1)} %get-tuple-element.47), channel_id=1, source_target_pairs={{0,3},{1,4},{2,5},{3,6},{4,7},{5,0},{6,1},{7,2},{8,11},{9,12},{10,... | collective-permute-start | bytes 393224 | tf_op jit(solution)/shard_map/ppermute | solution.py:26
  44.0 14.4 %collective-permute-start.6 = (bf16[64,1024]{1,0:T(8,128)(2,1)S(1)}, bf16[64,1024]{1,0:T(8,128)(2,1)S(1)}, u32[]{:S(2)}, u32[]{:S(2)}) collective-permute-start(bf16[64,1024]{1,0:T(8,128)(2,1)S(1)} %get-tuple-element.48), channel_id=1, source_target_pairs={{0,4},{1,5},{2,6},{3,7},{4,0},{5,1},{6,2},{7,3},{8,12},{9,13},{10,... | collective-permute-start | bytes 393224 | tf_op jit(solution)/shard_map/ppermute | solution.py:26
  46.5 11.9 %collective-permute-start.7 = (bf16[64,1024]{1,0:T(8,128)(2,1)S(1)}, bf16[64,1024]{1,0:T(8,128)(2,1)S(1)}, u32[]{:S(2)}, u32[]{:S(2)}) collective-permute-start(bf16[64,1024]{1,0:T(8,128)(2,1)S(1)} %get-tuple-element.49), channel_id=1, source_target_pairs={{0,5},{1,6},{2,7},{3,0},{4,1},{5,2},{6,3},{7,4},{8,13},{9,14},{10,... | collective-permute-start | bytes 393224 | tf_op jit(solution)/shard_map/ppermute | solution.py:26
  48.2 10.3 %collective-permute-start.8 = (bf16[64,1024]{1,0:T(8,128)(2,1)S(1)}, bf16[64,1024]{1,0:T(8,128)(2,1)S(1)}, u32[]{:S(2)}, u32[]{:S(2)}) collective-permute-start(bf16[64,1024]{1,0:T(8,128)(2,1)S(1)} %get-tuple-element.50), channel_id=1, source_target_pairs={{0,6},{1,7},{2,0},{3,1},{4,2},{5,3},{6,4},{7,5},{8,14},{9,15},{10,... | collective-permute-start | bytes 393224 | tf_op jit(solution)/shard_map/ppermute | solution.py:26
  50.2 8.3 %collective-permute-start.9 = (bf16[64,1024]{1,0:T(8,128)(2,1)S(1)}, bf16[64,1024]{1,0:T(8,128)(2,1)S(1)}, u32[]{:S(2)}, u32[]{:S(2)}) collective-permute-start(bf16[64,1024]{1,0:T(8,128)(2,1)S(1)} %get-tuple-element.51), channel_id=1, source_target_pairs={{0,7},{1,0},{2,1},{3,2},{4,3},{5,4},{6,5},{7,6},{8,15},{9,8},{10,9... | collective-permute-start | bytes 393224 | tf_op jit(solution)/shard_map/ppermute | solution.py:26
  52.7 0.7 copy-start.8
  53.4 30.1 %all-to-all-start.2 = ((bf16[8,64,1024]{2,1,0:T(8,128)(2,1)}), bf16[8,64,1024]{2,1,0:T(8,128)(2,1)S(1)}, u32[]{:S(2)}, u32[]{:S(2)}) async-start(bf16[8,64,1024]{2,1,0:T(8,128)(2,1)} %bitcast.9), calls=%async_computation.2 | async-start | bytes 2097152 | tf_op jit(solution)/shard_map/all_to_all | solution.py:284
  58.5 2.2 %copy-start = (bf16[2,1024,1024]{2,1,0:T(8,128)(2,1)S(1)}, bf16[2,1024,1024]{2,1,0:T(8,128)(2,1)}, u32[]{:S(2)}) copy-start(bf16[2,1024,1024]{2,1,0:T(8,128)(2,1)} %weight_ref.6) | copy-start | bytes 12582916
  63.1 9.3 %collective-permute-start.10 = (bf16[128,1024]{1,0:T(8,128)(2,1)S(1)}, bf16[128,1024]{1,0:T(8,128)(2,1)S(1)}, u32[]{:S(2)}, u32[]{:S(2)}) collective-permute-start(bf16[128,1024]{1,0:T(8,128)(2,1)S(1)} %get-tuple-element.53), channel_id=1, source_target_pairs={{0,192},{64,0},{128,64},{192,128},{1,193},{65,1},{129,65},{193,129... | collective-permute-start | bytes 786440 | tf_op jit(solution)/shard_map/ppermute | solution.py:26
  64.4 10.7 %collective-permute-start.11 = (bf16[128,1024]{1,0:T(8,128)(2,1)S(1)}, bf16[128,1024]{1,0:T(8,128)(2,1)S(1)}, u32[]{:S(2)}, u32[]{:S(2)}) collective-permute-start(bf16[128,1024]{1,0:T(8,128)(2,1)S(1)} %get-tuple-element.54), channel_id=1, source_target_pairs={{0,128},{64,192},{128,0},{192,64},{1,129},{65,193},{129,1},{193,65... | collective-permute-start | bytes 786440 | tf_op jit(solution)/shard_map/ppermute | solution.py:26
  65.8 14.5 %collective-permute-start.12 = (bf16[128,1024]{1,0:T(8,128)(2,1)S(1)}, bf16[128,1024]{1,0:T(8,128)(2,1)S(1)}, u32[]{:S(2)}, u32[]{:S(2)}) collective-permute-start(bf16[128,1024]{1,0:T(8,128)(2,1)S(1)} %get-tuple-element.55), channel_id=1, source_target_pairs={{0,64},{64,128},{128,192},{192,0},{1,65},{65,129},{129,193},{193,1... | collective-permute-start | bytes 786440 | tf_op jit(solution)/shard_map/ppermute | solution.py:26
  80.5 11.7 %collective-permute-start.15 = (bf16[128,1024]{1,0:T(8,128)(2,1)S(1)}, bf16[128,1024]{1,0:T(8,128)(2,1)S(1)}, u32[]{:S(2)}, u32[]{:S(2)}) collective-permute-start(bf16[128,1024]{1,0:T(8,128)(2,1)S(1)} %multiply_convert_fusion.1.refs_0_), channel_id=1, source_target_pairs={{0,192},{64,0},{128,64},{192,128},{1,193},{65,1},{129,65},{193,129... | collective-permute-start | bytes 786440 | tf_op jit(solution)/shard_map/ppermute | solution.py:26
  81.2 12.4 %collective-permute-start.14 = (bf16[128,1024]{1,0:T(8,128)(2,1)S(1)}, bf16[128,1024]{1,0:T(8,128)(2,1)S(1)}, u32[]{:S(2)}, u32[]{:S(2)}) collective-permute-start(bf16[128,1024]{1,0:T(8,128)(2,1)S(1)} %multiply_convert_fusion.1.refs_0_), channel_id=1, source_target_pairs={{0,128},{64,192},{128,0},{192,64},{1,129},{65,193},{129,1},{193,65... | collective-permute-start | bytes 786440 | tf_op jit(solution)/shard_map/ppermute | solution.py:26
  82.7 14.9 %collective-permute-start.13 = (bf16[128,1024]{1,0:T(8,128)(2,1)S(1)}, bf16[128,1024]{1,0:T(8,128)(2,1)S(1)}, u32[]{:S(2)}, u32[]{:S(2)}) collective-permute-start(bf16[128,1024]{1,0:T(8,128)(2,1)S(1)} %multiply_convert_fusion.1.refs_0_), channel_id=1, source_target_pairs={{0,64},{64,128},{128,192},{192,0},{1,65},{65,129},{129,193},{193,1... | collective-permute-start | bytes 786440 | tf_op jit(solution)/shard_map/ppermute | solution.py:26
  83.5 2.2 %copy-start.1 = (bf16[2,1024,1024]{2,1,0:T(8,128)(2,1)S(1)}, bf16[2,1024,1024]{2,1,0:T(8,128)(2,1)}, u32[]{:S(2)}) copy-start(bf16[2,1024,1024]{2,1,0:T(8,128)(2,1)} %weight_ref.6) | copy-start | bytes 12582916
  85.7 11.9 %copy-start.2 = (bf16[2,1024,1024]{2,1,0:T(8,128)(2,1)S(1)}, bf16[2,1024,1024]{2,1,0:T(8,128)(2,1)}, u32[]{:S(2)}) copy-start(bf16[2,1024,1024]{2,1,0:T(8,128)(2,1)} %weight_ref.7) | copy-start | bytes 12582916
  88.9 16.4 %collective-permute-start.23 = (bf16[128,1024]{1,0:T(8,128)(2,1)}, bf16[128,1024]{1,0:T(8,128)(2,1)}, u32[]{:S(2)}, u32[]{:S(2)}) collective-permute-start(bf16[128,1024]{1,0:T(8,128)(2,1)} %get-tuple-element.64), channel_id=1, source_target_pairs={{0,192},{64,0},{128,64},{192,128},{1,193},{65,1},{129,65},{193,129... | collective-permute-start | bytes 786440 | tf_op jit(solution)/shard_map/ppermute | solution.py:26
  91.4 14.0 %collective-permute-start.24 = (bf16[128,1024]{1,0:T(8,128)(2,1)}, bf16[128,1024]{1,0:T(8,128)(2,1)}, u32[]{:S(2)}, u32[]{:S(2)}) collective-permute-start(bf16[128,1024]{1,0:T(8,128)(2,1)} %get-tuple-element.65), channel_id=1, source_target_pairs={{0,128},{64,192},{128,0},{192,64},{1,129},{65,193},{129,1},{193,65... | collective-permute-start | bytes 786440 | tf_op jit(solution)/shard_map/ppermute | solution.py:26
  92.2 15.2 %collective-permute-start.25 = (bf16[128,1024]{1,0:T(8,128)(2,1)}, bf16[128,1024]{1,0:T(8,128)(2,1)}, u32[]{:S(2)}, u32[]{:S(2)}) collective-permute-start(bf16[128,1024]{1,0:T(8,128)(2,1)} %get-tuple-element.66), channel_id=1, source_target_pairs={{0,64},{64,128},{128,192},{192,0},{1,65},{65,129},{129,193},{193,1... | collective-permute-start | bytes 786440 | tf_op jit(solution)/shard_map/ppermute | solution.py:26
  101.0 37.6 %all-to-all-start.1 = ((bf16[8,64,1024]{2,1,0:T(8,128)(2,1)}), bf16[8,64,1024]{2,1,0:T(8,128)(2,1)S(1)}, u32[]{:S(2)}, u32[]{:S(2)}) async-start(bf16[8,64,1024]{2,1,0:T(8,128)(2,1)} %bitcast.7), calls=%async_computation.1 | async-start | bytes 2097152 | tf_op jit(solution)/shard_map/all_to_all | solution.py:318
  107.4 40.0 %copy-start.9 = (bf16[256,512]{1,0:T(8,128)(2,1)S(1)}, bf16[256,512]{1,0:T(8,128)(2,1)}, u32[]{:S(2)}) copy-start(bf16[256,512]{1,0:T(8,128)(2,1)} %copy-done.8) | copy-start | bytes 786436
  108.8 9.3 %collective-permute-start.28 = (bf16[128,1024]{1,0:T(8,128)(2,1)S(1)}, bf16[128,1024]{1,0:T(8,128)(2,1)S(1)}, u32[]{:S(2)}, u32[]{:S(2)}) collective-permute-start(bf16[128,1024]{1,0:T(8,128)(2,1)S(1)} %multiply_convert_fusion.refs_0_), channel_id=1, source_target_pairs={{0,192},{64,0},{128,64},{192,128},{1,193},{65,1},{129,65},{193,129... | collective-permute-start | bytes 786440 | tf_op jit(solution)/shard_map/ppermute | solution.py:26
  110.0 10.7 %collective-permute-start.27 = (bf16[128,1024]{1,0:T(8,128)(2,1)S(1)}, bf16[128,1024]{1,0:T(8,128)(2,1)S(1)}, u32[]{:S(2)}, u32[]{:S(2)}) collective-permute-start(bf16[128,1024]{1,0:T(8,128)(2,1)S(1)} %multiply_convert_fusion.refs_0_), channel_id=1, source_target_pairs={{0,128},{64,192},{128,0},{192,64},{1,129},{65,193},{129,1},{193,65... | collective-permute-start | bytes 786440 | tf_op jit(solution)/shard_map/ppermute | solution.py:26
  111.0 13.3 %collective-permute-start.26 = (bf16[128,1024]{1,0:T(8,128)(2,1)S(1)}, bf16[128,1024]{1,0:T(8,128)(2,1)S(1)}, u32[]{:S(2)}, u32[]{:S(2)}) collective-permute-start(bf16[128,1024]{1,0:T(8,128)(2,1)S(1)} %multiply_convert_fusion.refs_0_), channel_id=1, source_target_pairs={{0,64},{64,128},{128,192},{192,0},{1,65},{65,129},{129,193},{193,1... | collective-permute-start | bytes 786440 | tf_op jit(solution)/shard_map/ppermute | solution.py:26
  124.3 2.2 %copy-start.3 = (bf16[2,1024,1024]{2,1,0:T(8,128)(2,1)S(1)}, bf16[2,1024,1024]{2,1,0:T(8,128)(2,1)}, u32[]{:S(2)}) copy-start(bf16[2,1024,1024]{2,1,0:T(8,128)(2,1)} %weight_ref.7) | copy-start | bytes 12582916
  129.6 5.4 %collective-permute-start.29 = (bf16[64,1024]{1,0:T(8,128)(2,1)S(1)}, bf16[64,1024]{1,0:T(8,128)(2,1)S(1)}, u32[]{:S(2)}, u32[]{:S(2)}) collective-permute-start(bf16[64,1024]{1,0:T(8,128)(2,1)S(1)} %get-tuple-element.68), channel_id=1, source_target_pairs={{0,1},{1,2},{2,3},{3,4},{4,5},{5,6},{6,7},{7,0},{8,9},{9,10},{10,1... | collective-permute-start | bytes 393224 | tf_op jit(solution)/shard_map/ppermute | solution.py:26
  129.6 7.4 %collective-permute-start.30 = (bf16[64,1024]{1,0:T(8,128)(2,1)S(1)}, bf16[64,1024]{1,0:T(8,128)(2,1)S(1)}, u32[]{:S(2)}, u32[]{:S(2)}) collective-permute-start(bf16[64,1024]{1,0:T(8,128)(2,1)S(1)} %get-tuple-element.69), channel_id=1, source_target_pairs={{0,2},{1,3},{2,4},{3,5},{4,6},{5,7},{6,0},{7,1},{8,10},{9,11},{10,... | collective-permute-start | bytes 393224 | tf_op jit(solution)/shard_map/ppermute | solution.py:26
  130.3 9.1 %collective-permute-start.31 = (bf16[64,1024]{1,0:T(8,128)(2,1)}, bf16[64,1024]{1,0:T(8,128)(2,1)S(1)}, u32[]{:S(2)}, u32[]{:S(2)}) collective-permute-start(bf16[64,1024]{1,0:T(8,128)(2,1)} %get-tuple-element.70), channel_id=1, source_target_pairs={{0,3},{1,4},{2,5},{3,6},{4,7},{5,0},{6,1},{7,2},{8,11},{9,12},{10,... | collective-permute-start | bytes 393224 | tf_op jit(solution)/shard_map/ppermute | solution.py:26
  132.1 9.6 %collective-permute-start.32 = (bf16[64,1024]{1,0:T(8,128)(2,1)}, bf16[64,1024]{1,0:T(8,128)(2,1)S(1)}, u32[]{:S(2)}, u32[]{:S(2)}) collective-permute-start(bf16[64,1024]{1,0:T(8,128)(2,1)} %get-tuple-element.71), channel_id=1, source_target_pairs={{0,4},{1,5},{2,6},{3,7},{4,0},{5,1},{6,2},{7,3},{8,12},{9,13},{10,... | collective-permute-start | bytes 393224 | tf_op jit(solution)/shard_map/ppermute | solution.py:26
  133.8 9.6 %collective-permute-start.33 = (bf16[64,1024]{1,0:T(8,128)(2,1)S(1)}, bf16[64,1024]{1,0:T(8,128)(2,1)S(1)}, u32[]{:S(2)}, u32[]{:S(2)}) collective-permute-start(bf16[64,1024]{1,0:T(8,128)(2,1)S(1)} %get-tuple-element.72), channel_id=1, source_target_pairs={{0,5},{1,6},{2,7},{3,0},{4,1},{5,2},{6,3},{7,4},{8,13},{9,14},{10,... | collective-permute-start | bytes 393224 | tf_op jit(solution)/shard_map/ppermute | solution.py:26
  135.1 12.4 %collective-permute-start.34 = (bf16[64,1024]{1,0:T(8,128)(2,1)S(1)}, bf16[64,1024]{1,0:T(8,128)(2,1)S(1)}, u32[]{:S(2)}, u32[]{:S(2)}) collective-permute-start(bf16[64,1024]{1,0:T(8,128)(2,1)S(1)} %get-tuple-element.73), channel_id=1, source_target_pairs={{0,6},{1,7},{2,0},{3,1},{4,2},{5,3},{6,4},{7,5},{8,14},{9,15},{10,... | collective-permute-start | bytes 393224 | tf_op jit(solution)/shard_map/ppermute | solution.py:26
  137.1 10.4 %collective-permute-start.35 = (bf16[64,1024]{1,0:T(8,128)(2,1)S(1)}, bf16[64,1024]{1,0:T(8,128)(2,1)}, u32[]{:S(2)}, u32[]{:S(2)}) collective-permute-start(bf16[64,1024]{1,0:T(8,128)(2,1)S(1)} %get-tuple-element.74), channel_id=1, source_target_pairs={{0,7},{1,0},{2,1},{3,2},{4,3},{5,4},{6,5},{7,6},{8,15},{9,8},{10,9... | collective-permute-start | bytes 393224 | tf_op jit(solution)/shard_map/ppermute | solution.py:26
  139.4 12.7 %collective-permute-start.16 = (bf16[64,1024]{1,0:T(8,128)(2,1)S(1)}, bf16[64,1024]{1,0:T(8,128)(2,1)S(1)}, u32[]{:S(2)}, u32[]{:S(2)}) collective-permute-start(bf16[64,1024]{1,0:T(8,128)(2,1)S(1)} %get-tuple-element.57), channel_id=1, source_target_pairs={{0,56},{8,0},{16,8},{24,16},{32,24},{40,32},{48,40},{56,48},{1,57}... | collective-permute-start | bytes 393224 | tf_op jit(solution)/shard_map/ppermute | solution.py:26
  141.6 11.6 %collective-permute-start.17 = (bf16[64,1024]{1,0:T(8,128)(2,1)S(1)}, bf16[64,1024]{1,0:T(8,128)(2,1)S(1)}, u32[]{:S(2)}, u32[]{:S(2)}) collective-permute-start(bf16[64,1024]{1,0:T(8,128)(2,1)S(1)} %get-tuple-element.58), channel_id=1, source_target_pairs={{0,8},{8,16},{16,24},{24,32},{32,40},{40,48},{48,56},{56,0},{1,9},... | collective-permute-start | bytes 393224 | tf_op jit(solution)/shard_map/ppermute | solution.py:26
  143.4 12.5 %collective-permute-start.18 = (bf16[64,1024]{1,0:T(8,128)(2,1)S(1)}, bf16[64,1024]{1,0:T(8,128)(2,1)S(1)}, u32[]{:S(2)}, u32[]{:S(2)}) collective-permute-start(bf16[64,1024]{1,0:T(8,128)(2,1)S(1)} %get-tuple-element.59), channel_id=1, source_target_pairs={{0,32},{8,40},{16,48},{24,56},{32,0},{40,8},{48,16},{56,24},{1,33}... | collective-permute-start | bytes 393224 | tf_op jit(solution)/shard_map/ppermute | solution.py:26
  149.1 13.2 %collective-permute-start.36 = (bf16[64,1024]{1,0:T(8,128)(2,1)S(1)}, bf16[64,1024]{1,0:T(8,128)(2,1)S(1)}, u32[]{:S(2)}, u32[]{:S(2)}) collective-permute-start(bf16[64,1024]{1,0:T(8,128)(2,1)S(1)} %get-tuple-element.75), channel_id=1, source_target_pairs={{0,48},{8,56},{16,0},{24,8},{32,16},{40,24},{48,32},{56,40},{1,49}... | collective-permute-start | bytes 393224 | tf_op jit(solution)/shard_map/ppermute | solution.py:26
  149.1 13.1 %collective-permute-start.37 = (bf16[64,1024]{1,0:T(8,128)(2,1)S(1)}, bf16[64,1024]{1,0:T(8,128)(2,1)S(1)}, u32[]{:S(2)}, u32[]{:S(2)}) collective-permute-start(bf16[64,1024]{1,0:T(8,128)(2,1)S(1)} %get-tuple-element.76), channel_id=1, source_target_pairs={{0,16},{8,24},{16,32},{24,40},{32,48},{40,56},{48,0},{56,8},{1,17}... | collective-permute-start | bytes 393224 | tf_op jit(solution)/shard_map/ppermute | solution.py:26
  152.1 15.4 %collective-permute-start.38 = (bf16[64,1024]{1,0:T(8,128)(2,1)S(1)}, bf16[64,1024]{1,0:T(8,128)(2,1)S(1)}, u32[]{:S(2)}, u32[]{:S(2)}) collective-permute-start(bf16[64,1024]{1,0:T(8,128)(2,1)S(1)} %get-tuple-element.77), channel_id=1, source_target_pairs={{0,40},{8,48},{16,56},{24,0},{32,8},{40,16},{48,24},{56,32},{1,41}... | collective-permute-start | bytes 393224 | tf_op jit(solution)/shard_map/ppermute | solution.py:26
  153.3 15.6 %collective-permute-start.39 = (bf16[64,1024]{1,0:T(8,128)(2,1)S(1)}, bf16[64,1024]{1,0:T(8,128)(2,1)S(1)}, u32[]{:S(2)}, u32[]{:S(2)}) collective-permute-start(bf16[64,1024]{1,0:T(8,128)(2,1)S(1)} %get-tuple-element.78), channel_id=1, source_target_pairs={{0,24},{8,32},{16,40},{24,48},{32,56},{40,0},{48,8},{56,16},{1,25}... | collective-permute-start | bytes 393224 | tf_op jit(solution)/shard_map/ppermute | solution.py:26

commit v3 on v2

--- a/solution.py
+++ b/solution.py
@@ -10,7 +10,9 @@
 CAP_SLOTS = 2
 HOLD_CAP = 3
 META_COLS = 128
-TILE = 512
+TILE = 256
+WIDE = 1024
+COST = 4 << 30
 VMEM_LIMIT = 16 << 20
 BF = jnp.bfloat16
 F32 = jnp.float32
@@ -26,7 +28,7 @@
     return lax.ppermute(value, axis, [(source, (source + steps) % count) for source in range(count)])
 
 
-def local_call(kernel, inputs, outputs, scalars=(), hbm=(), scratch=(), flops=0):
+def local_call(kernel, inputs, outputs, scalars=(), hbm=(), scratch=()):
     moved = sum(a.size * a.dtype.itemsize for a in [*hbm, *inputs, *outputs])
     vmem = pl.BlockSpec(memory_space=pltpu.VMEM)
     return pl.pallas_call(
@@ -37,7 +39,7 @@
         out_specs=[vmem] * len(outputs),
         out_shape=outputs,
         scratch_shapes=list(scratch),
-        cost_estimate=pl.CostEstimate(flops=flops, bytes_accessed=moved, transcendentals=0),
+        cost_estimate=pl.CostEstimate(flops=COST, bytes_accessed=moved, transcendentals=0),
         compiler_params=pltpu.CompilerParams(vmem_limit_bytes=VMEM_LIMIT),
     )(*scalars, *hbm, *inputs)
 
@@ -123,27 +125,44 @@
     return (expert * CAP_SLOTS + index % CAP_SLOTS) + 256 * ((index % unit) // CAP_SLOTS)
 
 
-def gather_kernel(cells, per_dev, chosen, block_rows, pieces_in, ways, me_ref, *refs):
-    pieces, outs = refs[:pieces_in], refs[pieces_in:-2]
-    high_ref, low_ref = refs[-2:]
+def keys_of(info, block_rows):
+    mine = 256.0 * (iota(info.shape, 0) // block_rows).astype(F32)
+    return jnp.where(info < 0, -1.0, info + mine)
+
+
+def gather_kernel(cells, per_dev, chosen, block_rows, pieces_in, way, me_ref, *refs):
+    pieces, outs, info_ref = refs[:pieces_in], refs[pieces_in:-1], refs[-1]
     width = outs[0].shape[1]
     slots = sum(out.shape[0] for out in outs)
     blocks = pieces_in * pieces[0].shape[0] // block_rows
-    tok = jnp.concatenate([p[:, :width] for p in pieces], axis=0)
-    info = jnp.concatenate([p[:, width:] for p in pieces], axis=0).astype(F32)
-    count = tok.shape[0]
-    mine = 256.0 * (iota((count, META_COLS), 0) // block_rows).astype(F32)
-    keyed = jnp.where(info < 0, -1.0, info + mine)
-    turned = keyed.T
-    wanted = slot_code(me_ref, iota((slots, 1), 0), cells, per_dev, blocks, ways[0]).astype(F32)
+    info = jnp.concatenate([p[:, width:] for p in pieces], axis=0)
+    info_ref[...] = info
+    count = info.shape[0]
+    turned = keys_of(info.astype(F32), block_rows).T
+    wanted = slot_code(me_ref, iota((slots, 1), 0), cells, per_dev, blocks, way).astype(F32)
     pick = jnp.zeros((slots, count), F32)
     for k in range(chosen):
         pick = jnp.where(turned[k : k + 1, :] == wanted, 1.0, pick)
-    rows = jnp.dot(pick.astype(BF), tok, preferred_element_type=F32).astype(BF)
+    pick = pick.astype(BF)
     each = slots // len(outs)
-    for n, out in enumerate(outs):
-        out[...] = rows[n * each : (n + 1) * each]
-    wanted = slot_code(me_ref, iota((1, slots), 1), cells, per_dev, blocks, ways[1]).astype(F32)
+
+    def columns(j, _):
+        cols = pl.ds(pl.multiple_of(j * TILE, TILE), TILE)
+        tok = jnp.concatenate([p[:, cols] for p in pieces], axis=0)
+        rows = jnp.dot(pick, tok, preferred_element_type=F32).astype(BF)
+        for n, out in enumerate(outs):
+            out[:, cols] = rows[n * each : (n + 1) * each]
+        return 0
+
+    lax.fori_loop(0, width // TILE, columns, 0)
+
+
+def mix_kernel(cells, per_dev, chosen, block_rows, way, me_ref, info_ref, high_ref, low_ref):
+    count, slots = high_ref.shape
+    blocks = count // block_rows
+    info = info_ref[...].astype(F32)
+    keyed = keys_of(info, block_rows)
+    wanted = slot_code(me_ref, iota((1, slots), 1), cells, per_dev, blocks, way).astype(F32)
     high = jnp.zeros((count, slots), F32)
     low = jnp.zeros((count, slots), F32)
     for k in range(chosen):
@@ -174,16 +193,16 @@
         rows = jnp.concatenate(parts, axis=0)
 
         def columns(j, _):
-            cols = pl.ds(pl.multiple_of(j * TILE, TILE), TILE)
+            cols = pl.ds(pl.multiple_of(j * WIDE, WIDE), WIDE)
             result = jnp.dot(rows, weight_ref[s, :, cols], preferred_element_type=F32)
             for k, out in enumerate(outs):
                 out[s * half : (s + 1) * half, cols] = result[k * half : (k + 1) * half].astype(out.dtype)
             return 0
 
-        lax.fori_loop(0, weight_ref.shape[2] // TILE, columns, 0)
-
-
-def down_kernel(groups, arrival_way, me_ref, weight_ref, *refs):
+        lax.fori_loop(0, weight_ref.shape[2] // WIDE, columns, 0)
+
+
+def down_kernel(groups, me_ref, weight_ref, *refs):
     pieces, outs = refs[:groups], refs[groups:-1]
     rows_ref = refs[-1]
     cells, per_dev, unit, _ = rows_ref.shape
@@ -194,13 +213,13 @@
         rows = jnp.concatenate([piece[s * half : (s + 1) * half, :] for piece in pieces], axis=0)
 
         def columns(j, _):
-            cols = pl.ds(pl.multiple_of(j * TILE, TILE), TILE)
+            cols = pl.ds(pl.multiple_of(j * WIDE, WIDE), WIDE)
             result = jnp.dot(rows, weight_ref[s, :, cols], preferred_element_type=F32).astype(BF)
             for k in range(groups):
                 start = lax.rem(me_ref[0] + groups - k, groups) * span
                 for n in range(span):
                     index = start + n
-                    if arrival_way:
+                    if len(outs) == 1:
                         index = lax.rem(me_ref[2] + cells - index, cells)
                     else:
                         index = lax.rem(index + cells - me_ref[2], cells)
@@ -208,7 +227,7 @@
                     target[index, s, :, cols] = result[first : first + unit]
             return 0
 
-        lax.fori_loop(0, weight_ref.shape[2] // TILE, columns, 0)
+        lax.fori_loop(0, weight_ref.shape[2] // WIDE, columns, 0)
     if len(outs) > 1:
         for n, out in enumerate(outs):
             out[...] = rows_ref[n].reshape(out.shape)
@@ -216,12 +235,18 @@
 
 def combine_kernel(arrivals, high_ref, low_ref, *refs):
     sources, outs = refs[:arrivals], refs[arrivals:]
-    rows = jnp.concatenate([source[...] for source in sources], axis=0)
-    total = jnp.dot(high_ref[...], rows, preferred_element_type=F32)
-    total = total + jnp.dot(low_ref[...], rows, preferred_element_type=F32)
     count = outs[0].shape[0]
-    for n, out in enumerate(outs):
-        out[...] = total[n * count : (n + 1) * count].astype(out.dtype)
+
+    def columns(j, _):
+        cols = pl.ds(pl.multiple_of(j * TILE, TILE), TILE)
+        rows = jnp.concatenate([source[:, cols] for source in sources], axis=0)
+        total = jnp.dot(high_ref[...], rows, preferred_element_type=F32)
+        total = total + jnp.dot(low_ref[...], rows, preferred_element_type=F32)
+        for n, out in enumerate(outs):
+            out[:, cols] = total[n * count : (n + 1) * count].astype(out.dtype)
+        return 0
+
+    lax.fori_loop(0, outs[0].shape[1] // TILE, columns, 0)
 
 
 def layer(tokens, expert_ids, scores, up_weight, down_weight, swap_slot):
@@ -271,13 +296,13 @@
         tokens_in = [chunk[offset] for offset in chunk]
         one = jax.ShapeDtypeStruct((cell_rows, part_width), BF)
         whole = jax.ShapeDtypeStruct((slots, part_width), BF)
-        weights = [jax.ShapeDtypeStruct((len(chunk) * dp_rows, slots), BF)] * 2
-        *rows, high, low = local_call(
+        *rows, info = local_call(
             functools.partial(
-                gather_kernel, cells, per_dev, chosen, tok_rows, len(chunk), (0, -1) if n else (1, 0)
+                gather_kernel, cells, per_dev, chosen, tok_rows, len(chunk), 0 if n else 1
             ),
             tokens_in,
-            ([whole] if n else [one] * cells) + weights,
+            ([whole] if n else [one] * cells)
+            + [jax.ShapeDtypeStruct((len(chunk) * dp_rows, META_COLS), BF)],
             scalars=(me,),
         )
         if n:
@@ -291,7 +316,12 @@
             [jax.ShapeDtypeStruct((count, hidden_width), BF if k else F32) for k in range(groups)],
             scalars=(me,),
             scratch=scratch,
-            flops=2 * slots * part_width * hidden_width,
+        )
+        high, low = local_call(
+            functools.partial(mix_kernel, cells, per_dev, chosen, tok_rows, -n),
+            [info],
+            [jax.ShapeDtypeStruct((len(chunk) * dp_rows, slots), BF)] * 2,
+            scalars=(me,),
         )
         chunks.append((list(chunk), high, low, sent))
     pieces = []
@@ -305,12 +335,11 @@
     for n, (offsets, high, low, sent) in enumerate(chunks):
         hidden = pieces[n]
         result = local_call(
-            functools.partial(down_kernel, groups, n == 0),
+            functools.partial(down_kernel, groups),
             [down_weight] + hidden,
             [one] * cells if n else [jax.ShapeDtypeStruct(rows_shape, BF)],
             scalars=(me,),
             scratch=scratch,
-            flops=2 * slots * part_width * hidden_width,
         )
         if n:
             back = [result[0]] + [shift(result[k], "yc", k) for k in range(1, cells)]
@@ -320,13 +349,17 @@
         sums = local_call(
             functools.partial(combine_kernel, len(back)),
             [high, low] + back,
-            [jax.ShapeDtypeStruct((dp_rows, part_width), BF if offset else F32) for offset in offsets],
-            flops=4 * slots * part_width * len(offsets) * dp_rows,
-        )
-        for offset, value in zip(offsets, sums):
-            if offset:
-                value = shift(value, "z", -offset).astype(F32)
-            total = value if total is None else total + value
+            [jax.ShapeDtypeStruct((dp_rows, part_width), F32 if offset in (0, 2, -2) else BF) for offset in offsets],
+        )
+        sums = dict(zip(offsets, sums))
+        if n:
+            for way in (1, -1):
+                passed = shift(sums[3 * way], "z", -way).astype(F32) + sums[2 * way]
+                total = total + shift(passed.astype(BF), "z", -2 * way).astype(F32)
+        else:
+            total = sums[0]
+            for offset in offsets[1:]:
+                total = total + shift(sums[offset], "z", -offset).astype(F32)
     parts = total.astype(BF).reshape(groups, tok_rows, part_width)
     parts = lax.all_to_all(parts, "dp", 0, 0, tiled=True)
     return parts.transpose(1, 0, 2).reshape(tok_rows, width)

time: 181 us -> 186 us (1.028); the launches traced: 178 us -> 185 us
  starting transfers between devices: 67.4 us -> 76.5 us
  local copies, waits for them, and re-layouts: 10.9 us -> 7.98 us
  waiting for transfers between devices: 59.5 us -> 62 us
    ppermute x40, starting transfers between devices: 58.1 us -> 66.1 us  [shift(): lax.ppermute(value, axis, [(source, (source + steps) % count) for source...]
    unnamed x20 -> x16, local copies, waits for them, and re-layouts: 10.2 us -> 7.31 us
    ppermute x40, waiting for transfers between devices: 59.4 us -> 62 us  [shift(): lax.ppermute(value, axis, [(source, (source + steps) % count) for source...]
    pallas_call x9 -> x11, Pallas kernels: 19.8 us -> 19.5 us  [local_call(): pl.pallas_call(kernel, in_specs=[pl.BlockSpec(memory_space=pltpu.SMEM)] *...]
  transfers between devices with their start and end apart: 42 -> 42, of which waited for: 15 -> 22; matrix products, arithmetic and copies ran while one was open for 1% -> 0% of each run, Pallas kernels for 10% -> 8%
where the time goes in v3:
time: 186 us; the launch traced here: 185 us
  starting transfers between devices  76.5 us (41%)
  waiting for transfers between devices  62 us (33%)
  Pallas kernels  19.5 us (10%)
  blocking collectives  18.7 us (10%)
  local copies, waits for them, and re-layouts  7.98 us (4%)
    ppermute x40, starting transfers between devices, shift(): lax.ppermute(value, axis, [(source, (source + steps) % count) for source...  66.1 us
    ppermute x40, waiting for transfers between devices, shift(): lax.ppermute(value, axis, [(source, (source + steps) % count) for source...  62 us
    pallas_call x11, Pallas kernels, local_call(): pl.pallas_call(kernel, in_specs=[pl.BlockSpec(memory_space=pltpu.SMEM)] *...  19.5 us
    all_to_all x1, blocking collectives, layer(): own = lax.all_to_all(payload, 'dp', 0, 0, tiled=True).reshape(dp_rows, full)  10.2 us
    all_to_all x1, blocking collectives, layer(): parts = lax.all_to_all(parts, 'dp', 0, 0, tiled=True)  8.53 us
    unnamed x16, local copies, waits for them, and re-layouts  7.31 us
    all_to_all x1, starting transfers between devices, layer(): lax.all_to_all(result[0].reshape(cells, cell_rows, part_width), 'yc', 0,...  5.44 us
    all_to_all x1, starting transfers between devices, layer(): lax.all_to_all(rows[0].reshape(cells, cell_rows, part_width), 'yc', 0, 0,...  4.93 us
  transfers between devices with their start and end apart: 42, of which 22 were waited for; matrix products, arithmetic and copies ran while one was open for 0% of the time, Pallas kernels for 8%

profile of v3, /device:TPU:8, one launch (start us, length us, event | category | flops | bytes accessed | tf_op | source)
XLA Modules:
  0.0 185.5 jit_solution(12982410134662399079)
XLA Ops:
  0.0 0.9 copy-done.4
  2.9 0.8 shard_map.64
  3.7 10.2 %all_to_all.20 = bf16[4,16,1152]{2,1,0:T(8,128)(2,1)S(1)} all-to-all(bf16[4,16,1152]{2,1,0:T(8,128)(2,1)S(1)} %shard_map.64), channel_id=1, replica_groups=mesh['dp'=4,'z'=8,'yc'=8] {'dp'}, dimensions={0} | all-to-all | bytes 294912 | tf_op jit(solution)/shard_map/all_to_all | solution.py:275
  13.9 7.2 %collective-permute-start.2 = (bf16[64,1152]{1,0:T(8,128)(2,1)S(1)}, bf16[64,1152]{1,0:T(8,128)(2,1)S(1)}, u32[]{:S(2)}, u32[]{:S(2)}) collective-permute-start(bf16[64,1152]{1,0:T(8,128)(2,1)S(1)} %bitcast.17), channel_id=1, source_target_pairs={{0,32},{8,40},{16,48},{24,56},{32,0},{40,8},{48,16},{56,24},{1,33}... | collective-permute-start | bytes 442376 | tf_op jit(solution)/shard_map/ppermute | solution.py:28
  21.2 1.9 %collective-permute-start = (bf16[64,1152]{1,0:T(8,128)(2,1)S(1)}, bf16[64,1152]{1,0:T(8,128)(2,1)S(1)}, u32[]{:S(2)}, u32[]{:S(2)}) collective-permute-start(bf16[64,1152]{1,0:T(8,128)(2,1)S(1)} %bitcast.19), channel_id=1, source_target_pairs={{0,8},{8,16},{16,24},{24,32},{32,40},{40,48},{48,56},{56,0},{1,9},... | collective-permute-start | bytes 442376 | tf_op jit(solution)/shard_map/ppermute | solution.py:28
  23.1 3.9 %collective-permute-done.2.refs_3_ = bf16[64,1152]{1,0:T(8,128)(2,1)S(1)} collective-permute-done((bf16[64,1152]{1,0:T(8,128)(2,1)S(1)}, bf16[64,1152]{1,0:T(8,128)(2,1)S(1)}, u32[]{:S(2)}, u32[]{:S(2)}) %collective-permute-start.2) | collective-permute-done | bytes 147488 | tf_op jit(solution)/shard_map/ppermute | solution.py:28
  27.0 1.0 collective-permute-start.22
  28.1 3.3 %collective-permute-start.21 = (bf16[64,1152]{1,0:T(8,128)(2,1)S(1)}, bf16[64,1152]{1,0:T(8,128)(2,1)S(1)}, u32[]{:S(2)}, u32[]{:S(2)}) collective-permute-start(bf16[64,1152]{1,0:T(8,128)(2,1)S(1)} %collective-permute-done.2.refs_3_), channel_id=1, source_target_pairs={{0,56},{8,0},{16,8},{24,16},{32,24},{40,32},{48,40},{56,48},{1,57}... | collective-permute-start | bytes 442376 | tf_op jit(solution)/shard_map/ppermute | solution.py:28
  31.9 1.5 collective-permute-start.20
  34.5 1.1 collective-permute-done.21.refs_2_
  35.6 1.6 collective-permute-done.20.refs_1_
  37.2 2.6 %collective-permute-done.19.refs_0_ = bf16[64,1152]{1,0:T(8,128)(2,1)S(1)} collective-permute-done((bf16[64,1152]{1,0:T(8,128)(2,1)S(1)}, bf16[64,1152]{1,0:T(8,128)(2,1)S(1)}, u32[]{:S(2)}, u32[]{:S(2)}) %collective-permute-start.19) | collective-permute-done | bytes 147488 | tf_op jit(solution)/shard_map/ppermute | solution.py:28
  39.8 3.0 %shard_map.70 = (bf16[512,1024]{1,0:T(8,128)(2,1)}, bf16[256,128]{1,0:T(8,128)(2,1)S(1)}) custom-call(s32[3]{0:T(128)S(1)} %pad_add_fusion.me_ref, bf16[64,1152]{1,0:T(8,128)(2,1)S(1)} %collective-permute-done.19.refs_0_, bf16[64,1152]{1,0:T(8,128)(2,1)S(1)} %collective-permute-done.20.refs_1_, bf16[64,1152]{1,0:T(8,128)(2,1)S(1)} %collective-permute-done.21.refs_2_, ...), custom_call_target="tpu_custom_call" | custom-call | flops 4294967296 | bytes 1703936 | tf_op jit(solution)/shard_map/pallas_call | solution.py:34
  42.8 4.9 %all-to-all-start.2 = ((bf16[8,64,1024]{2,1,0:T(8,128)(2,1)}), bf16[8,64,1024]{2,1,0:T(8,128)(2,1)S(1)}, u32[]{:S(2)}, u32[]{:S(2)}) async-start(bf16[8,64,1024]{2,1,0:T(8,128)(2,1)} %bitcast.9), calls=%async_computation.2 | async-start | bytes 2097152 | tf_op jit(solution)/shard_map/all_to_all | solution.py:309
  47.7 2.1 %shard_map.65 = (bf16[64,1024]{1,0:T(8,128)(2,1)S(1)}, bf16[64,1024]{1,0:T(8,128)(2,1)S(1)}, bf16[64,1024]{1,0:T(8,128)(2,1)S(1)}, bf16[64,1024]{1,0:T(8,128)(2,...) custom-call(s32[3]{0:T(128)S(1)} %pad_add_fusion.me_ref, ...), custom_call_target="tpu_custom_call" | custom-call | flops 4294967296 | bytes 1703936 | tf_op jit(solution)/shard_map/pallas_call | solution.py:34
  49.9 1.4 collective-permute-start.4
  51.4 0.8 collective-permute-start.5
  52.2 2.6 %collective-permute-start.6 = (bf16[64,1024]{1,0:T(8,128)(2,1)S(1)}, bf16[64,1024]{1,0:T(8,128)(2,1)S(1)}, u32[]{:S(2)}, u32[]{:S(2)}) collective-permute-start(bf16[64,1024]{1,0:T(8,128)(2,1)S(1)} %get-tuple-element.51), channel_id=1, source_target_pairs={{0,4},{1,5},{2,6},{3,7},{4,0},{5,1},{6,2},{7,3},{8,12},{9,13},{10,... | collective-permute-start | bytes 393224 | tf_op jit(solution)/shard_map/ppermute | solution.py:28
  55.3 7.8 %collective-permute-done.3.refs_1_ = bf16[64,1024]{1,0:T(8,128)(2,1)S(1)} collective-permute-done((bf16[64,1024]{1,0:T(8,128)(2,1)S(1)}, bf16[64,1024]{1,0:T(8,128)(2,1)S(1)}, u32[]{:S(2)}, u32[]{:S(2)}) %collective-permute-start.3) | collective-permute-done | bytes 131104 | tf_op jit(solution)/shard_map/ppermute | solution.py:28
  63.2 2.6 %collective-permute-start.8 = (bf16[64,1024]{1,0:T(8,128)(2,1)S(1)}, bf16[64,1024]{1,0:T(8,128)(2,1)S(1)}, u32[]{:S(2)}, u32[]{:S(2)}) collective-permute-start(bf16[64,1024]{1,0:T(8,128)(2,1)S(1)} %get-tuple-element.53), channel_id=1, source_target_pairs={{0,6},{1,7},{2,0},{3,1},{4,2},{5,3},{6,4},{7,5},{8,14},{9,15},{10,... | collective-permute-start | bytes 393224 | tf_op jit(solution)/shard_map/ppermute | solution.py:28
  65.8 2.2 %collective-permute-start.9 = (bf16[64,1024]{1,0:T(8,128)(2,1)S(1)}, bf16[64,1024]{1,0:T(8,128)(2,1)S(1)}, u32[]{:S(2)}, u32[]{:S(2)}) collective-permute-start(bf16[64,1024]{1,0:T(8,128)(2,1)S(1)} %get-tuple-element.54), channel_id=1, source_target_pairs={{0,7},{1,0},{2,1},{3,2},{4,3},{5,4},{6,5},{7,6},{8,15},{9,8},{10,9... | collective-permute-start | bytes 393224 | tf_op jit(solution)/shard_map/ppermute | solution.py:28
  68.0 1.5 collective-permute-done.7.refs_5_
  69.5 1.2 collective-permute-done.8.refs_6_
  70.9 1.8 shard_map.67
  72.8 1.4 collective-permute-start.10
  74.2 1.5 collective-permute-start.11
  75.9 2.2 %copy-done.1 = bf16[2,1024,1024]{2,1,0:T(8,128)(2,1)S(1)} copy-done((bf16[2,1024,1024]{2,1,0:T(8,128)(2,1)S(1)}, bf16[2,1024,1024]{2,1,0:T(8,128)(2,1)}, u32[]{:S(2)}) %copy-start.1) | copy-done | bytes 4194328
  78.1 1.8 shard_map.72
  79.9 3.1 %collective-permute-start.23 = (bf16[128,1024]{1,0:T(8,128)(2,1)S(1)}, bf16[128,1024]{1,0:T(8,128)(2,1)S(1)}, u32[]{:S(2)}, u32[]{:S(2)}) collective-permute-start(bf16[128,1024]{1,0:T(8,128)(2,1)S(1)} %get-tuple-element.68), channel_id=1, source_target_pairs={{0,192},{64,0},{128,64},{192,128},{1,193},{65,1},{129,65},{193,129... | collective-permute-start | bytes 786440 | tf_op jit(solution)/shard_map/ppermute | solution.py:28
  83.0 0.9 collective-permute-start.24
  83.8 0.9 collective-permute-start.25
  84.7 6.3 %collective-permute-done.12 = bf16[128,1024]{1,0:T(8,128)(2,1)S(1)} collective-permute-done((bf16[128,1024]{1,0:T(8,128)(2,1)S(1)}, bf16[128,1024]{1,0:T(8,128)(2,1)S(1)}, u32[]{:S(2)}, u32[]{:S(2)}) %collective-permute-start.12) | collective-permute-done | bytes 262176 | tf_op jit(solution)/shard_map/ppermute | solution.py:28
  91.3 1.5 collective-permute-start.14
  92.8 2.2 %collective-permute-start.13 = (bf16[128,1024]{1,0:T(8,128)(2,1)S(1)}, bf16[128,1024]{1,0:T(8,128)(2,1)S(1)}, u32[]{:S(2)}, u32[]{:S(2)}) collective-permute-start(bf16[128,1024]{1,0:T(8,128)(2,1)S(1)} %multiply_convert_fusion.1.refs_0_), channel_id=1, source_target_pairs={{0,64},{64,128},{128,192},{192,0},{1,65},{65,129},{129,193},{193,1... | collective-permute-start | bytes 786440 | tf_op jit(solution)/shard_map/ppermute | solution.py:28
  95.7 6.4 %collective-permute-done.25 = bf16[128,1024]{1,0:T(8,128)(2,1)S(1)} collective-permute-done((bf16[128,1024]{1,0:T(8,128)(2,1)S(1)}, bf16[128,1024]{1,0:T(8,128)(2,1)S(1)}, u32[]{:S(2)}, u32[]{:S(2)}) %collective-permute-start.25) | collective-permute-done | bytes 262176 | tf_op jit(solution)/shard_map/ppermute | solution.py:28
  102.5 1.5 collective-permute-start.27
  104.0 2.2 %collective-permute-start.26 = (bf16[128,1024]{1,0:T(8,128)(2,1)S(1)}, bf16[128,1024]{1,0:T(8,128)(2,1)S(1)}, u32[]{:S(2)}, u32[]{:S(2)}) collective-permute-start(bf16[128,1024]{1,0:T(8,128)(2,1)S(1)} %multiply_convert_fusion.refs_0_), channel_id=1, source_target_pairs={{0,64},{64,128},{128,192},{192,0},{1,65},{65,129},{129,193},{193,1... | collective-permute-start | bytes 786440 | tf_op jit(solution)/shard_map/ppermute | solution.py:28
  106.3 0.8 collective-permute-done.14.refs_2_
  107.0 6.3 %collective-permute-done.13.refs_1_ = bf16[128,1024]{1,0:T(8,128)(2,1)S(1)} collective-permute-done((bf16[128,1024]{1,0:T(8,128)(2,1)S(1)}, bf16[128,1024]{1,0:T(8,128)(2,1)S(1)}, u32[]{:S(2)}, u32[]{:S(2)}) %collective-permute-start.13) | collective-permute-done | bytes 262176 | tf_op jit(solution)/shard_map/ppermute | solution.py:28
  113.4 2.8 %shard_map.68 = bf16[8,2,32,1024]{3,2,1,0:T(8,128)(2,1)} custom-call(s32[3]{0:T(128)S(1)} %pad_add_fusion.me_ref, bf16[2,1024,1024]{2,1,0:T(8,128)(2,1)S(1)} %copy-done.2, bf16[128,1024]{1,0:T(8,128)(2,1)S(1)} %multiply_convert_fusion.1.refs_0_, bf16[128,1024]{1,0:T(8,128)(2,1)S(1)} %collective-permute-done.13.refs_1_, ...), custom_call_target="tpu_custom_call" | custom-call | flops 4294967296 | bytes 6291456 | tf_op jit(solution)/shard_map/pallas_call | solution.py:34
  116.2 5.4 %all-to-all-start.1 = ((bf16[8,64,1024]{2,1,0:T(8,128)(2,1)}), bf16[8,64,1024]{2,1,0:T(8,128)(2,1)S(1)}, u32[]{:S(2)}, u32[]{:S(2)}) async-start(bf16[8,64,1024]{2,1,0:T(8,128)(2,1)} %bitcast.7), calls=%async_computation.1 | async-start | bytes 2097152 | tf_op jit(solution)/shard_map/all_to_all | solution.py:347
  121.6 2.6 %collective-permute-done.26.refs_1_ = bf16[128,1024]{1,0:T(8,128)(2,1)S(1)} collective-permute-done((bf16[128,1024]{1,0:T(8,128)(2,1)S(1)}, bf16[128,1024]{1,0:T(8,128)(2,1)S(1)}, u32[]{:S(2)}, u32[]{:S(2)}) %collective-permute-start.26) | collective-permute-done | bytes 262176 | tf_op jit(solution)/shard_map/ppermute | solution.py:28
  124.2 2.2 %copy-done.3 = bf16[2,1024,1024]{2,1,0:T(8,128)(2,1)S(1)} copy-done((bf16[2,1024,1024]{2,1,0:T(8,128)(2,1)S(1)}, bf16[2,1024,1024]{2,1,0:T(8,128)(2,1)}, u32[]{:S(2)}) %copy-start.3) | copy-done | bytes 4194328
  126.4 1.9 %shard_map.73 = (bf16[64,1024]{1,0:T(8,128)(2,1)S(1)}, bf16[64,1024]{1,0:T(8,128)(2,1)S(1)}, bf16[64,1024]{1,0:T(8,128)(2,1)S(1)}, bf16[64,1024]{1,0:T(8,128)(2,...) custom-call(s32[3]{0:T(128)S(1)} %pad_add_fusion.me_ref, ...), custom_call_target="tpu_custom_call" | custom-call | flops 4294967296 | bytes 6291456 | tf_op jit(solution)/shard_map/pallas_call | solution.py:34
  128.4 1.7 collective-permute-start.30
  130.1 1.4 shard_map.66
  131.6 2.0 %collective-permute-start.31 = (bf16[64,1024]{1,0:T(8,128)(2,1)S(1)}, bf16[64,1024]{1,0:T(8,128)(2,1)S(1)}, u32[]{:S(2)}, u32[]{:S(2)}) collective-permute-start(bf16[64,1024]{1,0:T(8,128)(2,1)S(1)} %get-tuple-element.74), channel_id=1, source_target_pairs={{0,3},{1,4},{2,5},{3,6},{4,7},{5,0},{6,1},{7,2},{8,11},{9,12},{10,... | collective-permute-start | bytes 393224 | tf_op jit(solution)/shard_map/ppermute | solution.py:28
  133.6 1.3 collective-permute-start.32
  134.9 2.0 %collective-permute-start.33 = (bf16[64,1024]{1,0:T(8,128)(2,1)S(1)}, bf16[64,1024]{1,0:T(8,128)(2,1)S(1)}, u32[]{:S(2)}, u32[]{:S(2)}) collective-permute-start(bf16[64,1024]{1,0:T(8,128)(2,1)S(1)} %get-tuple-element.76), channel_id=1, source_target_pairs={{0,5},{1,6},{2,7},{3,0},{4,1},{5,2},{6,3},{7,4},{8,13},{9,14},{10,... | collective-permute-start | bytes 393224 | tf_op jit(solution)/shard_map/ppermute | solution.py:28
  137.0 3.3 %collective-permute-start.34 = (bf16[64,1024]{1,0:T(8,128)(2,1)S(1)}, bf16[64,1024]{1,0:T(8,128)(2,1)S(1)}, u32[]{:S(2)}, u32[]{:S(2)}) collective-permute-start(bf16[64,1024]{1,0:T(8,128)(2,1)S(1)} %get-tuple-element.77), channel_id=1, source_target_pairs={{0,6},{1,7},{2,0},{3,1},{4,2},{5,3},{6,4},{7,5},{8,14},{9,15},{10,... | collective-permute-start | bytes 393224 | tf_op jit(solution)/shard_map/ppermute | solution.py:28
  140.3 3.0 %collective-permute-start.35 = (bf16[64,1024]{1,0:T(8,128)(2,1)S(1)}, bf16[64,1024]{1,0:T(8,128)(2,1)S(1)}, u32[]{:S(2)}, u32[]{:S(2)}) collective-permute-start(bf16[64,1024]{1,0:T(8,128)(2,1)S(1)} %get-tuple-element.78), channel_id=1, source_target_pairs={{0,7},{1,0},{2,1},{3,2},{4,3},{5,4},{6,5},{7,6},{8,15},{9,8},{10,9... | collective-permute-start | bytes 393224 | tf_op jit(solution)/shard_map/ppermute | solution.py:28
  143.3 1.4 shard_map.71
  145.8 1.2 shard_map.74
  147.0 1.2 collective-permute-start.36
  148.2 1.2 shard_map.69
  149.4 0.8 collective-permute-start.16
  150.2 1.3 collective-permute-start.17
  151.5 3.7 %collective-permute-start.18 = (bf16[64,1024]{1,0:T(8,128)(2,1)S(1)}, bf16[64,1024]{1,0:T(8,128)(2,1)S(1)}, u32[]{:S(2)}, u32[]{:S(2)}) collective-permute-start(bf16[64,1024]{1,0:T(8,128)(2,1)S(1)} %get-tuple-element.62), channel_id=1, source_target_pairs={{0,32},{8,40},{16,48},{24,56},{32,0},{40,8},{48,16},{56,24},{1,33}... | collective-permute-start | bytes 393224 | tf_op jit(solution)/shard_map/ppermute | solution.py:28
  155.8 2.3 %collective-permute-start.37 = (bf16[64,1024]{1,0:T(8,128)(2,1)S(1)}, bf16[64,1024]{1,0:T(8,128)(2,1)S(1)}, u32[]{:S(2)}, u32[]{:S(2)}) collective-permute-start(bf16[64,1024]{1,0:T(8,128)(2,1)S(1)} %add_convert_fusion.2), channel_id=1, source_target_pairs={{0,48},{8,56},{16,0},{24,8},{32,16},{40,24},{48,32},{56,40},{1,49}... | collective-permute-start | bytes 393224 | tf_op jit(solution)/shard_map/ppermute | solution.py:28
  158.1 8.2 %collective-permute-done.38 = bf16[64,1024]{1,0:T(8,128)(2,1)S(1)} collective-permute-done((bf16[64,1024]{1,0:T(8,128)(2,1)S(1)}, bf16[64,1024]{1,0:T(8,128)(2,1)S(1)}, u32[]{:S(2)}, u32[]{:S(2)}) %collective-permute-start.38) | collective-permute-done | bytes 131104 | tf_op jit(solution)/shard_map/ppermute | solution.py:28
  166.4 1.3 collective-permute-start.39
  167.7 1.7 collective-permute-done.37
  169.4 6.8 %collective-permute-done.39 = bf16[64,1024]{1,0:T(8,128)(2,1)S(1)} collective-permute-done((bf16[64,1024]{1,0:T(8,128)(2,1)S(1)}, bf16[64,1024]{1,0:T(8,128)(2,1)S(1)}, u32[]{:S(2)}, u32[]{:S(2)}) %collective-permute-start.39) | collective-permute-done | bytes 131104 | tf_op jit(solution)/shard_map/ppermute | solution.py:28
  176.3 8.5 %all_to_all.21 = bf16[4,16,1024]{2,1,0:T(8,128)(2,1)S(1)} all-to-all(bf16[4,16,1024]{2,1,0:T(8,128)(2,1)S(1)} %bitcast.25), channel_id=1, replica_groups=mesh['dp'=4,'z'=8,'yc'=8] {'dp'}, dimensions={0} | all-to-all | bytes 262144 | tf_op jit(solution)/shard_map/all_to_all | solution.py:364
  (56 shorter events, 8.9 us)
Async XLA Ops:
  0.0 0.9 copy-start.4
  0.9 0.7 copy-start.5
  1.6 0.7 copy-start.6
  2.3 0.7 copy-start.7
  13.9 13.2 %collective-permute-start.2 = (bf16[64,1152]{1,0:T(8,128)(2,1)S(1)}, bf16[64,1152]{1,0:T(8,128)(2,1)S(1)}, u32[]{:S(2)}, u32[]{:S(2)}) collective-permute-start(bf16[64,1152]{1,0:T(8,128)(2,1)S(1)} %bitcast.17), channel_id=1, source_target_pairs={{0,32},{8,40},{16,48},{24,56},{32,0},{40,8},{48,16},{56,24},{1,33}... | collective-permute-start | bytes 442376 | tf_op jit(solution)/shard_map/ppermute | solution.py:28
  21.1 10.9 %collective-permute-start.1 = (bf16[64,1152]{1,0:T(8,128)(2,1)S(1)}, bf16[64,1152]{1,0:T(8,128)(2,1)S(1)}, u32[]{:S(2)}, u32[]{:S(2)}) collective-permute-start(bf16[64,1152]{1,0:T(8,128)(2,1)S(1)} %bitcast.18), channel_id=1, source_target_pairs={{0,56},{8,0},{16,8},{24,16},{32,24},{40,32},{48,40},{56,48},{1,57}... | collective-permute-start | bytes 442376 | tf_op jit(solution)/shard_map/ppermute | solution.py:28
  21.2 12.2 %collective-permute-start = (bf16[64,1152]{1,0:T(8,128)(2,1)S(1)}, bf16[64,1152]{1,0:T(8,128)(2,1)S(1)}, u32[]{:S(2)}, u32[]{:S(2)}) collective-permute-start(bf16[64,1152]{1,0:T(8,128)(2,1)S(1)} %bitcast.19), channel_id=1, source_target_pairs={{0,8},{8,16},{16,24},{24,32},{32,40},{40,48},{48,56},{56,0},{1,9},... | collective-permute-start | bytes 442376 | tf_op jit(solution)/shard_map/ppermute | solution.py:28
  27.0 7.5 %collective-permute-start.22 = (bf16[64,1152]{1,0:T(8,128)(2,1)S(1)}, bf16[64,1152]{1,0:T(8,128)(2,1)S(1)}, u32[]{:S(2)}, u32[]{:S(2)}) collective-permute-start(bf16[64,1152]{1,0:T(8,128)(2,1)S(1)} %collective-permute-done.2.refs_3_), channel_id=1, source_target_pairs={{0,8},{8,16},{16,24},{24,32},{32,40},{40,48},{48,56},{56,0},{1,9},... | collective-permute-start | bytes 442376 | tf_op jit(solution)/shard_map/ppermute | solution.py:28
  28.1 7.6 %collective-permute-start.21 = (bf16[64,1152]{1,0:T(8,128)(2,1)S(1)}, bf16[64,1152]{1,0:T(8,128)(2,1)S(1)}, u32[]{:S(2)}, u32[]{:S(2)}) collective-permute-start(bf16[64,1152]{1,0:T(8,128)(2,1)S(1)} %collective-permute-done.2.refs_3_), channel_id=1, source_target_pairs={{0,56},{8,0},{16,8},{24,16},{32,24},{40,32},{48,40},{56,48},{1,57}... | collective-permute-start | bytes 442376 | tf_op jit(solution)/shard_map/ppermute | solution.py:28
  31.9 5.2 %collective-permute-start.20 = (bf16[64,1152]{1,0:T(8,128)(2,1)S(1)}, bf16[64,1152]{1,0:T(8,128)(2,1)S(1)}, u32[]{:S(2)}, u32[]{:S(2)}) collective-permute-start(bf16[64,1152]{1,0:T(8,128)(2,1)S(1)} %collective-permute-done.1.refs_2_), channel_id=1, source_target_pairs={{0,56},{8,0},{16,8},{24,16},{32,24},{40,32},{48,40},{56,48},{1,57}... | collective-permute-start | bytes 442376 | tf_op jit(solution)/shard_map/ppermute | solution.py:28
  33.4 6.4 %collective-permute-start.19 = (bf16[64,1152]{1,0:T(8,128)(2,1)S(1)}, bf16[64,1152]{1,0:T(8,128)(2,1)S(1)}, u32[]{:S(2)}, u32[]{:S(2)}) collective-permute-start(bf16[64,1152]{1,0:T(8,128)(2,1)S(1)} %collective-permute-done.refs_1_), channel_id=1, source_target_pairs={{0,8},{8,16},{16,24},{24,32},{32,40},{40,48},{48,56},{56,0},{1,9},... | collective-permute-start | bytes 442376 | tf_op jit(solution)/shard_map/ppermute | solution.py:28
  42.8 33.1 %all-to-all-start.2 = ((bf16[8,64,1024]{2,1,0:T(8,128)(2,1)}), bf16[8,64,1024]{2,1,0:T(8,128)(2,1)S(1)}, u32[]{:S(2)}, u32[]{:S(2)}) async-start(bf16[8,64,1024]{2,1,0:T(8,128)(2,1)} %bitcast.9), calls=%async_computation.2 | async-start | bytes 2097152 | tf_op jit(solution)/shard_map/all_to_all | solution.py:309
  47.7 23.2 %copy-start = (bf16[2,1024,1024]{2,1,0:T(8,128)(2,1)S(1)}, bf16[2,1024,1024]{2,1,0:T(8,128)(2,1)}, u32[]{:S(2)}) copy-start(bf16[2,1024,1024]{2,1,0:T(8,128)(2,1)} %weight_ref.6) | copy-start | bytes 12582916
  49.8 13.4 %collective-permute-start.3 = (bf16[64,1024]{1,0:T(8,128)(2,1)S(1)}, bf16[64,1024]{1,0:T(8,128)(2,1)S(1)}, u32[]{:S(2)}, u32[]{:S(2)}) collective-permute-start(bf16[64,1024]{1,0:T(8,128)(2,1)S(1)} %get-tuple-element.48), channel_id=1, source_target_pairs={{0,1},{1,2},{2,3},{3,4},{4,5},{5,6},{6,7},{7,0},{8,9},{9,10},{10,1... | collective-permute-start | bytes 393224 | tf_op jit(solution)/shard_map/ppermute | solution.py:28
  49.9 15.8 %collective-permute-start.4 = (bf16[64,1024]{1,0:T(8,128)(2,1)S(1)}, bf16[64,1024]{1,0:T(8,128)(2,1)S(1)}, u32[]{:S(2)}, u32[]{:S(2)}) collective-permute-start(bf16[64,1024]{1,0:T(8,128)(2,1)S(1)} %get-tuple-element.49), channel_id=1, source_target_pairs={{0,2},{1,3},{2,4},{3,5},{4,6},{5,7},{6,0},{7,1},{8,10},{9,11},{10,... | collective-permute-start | bytes 393224 | tf_op jit(solution)/shard_map/ppermute | solution.py:28
  51.4 16.6 %collective-permute-start.5 = (bf16[64,1024]{1,0:T(8,128)(2,1)S(1)}, bf16[64,1024]{1,0:T(8,128)(2,1)S(1)}, u32[]{:S(2)}, u32[]{:S(2)}) collective-permute-start(bf16[64,1024]{1,0:T(8,128)(2,1)S(1)} %get-tuple-element.50), channel_id=1, source_target_pairs={{0,3},{1,4},{2,5},{3,6},{4,7},{5,0},{6,1},{7,2},{8,11},{9,12},{10,... | collective-permute-start | bytes 393224 | tf_op jit(solution)/shard_map/ppermute | solution.py:28
  52.2 15.8 %collective-permute-start.6 = (bf16[64,1024]{1,0:T(8,128)(2,1)S(1)}, bf16[64,1024]{1,0:T(8,128)(2,1)S(1)}, u32[]{:S(2)}, u32[]{:S(2)}) collective-permute-start(bf16[64,1024]{1,0:T(8,128)(2,1)S(1)} %get-tuple-element.51), channel_id=1, source_target_pairs={{0,4},{1,5},{2,6},{3,7},{4,0},{5,1},{6,2},{7,3},{8,12},{9,13},{10,... | collective-permute-start | bytes 393224 | tf_op jit(solution)/shard_map/ppermute | solution.py:28
  54.8 14.7 %collective-permute-start.7 = (bf16[64,1024]{1,0:T(8,128)(2,1)S(1)}, bf16[64,1024]{1,0:T(8,128)(2,1)S(1)}, u32[]{:S(2)}, u32[]{:S(2)}) collective-permute-start(bf16[64,1024]{1,0:T(8,128)(2,1)S(1)} %get-tuple-element.52), channel_id=1, source_target_pairs={{0,5},{1,6},{2,7},{3,0},{4,1},{5,2},{6,3},{7,4},{8,13},{9,14},{10,... | collective-permute-start | bytes 393224 | tf_op jit(solution)/shard_map/ppermute | solution.py:28
  63.2 7.5 %collective-permute-start.8 = (bf16[64,1024]{1,0:T(8,128)(2,1)S(1)}, bf16[64,1024]{1,0:T(8,128)(2,1)S(1)}, u32[]{:S(2)}, u32[]{:S(2)}) collective-permute-start(bf16[64,1024]{1,0:T(8,128)(2,1)S(1)} %get-tuple-element.53), channel_id=1, source_target_pairs={{0,6},{1,7},{2,0},{3,1},{4,2},{5,3},{6,4},{7,5},{8,14},{9,15},{10,... | collective-permute-start | bytes 393224 | tf_op jit(solution)/shard_map/ppermute | solution.py:28
  65.8 5.2 %collective-permute-start.9 = (bf16[64,1024]{1,0:T(8,128)(2,1)S(1)}, bf16[64,1024]{1,0:T(8,128)(2,1)S(1)}, u32[]{:S(2)}, u32[]{:S(2)}) collective-permute-start(bf16[64,1024]{1,0:T(8,128)(2,1)S(1)} %get-tuple-element.54), channel_id=1, source_target_pairs={{0,7},{1,0},{2,1},{3,2},{4,3},{5,4},{6,5},{7,6},{8,15},{9,8},{10,9... | collective-permute-start | bytes 393224 | tf_op jit(solution)/shard_map/ppermute | solution.py:28
  72.8 11.1 %collective-permute-start.10 = (bf16[128,1024]{1,0:T(8,128)(2,1)S(1)}, bf16[128,1024]{1,0:T(8,128)(2,1)S(1)}, u32[]{:S(2)}, u32[]{:S(2)}) collective-permute-start(bf16[128,1024]{1,0:T(8,128)(2,1)S(1)} %get-tuple-element.56), channel_id=1, source_target_pairs={{0,192},{64,0},{128,64},{192,128},{1,193},{65,1},{129,65},{193,129... | collective-permute-start | bytes 786440 | tf_op jit(solution)/shard_map/ppermute | solution.py:28
  74.2 10.5 %collective-permute-start.11 = (bf16[128,1024]{1,0:T(8,128)(2,1)S(1)}, bf16[128,1024]{1,0:T(8,128)(2,1)S(1)}, u32[]{:S(2)}, u32[]{:S(2)}) collective-permute-start(bf16[128,1024]{1,0:T(8,128)(2,1)S(1)} %get-tuple-element.57), channel_id=1, source_target_pairs={{0,128},{64,192},{128,0},{192,64},{1,129},{65,193},{129,1},{193,65... | collective-permute-start | bytes 786440 | tf_op jit(solution)/shard_map/ppermute | solution.py:28
  75.7 15.3 %collective-permute-start.12 = (bf16[128,1024]{1,0:T(8,128)(2,1)S(1)}, bf16[128,1024]{1,0:T(8,128)(2,1)S(1)}, u32[]{:S(2)}, u32[]{:S(2)}) collective-permute-start(bf16[128,1024]{1,0:T(8,128)(2,1)S(1)} %get-tuple-element.58), channel_id=1, source_target_pairs={{0,64},{64,128},{128,192},{192,0},{1,65},{65,129},{129,193},{193,1... | collective-permute-start | bytes 786440 | tf_op jit(solution)/shard_map/ppermute | solution.py:28
  75.9 2.2 %copy-start.1 = (bf16[2,1024,1024]{2,1,0:T(8,128)(2,1)S(1)}, bf16[2,1024,1024]{2,1,0:T(8,128)(2,1)}, u32[]{:S(2)}) copy-start(bf16[2,1024,1024]{2,1,0:T(8,128)(2,1)} %weight_ref.6) | copy-start | bytes 12582916
  78.1 35.3 %copy-start.2 = (bf16[2,1024,1024]{2,1,0:T(8,128)(2,1)S(1)}, bf16[2,1024,1024]{2,1,0:T(8,128)(2,1)}, u32[]{:S(2)}) copy-start(bf16[2,1024,1024]{2,1,0:T(8,128)(2,1)} %weight_ref.7) | copy-start | bytes 12582916
  79.9 12.9 %collective-permute-start.23 = (bf16[128,1024]{1,0:T(8,128)(2,1)S(1)}, bf16[128,1024]{1,0:T(8,128)(2,1)S(1)}, u32[]{:S(2)}, u32[]{:S(2)}) collective-permute-start(bf16[128,1024]{1,0:T(8,128)(2,1)S(1)} %get-tuple-element.68), channel_id=1, source_target_pairs={{0,192},{64,0},{128,64},{192,128},{1,193},{65,1},{129,65},{193,129... | collective-permute-start | bytes 786440 | tf_op jit(solution)/shard_map/ppermute | solution.py:28
  83.0 12.8 %collective-permute-start.24 = (bf16[128,1024]{1,0:T(8,128)(2,1)S(1)}, bf16[128,1024]{1,0:T(8,128)(2,1)S(1)}, u32[]{:S(2)}, u32[]{:S(2)}) collective-permute-start(bf16[128,1024]{1,0:T(8,128)(2,1)S(1)} %get-tuple-element.69), channel_id=1, source_target_pairs={{0,128},{64,192},{128,0},{192,64},{1,129},{65,193},{129,1},{193,65... | collective-permute-start | bytes 786440 | tf_op jit(solution)/shard_map/ppermute | solution.py:28
  83.8 18.3 %collective-permute-start.25 = (bf16[128,1024]{1,0:T(8,128)(2,1)S(1)}, bf16[128,1024]{1,0:T(8,128)(2,1)S(1)}, u32[]{:S(2)}, u32[]{:S(2)}) collective-permute-start(bf16[128,1024]{1,0:T(8,128)(2,1)S(1)} %get-tuple-element.70), channel_id=1, source_target_pairs={{0,64},{64,128},{128,192},{192,0},{1,65},{65,129},{129,193},{193,1... | collective-permute-start | bytes 786440 | tf_op jit(solution)/shard_map/ppermute | solution.py:28
  91.2 12.8 %collective-permute-start.15 = (bf16[128,1024]{1,0:T(8,128)(2,1)S(1)}, bf16[128,1024]{1,0:T(8,128)(2,1)S(1)}, u32[]{:S(2)}, u32[]{:S(2)}) collective-permute-start(bf16[128,1024]{1,0:T(8,128)(2,1)S(1)} %multiply_convert_fusion.1.refs_0_), channel_id=1, source_target_pairs={{0,192},{64,0},{128,64},{192,128},{1,193},{65,1},{129,65},{193,129... | collective-permute-start | bytes 786440 | tf_op jit(solution)/shard_map/ppermute | solution.py:28
  91.3 15.7 %collective-permute-start.14 = (bf16[128,1024]{1,0:T(8,128)(2,1)S(1)}, bf16[128,1024]{1,0:T(8,128)(2,1)S(1)}, u32[]{:S(2)}, u32[]{:S(2)}) collective-permute-start(bf16[128,1024]{1,0:T(8,128)(2,1)S(1)} %multiply_convert_fusion.1.refs_0_), channel_id=1, source_target_pairs={{0,128},{64,192},{128,0},{192,64},{1,129},{65,193},{129,1},{193,65... | collective-permute-start | bytes 786440 | tf_op jit(solution)/shard_map/ppermute | solution.py:28
  92.8 20.5 %collective-permute-start.13 = (bf16[128,1024]{1,0:T(8,128)(2,1)S(1)}, bf16[128,1024]{1,0:T(8,128)(2,1)S(1)}, u32[]{:S(2)}, u32[]{:S(2)}) collective-permute-start(bf16[128,1024]{1,0:T(8,128)(2,1)S(1)} %multiply_convert_fusion.1.refs_0_), channel_id=1, source_target_pairs={{0,64},{64,128},{128,192},{192,0},{1,65},{65,129},{129,193},{193,1... | collective-permute-start | bytes 786440 | tf_op jit(solution)/shard_map/ppermute | solution.py:28
  102.4 19.2 %collective-permute-start.28 = (bf16[128,1024]{1,0:T(8,128)(2,1)S(1)}, bf16[128,1024]{1,0:T(8,128)(2,1)S(1)}, u32[]{:S(2)}, u32[]{:S(2)}) collective-permute-start(bf16[128,1024]{1,0:T(8,128)(2,1)S(1)} %multiply_convert_fusion.refs_0_), channel_id=1, source_target_pairs={{0,192},{64,0},{128,64},{192,128},{1,193},{65,1},{129,65},{193,129... | collective-permute-start | bytes 786440 | tf_op jit(solution)/shard_map/ppermute | solution.py:28
  102.5 19.2 %collective-permute-start.27 = (bf16[128,1024]{1,0:T(8,128)(2,1)S(1)}, bf16[128,1024]{1,0:T(8,128)(2,1)S(1)}, u32[]{:S(2)}, u32[]{:S(2)}) collective-permute-start(bf16[128,1024]{1,0:T(8,128)(2,1)S(1)} %multiply_convert_fusion.refs_0_), channel_id=1, source_target_pairs={{0,128},{64,192},{128,0},{192,64},{1,129},{65,193},{129,1},{193,65... | collective-permute-start | bytes 786440 | tf_op jit(solution)/shard_map/ppermute | solution.py:28
  104.0 20.2 %collective-permute-start.26 = (bf16[128,1024]{1,0:T(8,128)(2,1)S(1)}, bf16[128,1024]{1,0:T(8,128)(2,1)S(1)}, u32[]{:S(2)}, u32[]{:S(2)}) collective-permute-start(bf16[128,1024]{1,0:T(8,128)(2,1)S(1)} %multiply_convert_fusion.refs_0_), channel_id=1, source_target_pairs={{0,64},{64,128},{128,192},{192,0},{1,65},{65,129},{129,193},{193,1... | collective-permute-start | bytes 786440 | tf_op jit(solution)/shard_map/ppermute | solution.py:28
  116.2 32.0 %all-to-all-start.1 = ((bf16[8,64,1024]{2,1,0:T(8,128)(2,1)}), bf16[8,64,1024]{2,1,0:T(8,128)(2,1)S(1)}, u32[]{:S(2)}, u32[]{:S(2)}) async-start(bf16[8,64,1024]{2,1,0:T(8,128)(2,1)} %bitcast.7), calls=%async_computation.1 | async-start | bytes 2097152 | tf_op jit(solution)/shard_map/all_to_all | solution.py:347
  124.2 2.2 %copy-start.3 = (bf16[2,1024,1024]{2,1,0:T(8,128)(2,1)S(1)}, bf16[2,1024,1024]{2,1,0:T(8,128)(2,1)}, u32[]{:S(2)}) copy-start(bf16[2,1024,1024]{2,1,0:T(8,128)(2,1)} %weight_ref.7) | copy-start | bytes 12582916
  128.3 8.8 %collective-permute-start.29 = (bf16[64,1024]{1,0:T(8,128)(2,1)S(1)}, bf16[64,1024]{1,0:T(8,128)(2,1)S(1)}, u32[]{:S(2)}, u32[]{:S(2)}) collective-permute-start(bf16[64,1024]{1,0:T(8,128)(2,1)S(1)} %get-tuple-element.72), channel_id=1, source_target_pairs={{0,1},{1,2},{2,3},{3,4},{4,5},{5,6},{6,7},{7,0},{8,9},{9,10},{10,1... | collective-permute-start | bytes 393224 | tf_op jit(solution)/shard_map/ppermute | solution.py:28
  128.4 11.9 %collective-permute-start.30 = (bf16[64,1024]{1,0:T(8,128)(2,1)S(1)}, bf16[64,1024]{1,0:T(8,128)(2,1)S(1)}, u32[]{:S(2)}, u32[]{:S(2)}) collective-permute-start(bf16[64,1024]{1,0:T(8,128)(2,1)S(1)} %get-tuple-element.73), channel_id=1, source_target_pairs={{0,2},{1,3},{2,4},{3,5},{4,6},{5,7},{6,0},{7,1},{8,10},{9,11},{10,... | collective-permute-start | bytes 393224 | tf_op jit(solution)/shard_map/ppermute | solution.py:28
  131.6 13.1 %collective-permute-start.31 = (bf16[64,1024]{1,0:T(8,128)(2,1)S(1)}, bf16[64,1024]{1,0:T(8,128)(2,1)S(1)}, u32[]{:S(2)}, u32[]{:S(2)}) collective-permute-start(bf16[64,1024]{1,0:T(8,128)(2,1)S(1)} %get-tuple-element.74), channel_id=1, source_target_pairs={{0,3},{1,4},{2,5},{3,6},{4,7},{5,0},{6,1},{7,2},{8,11},{9,12},{10,... | collective-permute-start | bytes 393224 | tf_op jit(solution)/shard_map/ppermute | solution.py:28
  133.6 11.1 %collective-permute-start.32 = (bf16[64,1024]{1,0:T(8,128)(2,1)S(1)}, bf16[64,1024]{1,0:T(8,128)(2,1)S(1)}, u32[]{:S(2)}, u32[]{:S(2)}) collective-permute-start(bf16[64,1024]{1,0:T(8,128)(2,1)S(1)} %get-tuple-element.75), channel_id=1, source_target_pairs={{0,4},{1,5},{2,6},{3,7},{4,0},{5,1},{6,2},{7,3},{8,12},{9,13},{10,... | collective-permute-start | bytes 393224 | tf_op jit(solution)/shard_map/ppermute | solution.py:28
  134.9 9.9 %collective-permute-start.33 = (bf16[64,1024]{1,0:T(8,128)(2,1)S(1)}, bf16[64,1024]{1,0:T(8,128)(2,1)S(1)}, u32[]{:S(2)}, u32[]{:S(2)}) collective-permute-start(bf16[64,1024]{1,0:T(8,128)(2,1)S(1)} %get-tuple-element.76), channel_id=1, source_target_pairs={{0,5},{1,6},{2,7},{3,0},{4,1},{5,2},{6,3},{7,4},{8,13},{9,14},{10,... | collective-permute-start | bytes 393224 | tf_op jit(solution)/shard_map/ppermute | solution.py:28
  137.0 8.2 %collective-permute-start.34 = (bf16[64,1024]{1,0:T(8,128)(2,1)S(1)}, bf16[64,1024]{1,0:T(8,128)(2,1)S(1)}, u32[]{:S(2)}, u32[]{:S(2)}) collective-permute-start(bf16[64,1024]{1,0:T(8,128)(2,1)S(1)} %get-tuple-element.77), channel_id=1, source_target_pairs={{0,6},{1,7},{2,0},{3,1},{4,2},{5,3},{6,4},{7,5},{8,14},{9,15},{10,... | collective-permute-start | bytes 393224 | tf_op jit(solution)/shard_map/ppermute | solution.py:28
  140.3 5.5 %collective-permute-start.35 = (bf16[64,1024]{1,0:T(8,128)(2,1)S(1)}, bf16[64,1024]{1,0:T(8,128)(2,1)S(1)}, u32[]{:S(2)}, u32[]{:S(2)}) collective-permute-start(bf16[64,1024]{1,0:T(8,128)(2,1)S(1)} %get-tuple-element.78), channel_id=1, source_target_pairs={{0,7},{1,0},{2,1},{3,2},{4,3},{5,4},{6,5},{7,6},{8,15},{9,8},{10,9... | collective-permute-start | bytes 393224 | tf_op jit(solution)/shard_map/ppermute | solution.py:28
  147.0 8.8 %collective-permute-start.36 = (bf16[64,1024]{1,0:T(8,128)(2,1)S(1)}, bf16[64,1024]{1,0:T(8,128)(2,1)S(1)}, u32[]{:S(2)}, u32[]{:S(2)}) collective-permute-start(bf16[64,1024]{1,0:T(8,128)(2,1)S(1)} %get-tuple-element.79), channel_id=1, source_target_pairs={{0,56},{8,0},{16,8},{24,16},{32,24},{40,32},{48,40},{56,48},{1,57}... | collective-permute-start | bytes 393224 | tf_op jit(solution)/shard_map/ppermute | solution.py:28
  149.4 18.3 %collective-permute-start.16 = (bf16[64,1024]{1,0:T(8,128)(2,1)S(1)}, bf16[64,1024]{1,0:T(8,128)(2,1)S(1)}, u32[]{:S(2)}, u32[]{:S(2)}) collective-permute-start(bf16[64,1024]{1,0:T(8,128)(2,1)S(1)} %get-tuple-element.60), channel_id=1, source_target_pairs={{0,56},{8,0},{16,8},{24,16},{32,24},{40,32},{48,40},{56,48},{1,57}... | collective-permute-start | bytes 393224 | tf_op jit(solution)/shard_map/ppermute | solution.py:28
  150.2 17.5 %collective-permute-start.17 = (bf16[64,1024]{1,0:T(8,128)(2,1)S(1)}, bf16[64,1024]{1,0:T(8,128)(2,1)S(1)}, u32[]{:S(2)}, u32[]{:S(2)}) collective-permute-start(bf16[64,1024]{1,0:T(8,128)(2,1)S(1)} %get-tuple-element.61), channel_id=1, source_target_pairs={{0,8},{8,16},{16,24},{24,32},{32,40},{40,48},{48,56},{56,0},{1,9},... | collective-permute-start | bytes 393224 | tf_op jit(solution)/shard_map/ppermute | solution.py:28
  151.5 16.2 %collective-permute-start.18 = (bf16[64,1024]{1,0:T(8,128)(2,1)S(1)}, bf16[64,1024]{1,0:T(8,128)(2,1)S(1)}, u32[]{:S(2)}, u32[]{:S(2)}) collective-permute-start(bf16[64,1024]{1,0:T(8,128)(2,1)S(1)} %get-tuple-element.62), channel_id=1, source_target_pairs={{0,32},{8,40},{16,48},{24,56},{32,0},{40,8},{48,16},{56,24},{1,33}... | collective-permute-start | bytes 393224 | tf_op jit(solution)/shard_map/ppermute | solution.py:28
  155.3 11.1 %collective-permute-start.38 = (bf16[64,1024]{1,0:T(8,128)(2,1)S(1)}, bf16[64,1024]{1,0:T(8,128)(2,1)S(1)}, u32[]{:S(2)}, u32[]{:S(2)}) collective-permute-start(bf16[64,1024]{1,0:T(8,128)(2,1)S(1)} %get-tuple-element.81), channel_id=1, source_target_pairs={{0,8},{8,16},{16,24},{24,32},{32,40},{40,48},{48,56},{56,0},{1,9},... | collective-permute-start | bytes 393224 | tf_op jit(solution)/shard_map/ppermute | solution.py:28
  155.8 13.6 %collective-permute-start.37 = (bf16[64,1024]{1,0:T(8,128)(2,1)S(1)}, bf16[64,1024]{1,0:T(8,128)(2,1)S(1)}, u32[]{:S(2)}, u32[]{:S(2)}) collective-permute-start(bf16[64,1024]{1,0:T(8,128)(2,1)S(1)} %add_convert_fusion.2), channel_id=1, source_target_pairs={{0,48},{8,56},{16,0},{24,8},{32,16},{40,24},{48,32},{56,40},{1,49}... | collective-permute-start | bytes 393224 | tf_op jit(solution)/shard_map/ppermute | solution.py:28
  166.4 9.8 %collective-permute-start.39 = (bf16[64,1024]{1,0:T(8,128)(2,1)S(1)}, bf16[64,1024]{1,0:T(8,128)(2,1)S(1)}, u32[]{:S(2)}, u32[]{:S(2)}) collective-permute-start(bf16[64,1024]{1,0:T(8,128)(2,1)S(1)} %add_convert_fusion.1), channel_id=1, source_target_pairs={{0,16},{8,24},{16,32},{24,40},{32,48},{40,56},{48,0},{56,8},{1,17}... | collective-permute-start | bytes 393224 | tf_op jit(solution)/shard_map/ppermute | solution.py:28

commit v4 on v3

--- a/solution.py
+++ b/solution.py
@@ -349,13 +349,12 @@
         sums = local_call(
             functools.partial(combine_kernel, len(back)),
             [high, low] + back,
-            [jax.ShapeDtypeStruct((dp_rows, part_width), F32 if offset in (0, 2, -2) else BF) for offset in offsets],
+            [jax.ShapeDtypeStruct((dp_rows, part_width), BF if offset else F32) for offset in offsets],
         )
         sums = dict(zip(offsets, sums))
         if n:
-            for way in (1, -1):
-                passed = shift(sums[3 * way], "z", -way).astype(F32) + sums[2 * way]
-                total = total + shift(passed.astype(BF), "z", -2 * way).astype(F32)
+            for offset in offsets:
+                total = total + shift(sums[offset], "z", -offset).astype(F32)
         else:
             total = sums[0]
             for offset in offsets[1:]:

time: 186 us -> 178 us (0.957); the launches traced: 185 us -> 175 us
  starting transfers between devices: 76.5 us -> 66.1 us
  waiting for transfers between devices: 62 us -> 59.1 us
    ppermute x40, starting transfers between devices: 66.1 us -> 56.9 us  [shift(): lax.ppermute(value, axis, [(source, (source + steps) % count) for source...]
    ppermute x40, waiting for transfers between devices: 62 us -> 59.1 us  [shift(): lax.ppermute(value, axis, [(source, (source + steps) % count) for source...]
    unnamed x16 -> x24, local copies, waits for them, and re-layouts: 7.31 us -> 8.99 us
  transfers between devices with their start and end apart: 42 -> 42, of which waited for: 22 -> 14; matrix products, arithmetic and copies ran while one was open for 0% -> 1% of each run, Pallas kernels for 8% -> 10%
where the time goes in v4:
time: 178 us; the launch traced here: 175 us
  starting transfers between devices  66.1 us (37%)
  waiting for transfers between devices  59.1 us (33%)
  Pallas kernels  19.6 us (11%)
  blocking collectives  18.7 us (11%)
  local copies, waits for them, and re-layouts  9.66 us (5%)
    ppermute x40, waiting for transfers between devices, shift(): lax.ppermute(value, axis, [(source, (source + steps) % count) for source...  59.1 us
    ppermute x40, starting transfers between devices, shift(): lax.ppermute(value, axis, [(source, (source + steps) % count) for source...  56.9 us
    pallas_call x11, Pallas kernels, local_call(): pl.pallas_call(kernel, in_specs=[pl.BlockSpec(memory_space=pltpu.SMEM)] *...  19.6 us
    all_to_all x1, blocking collectives, layer(): own = lax.all_to_all(payload, 'dp', 0, 0, tiled=True).reshape(dp_rows, full)  10.2 us
    unnamed x24, local copies, waits for them, and re-layouts  8.99 us
    all_to_all x1, blocking collectives, layer(): parts = lax.all_to_all(parts, 'dp', 0, 0, tiled=True)  8.52 us
    all_to_all x1, starting transfers between devices, layer(): lax.all_to_all(rows[0].reshape(cells, cell_rows, part_width), 'yc', 0, 0,...  4.81 us
    all_to_all x1, starting transfers between devices, layer(): lax.all_to_all(result[0].reshape(cells, cell_rows, part_width), 'yc', 0,...  4.41 us
  transfers between devices with their start and end apart: 42, of which 14 were waited for; matrix products, arithmetic and copies ran while one was open for 1% of the time, Pallas kernels for 10%

profile of v4, /device:TPU:8, one launch (start us, length us, event | category | flops | bytes accessed | tf_op | source)
XLA Modules:
  0.0 175.1 jit_solution(6781155216781623406)
XLA Ops:
  0.0 0.9 copy-done.4
  0.9 0.7 copy-done.5
  2.9 0.8 shard_map.64
  3.7 10.2 %all_to_all.20 = bf16[4,16,1152]{2,1,0:T(8,128)(2,1)S(1)} all-to-all(bf16[4,16,1152]{2,1,0:T(8,128)(2,1)S(1)} %shard_map.64), channel_id=1, replica_groups=mesh['dp'=4,'z'=8,'yc'=8] {'dp'}, dimensions={0} | all-to-all | bytes 294912 | tf_op jit(solution)/shard_map/all_to_all | solution.py:275
  13.9 7.2 %collective-permute-start.2 = (bf16[64,1152]{1,0:T(8,128)(2,1)S(1)}, bf16[64,1152]{1,0:T(8,128)(2,1)S(1)}, u32[]{:S(2)}, u32[]{:S(2)}) collective-permute-start(bf16[64,1152]{1,0:T(8,128)(2,1)S(1)} %bitcast.17), channel_id=1, source_target_pairs={{0,32},{8,40},{16,48},{24,56},{32,0},{40,8},{48,16},{56,24},{1,33}... | collective-permute-start | bytes 442376 | tf_op jit(solution)/shard_map/ppermute | solution.py:28
  21.2 1.9 %collective-permute-start = (bf16[64,1152]{1,0:T(8,128)(2,1)S(1)}, bf16[64,1152]{1,0:T(8,128)(2,1)S(1)}, u32[]{:S(2)}, u32[]{:S(2)}) collective-permute-start(bf16[64,1152]{1,0:T(8,128)(2,1)S(1)} %bitcast.19), channel_id=1, source_target_pairs={{0,8},{8,16},{16,24},{24,32},{32,40},{40,48},{48,56},{56,0},{1,9},... | collective-permute-start | bytes 442376 | tf_op jit(solution)/shard_map/ppermute | solution.py:28
  23.2 3.6 %collective-permute-done.2.refs_3_ = bf16[64,1152]{1,0:T(8,128)(2,1)S(1)} collective-permute-done((bf16[64,1152]{1,0:T(8,128)(2,1)S(1)}, bf16[64,1152]{1,0:T(8,128)(2,1)S(1)}, u32[]{:S(2)}, u32[]{:S(2)}) %collective-permute-start.2) | collective-permute-done | bytes 147488 | tf_op jit(solution)/shard_map/ppermute | solution.py:28
  26.8 3.8 %collective-permute-done.1.refs_2_ = bf16[64,1152]{1,0:T(8,128)(2,1)S(1)} collective-permute-done((bf16[64,1152]{1,0:T(8,128)(2,1)S(1)}, bf16[64,1152]{1,0:T(8,128)(2,1)S(1)}, u32[]{:S(2)}, u32[]{:S(2)}) %collective-permute-start.1) | collective-permute-done | bytes 147488 | tf_op jit(solution)/shard_map/ppermute | solution.py:28
  30.6 2.1 %shard_map.65 = (bf16[64,1024]{1,0:T(8,128)(2,1)S(1)}, bf16[64,1024]{1,0:T(8,128)(2,1)S(1)}, bf16[64,1024]{1,0:T(8,128)(2,1)S(1)}, bf16[64,1024]{1,0:T(8,128)(2,...) custom-call(s32[3]{0:T(128)S(1)} %pad_add_fusion.me_ref, ...), custom_call_target="tpu_custom_call" | custom-call | flops 4294967296 | bytes 1703936 | tf_op jit(solution)/shard_map/pallas_call | solution.py:34
  33.0 3.0 %collective-permute-start.21 = (bf16[64,1152]{1,0:T(8,128)(2,1)S(1)}, bf16[64,1152]{1,0:T(8,128)(2,1)S(1)}, u32[]{:S(2)}, u32[]{:S(2)}) collective-permute-start(bf16[64,1152]{1,0:T(8,128)(2,1)S(1)} %collective-permute-done.2.refs_3_), channel_id=1, source_target_pairs={{0,56},{8,0},{16,8},{24,16},{32,24},{40,32},{48,40},{56,48},{1,57}... | collective-permute-start | bytes 442376 | tf_op jit(solution)/shard_map/ppermute | solution.py:28
  36.0 1.0 collective-permute-start.20
  37.0 1.1 collective-permute-start.19
  38.1 1.6 collective-permute-start.4
  39.6 4.3 %collective-permute-done.4.refs_2_ = bf16[64,1024]{1,0:T(8,128)(2,1)S(1)} collective-permute-done((bf16[64,1024]{1,0:T(8,128)(2,1)S(1)}, bf16[64,1024]{1,0:T(8,128)(2,1)S(1)}, u32[]{:S(2)}, u32[]{:S(2)}) %collective-permute-start.4) | collective-permute-done | bytes 131104 | tf_op jit(solution)/shard_map/ppermute | solution.py:28
  44.2 2.5 %collective-permute-start.6 = (bf16[64,1024]{1,0:T(8,128)(2,1)S(1)}, bf16[64,1024]{1,0:T(8,128)(2,1)S(1)}, u32[]{:S(2)}, u32[]{:S(2)}) collective-permute-start(bf16[64,1024]{1,0:T(8,128)(2,1)S(1)} %get-tuple-element.51), channel_id=1, source_target_pairs={{0,4},{1,5},{2,6},{3,7},{4,0},{5,1},{6,2},{7,3},{8,12},{9,13},{10,... | collective-permute-start | bytes 393224 | tf_op jit(solution)/shard_map/ppermute | solution.py:28
  46.7 1.6 collective-permute-start.7
  48.3 2.0 %collective-permute-start.8 = (bf16[64,1024]{1,0:T(8,128)(2,1)S(1)}, bf16[64,1024]{1,0:T(8,128)(2,1)S(1)}, u32[]{:S(2)}, u32[]{:S(2)}) collective-permute-start(bf16[64,1024]{1,0:T(8,128)(2,1)S(1)} %get-tuple-element.53), channel_id=1, source_target_pairs={{0,6},{1,7},{2,0},{3,1},{4,2},{5,3},{6,4},{7,5},{8,14},{9,15},{10,... | collective-permute-start | bytes 393224 | tf_op jit(solution)/shard_map/ppermute | solution.py:28
  50.3 3.0 %shard_map.70 = (bf16[512,1024]{1,0:T(8,128)(2,1)}, bf16[256,128]{1,0:T(8,128)(2,1)S(1)}) custom-call(s32[3]{0:T(128)S(1)} %pad_add_fusion.me_ref, bf16[64,1152]{1,0:T(8,128)(2,1)S(1)} %collective-permute-done.19.refs_0_, bf16[64,1152]{1,0:T(8,128)(2,1)S(1)} %collective-permute-done.20.refs_1_, bf16[64,1152]{1,0:T(8,128)(2,1)S(1)} %collective-permute-done.21.refs_2_, ...), custom_call_target="tpu_custom_call" | custom-call | flops 4294967296 | bytes 1703936 | tf_op jit(solution)/shard_map/pallas_call | solution.py:34
  53.3 4.8 %all-to-all-start.2 = ((bf16[8,64,1024]{2,1,0:T(8,128)(2,1)}), bf16[8,64,1024]{2,1,0:T(8,128)(2,1)S(1)}, u32[]{:S(2)}, u32[]{:S(2)}) async-start(bf16[8,64,1024]{2,1,0:T(8,128)(2,1)} %bitcast.9), calls=%async_computation.2 | async-start | bytes 2097152 | tf_op jit(solution)/shard_map/all_to_all | solution.py:309
  58.2 2.2 %copy-done = bf16[2,1024,1024]{2,1,0:T(8,128)(2,1)S(1)} copy-done((bf16[2,1024,1024]{2,1,0:T(8,128)(2,1)S(1)}, bf16[2,1024,1024]{2,1,0:T(8,128)(2,1)}, u32[]{:S(2)}) %copy-start) | copy-done | bytes 4194328
  60.4 1.8 %shard_map.67 = (f32[128,1024]{1,0:T(8,128)S(1)}, bf16[128,1024]{1,0:T(8,128)(2,1)S(1)}, bf16[128,1024]{1,0:T(8,128)(2,1)S(1)}, bf16[128,1024]{1,0:T(8,128)(2,1)S(1)}) custom-call(s32[3]{0:T(128)S(1)} %pad_add_fusion.me_ref, bf16[2,1024,1024]{2,1,0:T(8,128)(2,1)S(1)} %copy-done, bf16[64,1024]{1,0:T(8,128)(2,1)S(1)} %get-tuple-element.47.refs_0_, ...), custom_call_target="tpu_custom_call" | custom-call | flops 4294967296 | bytes 6553600 | tf_op jit(solution)/shard_map/pallas_call | solution.py:34
  62.2 1.4 collective-permute-start.10
  63.6 1.5 collective-permute-start.11
  65.3 6.0 %collective-permute-done.10 = bf16[128,1024]{1,0:T(8,128)(2,1)S(1)} collective-permute-done((bf16[128,1024]{1,0:T(8,128)(2,1)S(1)}, bf16[128,1024]{1,0:T(8,128)(2,1)S(1)}, u32[]{:S(2)}, u32[]{:S(2)}) %collective-permute-start.10) | collective-permute-done | bytes 262176 | tf_op jit(solution)/shard_map/ppermute | solution.py:28
  71.3 3.1 %collective-permute-done.11 = bf16[128,1024]{1,0:T(8,128)(2,1)S(1)} collective-permute-done((bf16[128,1024]{1,0:T(8,128)(2,1)S(1)}, bf16[128,1024]{1,0:T(8,128)(2,1)S(1)}, u32[]{:S(2)}, u32[]{:S(2)}) %collective-permute-start.11) | collective-permute-done | bytes 262176 | tf_op jit(solution)/shard_map/ppermute | solution.py:28
  74.4 5.6 %collective-permute-done.12 = bf16[128,1024]{1,0:T(8,128)(2,1)S(1)} collective-permute-done((bf16[128,1024]{1,0:T(8,128)(2,1)S(1)}, bf16[128,1024]{1,0:T(8,128)(2,1)S(1)}, u32[]{:S(2)}, u32[]{:S(2)}) %collective-permute-start.12) | collective-permute-done | bytes 262176 | tf_op jit(solution)/shard_map/ppermute | solution.py:28
  80.8 1.5 collective-permute-start.14
  82.2 0.9 collective-permute-start.13
  83.1 2.2 %copy-done.1 = bf16[2,1024,1024]{2,1,0:T(8,128)(2,1)S(1)} copy-done((bf16[2,1024,1024]{2,1,0:T(8,128)(2,1)S(1)}, bf16[2,1024,1024]{2,1,0:T(8,128)(2,1)}, u32[]{:S(2)}) %copy-start.1) | copy-done | bytes 4194328
  85.3 1.8 %shard_map.72 = (f32[128,1024]{1,0:T(8,128)S(1)}, bf16[128,1024]{1,0:T(8,128)(2,1)S(1)}, bf16[128,1024]{1,0:T(8,128)(2,1)S(1)}, bf16[128,1024]{1,0:T(8,128)(2,1)S(1)}) custom-call(s32[3]{0:T(128)S(1)} %pad_add_fusion.me_ref, bf16[2,1024,1024]{2,1,0:T(8,128)(2,1)S(1)} %copy-done.1, bf16[8,2,32,1024]{3,2,1,0:T(8,128)(2,1)S(1)} %bitcast.16), custom_call_target="tpu_custom_call" | custom-call | flops 4294967296 | bytes 6553600 | tf_op jit(solution)/shard_map/pallas_call | solution.py:34
  87.1 2.4 %collective-permute-start.23 = (bf16[128,1024]{1,0:T(8,128)(2,1)S(1)}, bf16[128,1024]{1,0:T(8,128)(2,1)}, u32[]{:S(2)}, u32[]{:S(2)}) collective-permute-start(bf16[128,1024]{1,0:T(8,128)(2,1)S(1)} %get-tuple-element.68), channel_id=1, source_target_pairs={{0,192},{64,0},{128,64},{192,128},{1,193},{65,1},{129,65},{193,129... | collective-permute-start | bytes 786440 | tf_op jit(solution)/shard_map/ppermute | solution.py:28
  89.5 1.0 collective-permute-start.24
  90.6 1.3 collective-permute-start.25
  91.9 5.3 %collective-permute-done.13.refs_1_ = bf16[128,1024]{1,0:T(8,128)(2,1)S(1)} collective-permute-done((bf16[128,1024]{1,0:T(8,128)(2,1)S(1)}, bf16[128,1024]{1,0:T(8,128)(2,1)S(1)}, u32[]{:S(2)}, u32[]{:S(2)}) %collective-permute-start.13) | collective-permute-done | bytes 262176 | tf_op jit(solution)/shard_map/ppermute | solution.py:28
  97.2 2.8 %shard_map.68 = bf16[8,2,32,1024]{3,2,1,0:T(8,128)(2,1)} custom-call(s32[3]{0:T(128)S(1)} %pad_add_fusion.me_ref, bf16[2,1024,1024]{2,1,0:T(8,128)(2,1)S(1)} %copy-done.2, bf16[128,1024]{1,0:T(8,128)(2,1)S(1)} %multiply_convert_fusion.1.refs_0_, bf16[128,1024]{1,0:T(8,128)(2,1)S(1)} %collective-permute-done.13.refs_1_, ...), custom_call_target="tpu_custom_call" | custom-call | flops 4294967296 | bytes 6291456 | tf_op jit(solution)/shard_map/pallas_call | solution.py:34
  100.0 4.4 %all-to-all-start.1 = ((bf16[8,64,1024]{2,1,0:T(8,128)(2,1)}), bf16[8,64,1024]{2,1,0:T(8,128)(2,1)S(1)}, u32[]{:S(2)}, u32[]{:S(2)}) async-start(bf16[8,64,1024]{2,1,0:T(8,128)(2,1)} %bitcast.7), calls=%async_computation.1 | async-start | bytes 2097152 | tf_op jit(solution)/shard_map/all_to_all | solution.py:347
  104.4 2.8 %collective-permute-done.25 = bf16[128,1024]{1,0:T(8,128)(2,1)} collective-permute-done((bf16[128,1024]{1,0:T(8,128)(2,1)S(1)}, bf16[128,1024]{1,0:T(8,128)(2,1)}, u32[]{:S(2)}, u32[]{:S(2)}) %collective-permute-start.25) | collective-permute-done | bytes 262176 | tf_op jit(solution)/shard_map/ppermute | solution.py:28
  107.3 1.3 multiply_convert_fusion.refs_0_
  108.6 1.0 collective-permute-start.28
  109.6 1.2 collective-permute-start.27
  110.8 0.8 collective-permute-start.26
  111.6 1.4 shard_map.66
  113.0 0.7 copy-done.8
  113.8 4.1 %collective-permute-done.28.refs_3_ = bf16[128,1024]{1,0:T(8,128)(2,1)S(1)} collective-permute-done((bf16[128,1024]{1,0:T(8,128)(2,1)S(1)}, bf16[128,1024]{1,0:T(8,128)(2,1)S(1)}, u32[]{:S(2)}, u32[]{:S(2)}) %collective-permute-start.28) | collective-permute-done | bytes 262176 | tf_op jit(solution)/shard_map/ppermute | solution.py:28
  117.9 2.5 %collective-permute-done.27.refs_2_ = bf16[128,1024]{1,0:T(8,128)(2,1)S(1)} collective-permute-done((bf16[128,1024]{1,0:T(8,128)(2,1)S(1)}, bf16[128,1024]{1,0:T(8,128)(2,1)S(1)}, u32[]{:S(2)}, u32[]{:S(2)}) %collective-permute-start.27) | collective-permute-done | bytes 262176 | tf_op jit(solution)/shard_map/ppermute | solution.py:28
  120.4 3.8 %collective-permute-done.26.refs_1_ = bf16[128,1024]{1,0:T(8,128)(2,1)S(1)} collective-permute-done((bf16[128,1024]{1,0:T(8,128)(2,1)S(1)}, bf16[128,1024]{1,0:T(8,128)(2,1)S(1)}, u32[]{:S(2)}, u32[]{:S(2)}) %collective-permute-start.26) | collective-permute-done | bytes 262176 | tf_op jit(solution)/shard_map/ppermute | solution.py:28
  124.2 1.9 %shard_map.73 = (bf16[64,1024]{1,0:T(8,128)(2,1)S(1)}, bf16[64,1024]{1,0:T(8,128)(2,1)S(1)}, bf16[64,1024]{1,0:T(8,128)(2,1)S(1)}, bf16[64,1024]{1,0:T(8,128)(2,...) custom-call(s32[3]{0:T(128)S(1)} %pad_add_fusion.me_ref, ...), custom_call_target="tpu_custom_call" | custom-call | flops 4294967296 | bytes 6291456 | tf_op jit(solution)/shard_map/pallas_call | solution.py:34
  126.5 1.4 shard_map.71
  128.0 1.9 %collective-permute-start.31 = (bf16[64,1024]{1,0:T(8,128)(2,1)S(1)}, bf16[64,1024]{1,0:T(8,128)(2,1)S(1)}, u32[]{:S(2)}, u32[]{:S(2)}) collective-permute-start(bf16[64,1024]{1,0:T(8,128)(2,1)S(1)} %get-tuple-element.74), channel_id=1, source_target_pairs={{0,3},{1,4},{2,5},{3,6},{4,7},{5,0},{6,1},{7,2},{8,11},{9,12},{10,... | collective-permute-start | bytes 393224 | tf_op jit(solution)/shard_map/ppermute | solution.py:28
  129.9 1.6 collective-permute-start.32
  131.5 1.4 collective-permute-start.33
  132.9 2.1 %collective-permute-start.34 = (bf16[64,1024]{1,0:T(8,128)(2,1)S(1)}, bf16[64,1024]{1,0:T(8,128)(2,1)S(1)}, u32[]{:S(2)}, u32[]{:S(2)}) collective-permute-start(bf16[64,1024]{1,0:T(8,128)(2,1)S(1)} %get-tuple-element.77), channel_id=1, source_target_pairs={{0,6},{1,7},{2,0},{3,1},{4,2},{5,3},{6,4},{7,5},{8,14},{9,15},{10,... | collective-permute-start | bytes 393224 | tf_op jit(solution)/shard_map/ppermute | solution.py:28
  135.1 0.9 copy-done.9
  136.0 1.2 shard_map.69
  137.2 2.2 %collective-permute-start.16 = (bf16[64,1024]{1,0:T(8,128)(2,1)S(1)}, bf16[64,1024]{1,0:T(8,128)(2,1)S(1)}, u32[]{:S(2)}, u32[]{:S(2)}) collective-permute-start(bf16[64,1024]{1,0:T(8,128)(2,1)S(1)} %get-tuple-element.60), channel_id=1, source_target_pairs={{0,56},{8,0},{16,8},{24,16},{32,24},{40,32},{48,40},{56,48},{1,57}... | collective-permute-start | bytes 393224 | tf_op jit(solution)/shard_map/ppermute | solution.py:28
  139.5 1.5 collective-permute-done.33.refs_5_
  141.0 4.0 %collective-permute-start.18 = (bf16[64,1024]{1,0:T(8,128)(2,1)S(1)}, bf16[64,1024]{1,0:T(8,128)(2,1)S(1)}, u32[]{:S(2)}, u32[]{:S(2)}) collective-permute-start(bf16[64,1024]{1,0:T(8,128)(2,1)S(1)} %get-tuple-element.62), channel_id=1, source_target_pairs={{0,32},{8,40},{16,48},{24,56},{32,0},{40,8},{48,16},{56,24},{1,33}... | collective-permute-start | bytes 393224 | tf_op jit(solution)/shard_map/ppermute | solution.py:28
  145.0 1.2 shard_map.74
  146.3 2.9 %collective-permute-start.37 = (bf16[64,1024]{1,0:T(8,128)(2,1)S(1)}, bf16[64,1024]{1,0:T(8,128)(2,1)S(1)}, u32[]{:S(2)}, u32[]{:S(2)}) collective-permute-start(bf16[64,1024]{1,0:T(8,128)(2,1)S(1)} %get-tuple-element.80), channel_id=1, source_target_pairs={{0,16},{8,24},{16,32},{24,40},{32,48},{40,56},{48,0},{56,8},{1,17}... | collective-permute-start | bytes 393224 | tf_op jit(solution)/shard_map/ppermute | solution.py:28
  149.2 1.2 collective-permute-start.38
  150.4 2.6 %collective-permute-start.39 = (bf16[64,1024]{1,0:T(8,128)(2,1)S(1)}, bf16[64,1024]{1,0:T(8,128)(2,1)S(1)}, u32[]{:S(2)}, u32[]{:S(2)}) collective-permute-start(bf16[64,1024]{1,0:T(8,128)(2,1)S(1)} %get-tuple-element.82), channel_id=1, source_target_pairs={{0,24},{8,32},{16,40},{24,48},{32,56},{40,0},{48,8},{56,16},{1,25}... | collective-permute-start | bytes 393224 | tf_op jit(solution)/shard_map/ppermute | solution.py:28
  153.1 6.6 %collective-permute-done.36 = bf16[64,1024]{1,0:T(8,128)(2,1)S(1)} collective-permute-done((bf16[64,1024]{1,0:T(8,128)(2,1)S(1)}, bf16[64,1024]{1,0:T(8,128)(2,1)S(1)}, u32[]{:S(2)}, u32[]{:S(2)}) %collective-permute-start.36) | collective-permute-done | bytes 131104 | tf_op jit(solution)/shard_map/ppermute | solution.py:28
  159.6 6.1 %collective-permute-done.38 = bf16[64,1024]{1,0:T(8,128)(2,1)S(1)} collective-permute-done((bf16[64,1024]{1,0:T(8,128)(2,1)S(1)}, bf16[64,1024]{1,0:T(8,128)(2,1)S(1)}, u32[]{:S(2)}, u32[]{:S(2)}) %collective-permute-start.38) | collective-permute-done | bytes 131104 | tf_op jit(solution)/shard_map/ppermute | solution.py:28
  165.9 8.5 %all_to_all.21 = bf16[4,16,1024]{2,1,0:T(8,128)(2,1)S(1)} all-to-all(bf16[4,16,1024]{2,1,0:T(8,128)(2,1)S(1)} %bitcast.24), channel_id=1, replica_groups=mesh['dp'=4,'z'=8,'yc'=8] {'dp'}, dimensions={0} | all-to-all | bytes 262144 | tf_op jit(solution)/shard_map/all_to_all | solution.py:363
  (62 shorter events, 4.6 us)
Async XLA Ops:
  0.0 0.9 copy-start.4
  0.9 0.7 copy-start.5
  1.6 0.7 copy-start.6
  2.3 0.7 copy-start.7
  13.9 12.9 %collective-permute-start.2 = (bf16[64,1152]{1,0:T(8,128)(2,1)S(1)}, bf16[64,1152]{1,0:T(8,128)(2,1)S(1)}, u32[]{:S(2)}, u32[]{:S(2)}) collective-permute-start(bf16[64,1152]{1,0:T(8,128)(2,1)S(1)} %bitcast.17), channel_id=1, source_target_pairs={{0,32},{8,40},{16,48},{24,56},{32,0},{40,8},{48,16},{56,24},{1,33}... | collective-permute-start | bytes 442376 | tf_op jit(solution)/shard_map/ppermute | solution.py:28
  21.1 9.5 %collective-permute-start.1 = (bf16[64,1152]{1,0:T(8,128)(2,1)S(1)}, bf16[64,1152]{1,0:T(8,128)(2,1)S(1)}, u32[]{:S(2)}, u32[]{:S(2)}) collective-permute-start(bf16[64,1152]{1,0:T(8,128)(2,1)S(1)} %bitcast.18), channel_id=1, source_target_pairs={{0,56},{8,0},{16,8},{24,16},{32,24},{40,32},{48,40},{56,48},{1,57}... | collective-permute-start | bytes 442376 | tf_op jit(solution)/shard_map/ppermute | solution.py:28
  21.2 9.4 %collective-permute-start = (bf16[64,1152]{1,0:T(8,128)(2,1)S(1)}, bf16[64,1152]{1,0:T(8,128)(2,1)S(1)}, u32[]{:S(2)}, u32[]{:S(2)}) collective-permute-start(bf16[64,1152]{1,0:T(8,128)(2,1)S(1)} %bitcast.19), channel_id=1, source_target_pairs={{0,8},{8,16},{16,24},{24,32},{32,40},{40,48},{48,56},{56,0},{1,9},... | collective-permute-start | bytes 442376 | tf_op jit(solution)/shard_map/ppermute | solution.py:28
  32.7 5.4 %collective-permute-start.3 = (bf16[64,1024]{1,0:T(8,128)(2,1)S(1)}, bf16[64,1024]{1,0:T(8,128)(2,1)S(1)}, u32[]{:S(2)}, u32[]{:S(2)}) collective-permute-start(bf16[64,1024]{1,0:T(8,128)(2,1)S(1)} %get-tuple-element.48), channel_id=1, source_target_pairs={{0,1},{1,2},{2,3},{3,4},{4,5},{5,6},{6,7},{7,0},{8,9},{9,10},{10,1... | collective-permute-start | bytes 393224 | tf_op jit(solution)/shard_map/ppermute | solution.py:28
  32.7 11.4 %collective-permute-start.22 = (bf16[64,1152]{1,0:T(8,128)(2,1)S(1)}, bf16[64,1152]{1,0:T(8,128)(2,1)S(1)}, u32[]{:S(2)}, u32[]{:S(2)}) collective-permute-start(bf16[64,1152]{1,0:T(8,128)(2,1)S(1)} %collective-permute-done.2.refs_3_), channel_id=1, source_target_pairs={{0,8},{8,16},{16,24},{24,32},{32,40},{40,48},{48,56},{56,0},{1,9},... | collective-permute-start | bytes 442376 | tf_op jit(solution)/shard_map/ppermute | solution.py:28
  33.0 13.6 %collective-permute-start.21 = (bf16[64,1152]{1,0:T(8,128)(2,1)S(1)}, bf16[64,1152]{1,0:T(8,128)(2,1)S(1)}, u32[]{:S(2)}, u32[]{:S(2)}) collective-permute-start(bf16[64,1152]{1,0:T(8,128)(2,1)S(1)} %collective-permute-done.2.refs_3_), channel_id=1, source_target_pairs={{0,56},{8,0},{16,8},{24,16},{32,24},{40,32},{48,40},{56,48},{1,57}... | collective-permute-start | bytes 442376 | tf_op jit(solution)/shard_map/ppermute | solution.py:28
  36.0 12.3 %collective-permute-start.20 = (bf16[64,1152]{1,0:T(8,128)(2,1)S(1)}, bf16[64,1152]{1,0:T(8,128)(2,1)S(1)}, u32[]{:S(2)}, u32[]{:S(2)}) collective-permute-start(bf16[64,1152]{1,0:T(8,128)(2,1)S(1)} %collective-permute-done.1.refs_2_), channel_id=1, source_target_pairs={{0,56},{8,0},{16,8},{24,16},{32,24},{40,32},{48,40},{56,48},{1,57}... | collective-permute-start | bytes 442376 | tf_op jit(solution)/shard_map/ppermute | solution.py:28
  37.0 13.3 %collective-permute-start.19 = (bf16[64,1152]{1,0:T(8,128)(2,1)S(1)}, bf16[64,1152]{1,0:T(8,128)(2,1)S(1)}, u32[]{:S(2)}, u32[]{:S(2)}) collective-permute-start(bf16[64,1152]{1,0:T(8,128)(2,1)S(1)} %collective-permute-done.refs_1_), channel_id=1, source_target_pairs={{0,8},{8,16},{16,24},{24,32},{32,40},{40,48},{48,56},{56,0},{1,9},... | collective-permute-start | bytes 442376 | tf_op jit(solution)/shard_map/ppermute | solution.py:28
  38.1 5.9 %collective-permute-start.4 = (bf16[64,1024]{1,0:T(8,128)(2,1)S(1)}, bf16[64,1024]{1,0:T(8,128)(2,1)S(1)}, u32[]{:S(2)}, u32[]{:S(2)}) collective-permute-start(bf16[64,1024]{1,0:T(8,128)(2,1)S(1)} %get-tuple-element.49), channel_id=1, source_target_pairs={{0,2},{1,3},{2,4},{3,5},{4,6},{5,7},{6,0},{7,1},{8,10},{9,11},{10,... | collective-permute-start | bytes 393224 | tf_op jit(solution)/shard_map/ppermute | solution.py:28
  43.9 14.2 %collective-permute-start.5 = (bf16[64,1024]{1,0:T(8,128)(2,1)S(1)}, bf16[64,1024]{1,0:T(8,128)(2,1)S(1)}, u32[]{:S(2)}, u32[]{:S(2)}) collective-permute-start(bf16[64,1024]{1,0:T(8,128)(2,1)S(1)} %get-tuple-element.50), channel_id=1, source_target_pairs={{0,3},{1,4},{2,5},{3,6},{4,7},{5,0},{6,1},{7,2},{8,11},{9,12},{10,... | collective-permute-start | bytes 393224 | tf_op jit(solution)/shard_map/ppermute | solution.py:28
  44.2 14.0 %collective-permute-start.6 = (bf16[64,1024]{1,0:T(8,128)(2,1)S(1)}, bf16[64,1024]{1,0:T(8,128)(2,1)S(1)}, u32[]{:S(2)}, u32[]{:S(2)}) collective-permute-start(bf16[64,1024]{1,0:T(8,128)(2,1)S(1)} %get-tuple-element.51), channel_id=1, source_target_pairs={{0,4},{1,5},{2,6},{3,7},{4,0},{5,1},{6,2},{7,3},{8,12},{9,13},{10,... | collective-permute-start | bytes 393224 | tf_op jit(solution)/shard_map/ppermute | solution.py:28
  46.7 11.5 %collective-permute-start.7 = (bf16[64,1024]{1,0:T(8,128)(2,1)S(1)}, bf16[64,1024]{1,0:T(8,128)(2,1)S(1)}, u32[]{:S(2)}, u32[]{:S(2)}) collective-permute-start(bf16[64,1024]{1,0:T(8,128)(2,1)S(1)} %get-tuple-element.52), channel_id=1, source_target_pairs={{0,5},{1,6},{2,7},{3,0},{4,1},{5,2},{6,3},{7,4},{8,13},{9,14},{10,... | collective-permute-start | bytes 393224 | tf_op jit(solution)/shard_map/ppermute | solution.py:28
  48.3 9.8 %collective-permute-start.8 = (bf16[64,1024]{1,0:T(8,128)(2,1)S(1)}, bf16[64,1024]{1,0:T(8,128)(2,1)S(1)}, u32[]{:S(2)}, u32[]{:S(2)}) collective-permute-start(bf16[64,1024]{1,0:T(8,128)(2,1)S(1)} %get-tuple-element.53), channel_id=1, source_target_pairs={{0,6},{1,7},{2,0},{3,1},{4,2},{5,3},{6,4},{7,5},{8,14},{9,15},{10,... | collective-permute-start | bytes 393224 | tf_op jit(solution)/shard_map/ppermute | solution.py:28
  50.3 7.9 %collective-permute-start.9 = (bf16[64,1024]{1,0:T(8,128)(2,1)S(1)}, bf16[64,1024]{1,0:T(8,128)(2,1)S(1)}, u32[]{:S(2)}, u32[]{:S(2)}) collective-permute-start(bf16[64,1024]{1,0:T(8,128)(2,1)S(1)} %get-tuple-element.54), channel_id=1, source_target_pairs={{0,7},{1,0},{2,1},{3,2},{4,3},{5,4},{6,5},{7,6},{8,15},{9,8},{10,9... | collective-permute-start | bytes 393224 | tf_op jit(solution)/shard_map/ppermute | solution.py:28
  53.3 4.9 %copy-start.10 = (bf16[256,128]{1,0:T(8,128)(2,1)}, bf16[256,128]{1,0:T(8,128)(2,1)S(1)}, u32[]{:S(2)}) copy-start(bf16[256,128]{1,0:T(8,128)(2,1)S(1)} %get-tuple-element.63.info_ref) | copy-start | bytes 196612
  53.3 29.8 %all-to-all-start.2 = ((bf16[8,64,1024]{2,1,0:T(8,128)(2,1)}), bf16[8,64,1024]{2,1,0:T(8,128)(2,1)S(1)}, u32[]{:S(2)}, u32[]{:S(2)}) async-start(bf16[8,64,1024]{2,1,0:T(8,128)(2,1)} %bitcast.9), calls=%async_computation.2 | async-start | bytes 2097152 | tf_op jit(solution)/shard_map/all_to_all | solution.py:309
  58.2 2.2 %copy-start = (bf16[2,1024,1024]{2,1,0:T(8,128)(2,1)S(1)}, bf16[2,1024,1024]{2,1,0:T(8,128)(2,1)}, u32[]{:S(2)}) copy-start(bf16[2,1024,1024]{2,1,0:T(8,128)(2,1)} %weight_ref.6) | copy-start | bytes 12582916
  62.2 9.1 %collective-permute-start.10 = (bf16[128,1024]{1,0:T(8,128)(2,1)S(1)}, bf16[128,1024]{1,0:T(8,128)(2,1)S(1)}, u32[]{:S(2)}, u32[]{:S(2)}) collective-permute-start(bf16[128,1024]{1,0:T(8,128)(2,1)S(1)} %get-tuple-element.56), channel_id=1, source_target_pairs={{0,192},{64,0},{128,64},{192,128},{1,193},{65,1},{129,65},{193,129... | collective-permute-start | bytes 786440 | tf_op jit(solution)/shard_map/ppermute | solution.py:28
  63.6 10.7 %collective-permute-start.11 = (bf16[128,1024]{1,0:T(8,128)(2,1)S(1)}, bf16[128,1024]{1,0:T(8,128)(2,1)S(1)}, u32[]{:S(2)}, u32[]{:S(2)}) collective-permute-start(bf16[128,1024]{1,0:T(8,128)(2,1)S(1)} %get-tuple-element.57), channel_id=1, source_target_pairs={{0,128},{64,192},{128,0},{192,64},{1,129},{65,193},{129,1},{193,65... | collective-permute-start | bytes 786440 | tf_op jit(solution)/shard_map/ppermute | solution.py:28
  65.1 14.8 %collective-permute-start.12 = (bf16[128,1024]{1,0:T(8,128)(2,1)S(1)}, bf16[128,1024]{1,0:T(8,128)(2,1)S(1)}, u32[]{:S(2)}, u32[]{:S(2)}) collective-permute-start(bf16[128,1024]{1,0:T(8,128)(2,1)S(1)} %get-tuple-element.58), channel_id=1, source_target_pairs={{0,64},{64,128},{128,192},{192,0},{1,65},{65,129},{129,193},{193,1... | collective-permute-start | bytes 786440 | tf_op jit(solution)/shard_map/ppermute | solution.py:28
  80.2 10.4 %collective-permute-start.15 = (bf16[128,1024]{1,0:T(8,128)(2,1)S(1)}, bf16[128,1024]{1,0:T(8,128)(2,1)S(1)}, u32[]{:S(2)}, u32[]{:S(2)}) collective-permute-start(bf16[128,1024]{1,0:T(8,128)(2,1)S(1)} %multiply_convert_fusion.1.refs_0_), channel_id=1, source_target_pairs={{0,192},{64,0},{128,64},{192,128},{1,193},{65,1},{129,65},{193,129... | collective-permute-start | bytes 786440 | tf_op jit(solution)/shard_map/ppermute | solution.py:28
  80.8 11.1 %collective-permute-start.14 = (bf16[128,1024]{1,0:T(8,128)(2,1)S(1)}, bf16[128,1024]{1,0:T(8,128)(2,1)S(1)}, u32[]{:S(2)}, u32[]{:S(2)}) collective-permute-start(bf16[128,1024]{1,0:T(8,128)(2,1)S(1)} %multiply_convert_fusion.1.refs_0_), channel_id=1, source_target_pairs={{0,128},{64,192},{128,0},{192,64},{1,129},{65,193},{129,1},{193,65... | collective-permute-start | bytes 786440 | tf_op jit(solution)/shard_map/ppermute | solution.py:28
  82.2 14.9 %collective-permute-start.13 = (bf16[128,1024]{1,0:T(8,128)(2,1)S(1)}, bf16[128,1024]{1,0:T(8,128)(2,1)S(1)}, u32[]{:S(2)}, u32[]{:S(2)}) collective-permute-start(bf16[128,1024]{1,0:T(8,128)(2,1)S(1)} %multiply_convert_fusion.1.refs_0_), channel_id=1, source_target_pairs={{0,64},{64,128},{128,192},{192,0},{1,65},{65,129},{129,193},{193,1... | collective-permute-start | bytes 786440 | tf_op jit(solution)/shard_map/ppermute | solution.py:28
  83.1 2.2 %copy-start.1 = (bf16[2,1024,1024]{2,1,0:T(8,128)(2,1)S(1)}, bf16[2,1024,1024]{2,1,0:T(8,128)(2,1)}, u32[]{:S(2)}) copy-start(bf16[2,1024,1024]{2,1,0:T(8,128)(2,1)} %weight_ref.6) | copy-start | bytes 12582916
  85.3 11.9 %copy-start.2 = (bf16[2,1024,1024]{2,1,0:T(8,128)(2,1)S(1)}, bf16[2,1024,1024]{2,1,0:T(8,128)(2,1)}, u32[]{:S(2)}) copy-start(bf16[2,1024,1024]{2,1,0:T(8,128)(2,1)} %weight_ref.7) | copy-start | bytes 12582916
  87.1 17.3 %collective-permute-start.23 = (bf16[128,1024]{1,0:T(8,128)(2,1)S(1)}, bf16[128,1024]{1,0:T(8,128)(2,1)}, u32[]{:S(2)}, u32[]{:S(2)}) collective-permute-start(bf16[128,1024]{1,0:T(8,128)(2,1)S(1)} %get-tuple-element.68), channel_id=1, source_target_pairs={{0,192},{64,0},{128,64},{192,128},{1,193},{65,1},{129,65},{193,129... | collective-permute-start | bytes 786440 | tf_op jit(solution)/shard_map/ppermute | solution.py:28
  89.5 14.9 %collective-permute-start.24 = (bf16[128,1024]{1,0:T(8,128)(2,1)S(1)}, bf16[128,1024]{1,0:T(8,128)(2,1)}, u32[]{:S(2)}, u32[]{:S(2)}) collective-permute-start(bf16[128,1024]{1,0:T(8,128)(2,1)S(1)} %get-tuple-element.69), channel_id=1, source_target_pairs={{0,128},{64,192},{128,0},{192,64},{1,129},{65,193},{129,1},{193,65... | collective-permute-start | bytes 786440 | tf_op jit(solution)/shard_map/ppermute | solution.py:28
  90.6 16.7 %collective-permute-start.25 = (bf16[128,1024]{1,0:T(8,128)(2,1)S(1)}, bf16[128,1024]{1,0:T(8,128)(2,1)}, u32[]{:S(2)}, u32[]{:S(2)}) collective-permute-start(bf16[128,1024]{1,0:T(8,128)(2,1)S(1)} %get-tuple-element.70), channel_id=1, source_target_pairs={{0,64},{64,128},{128,192},{192,0},{1,65},{65,129},{129,193},{193,1... | collective-permute-start | bytes 786440 | tf_op jit(solution)/shard_map/ppermute | solution.py:28
  100.0 35.0 %all-to-all-start.1 = ((bf16[8,64,1024]{2,1,0:T(8,128)(2,1)}), bf16[8,64,1024]{2,1,0:T(8,128)(2,1)S(1)}, u32[]{:S(2)}, u32[]{:S(2)}) async-start(bf16[8,64,1024]{2,1,0:T(8,128)(2,1)} %bitcast.7), calls=%async_computation.1 | async-start | bytes 2097152 | tf_op jit(solution)/shard_map/all_to_all | solution.py:347
  108.6 9.3 %collective-permute-start.28 = (bf16[128,1024]{1,0:T(8,128)(2,1)S(1)}, bf16[128,1024]{1,0:T(8,128)(2,1)S(1)}, u32[]{:S(2)}, u32[]{:S(2)}) collective-permute-start(bf16[128,1024]{1,0:T(8,128)(2,1)S(1)} %multiply_convert_fusion.refs_0_), channel_id=1, source_target_pairs={{0,192},{64,0},{128,64},{192,128},{1,193},{65,1},{129,65},{193,129... | collective-permute-start | bytes 786440 | tf_op jit(solution)/shard_map/ppermute | solution.py:28
  109.6 10.7 %collective-permute-start.27 = (bf16[128,1024]{1,0:T(8,128)(2,1)S(1)}, bf16[128,1024]{1,0:T(8,128)(2,1)S(1)}, u32[]{:S(2)}, u32[]{:S(2)}) collective-permute-start(bf16[128,1024]{1,0:T(8,128)(2,1)S(1)} %multiply_convert_fusion.refs_0_), channel_id=1, source_target_pairs={{0,128},{64,192},{128,0},{192,64},{1,129},{65,193},{129,1},{193,65... | collective-permute-start | bytes 786440 | tf_op jit(solution)/shard_map/ppermute | solution.py:28
  110.8 13.3 %collective-permute-start.26 = (bf16[128,1024]{1,0:T(8,128)(2,1)S(1)}, bf16[128,1024]{1,0:T(8,128)(2,1)S(1)}, u32[]{:S(2)}, u32[]{:S(2)}) collective-permute-start(bf16[128,1024]{1,0:T(8,128)(2,1)S(1)} %multiply_convert_fusion.refs_0_), channel_id=1, source_target_pairs={{0,64},{64,128},{128,192},{192,0},{1,65},{65,129},{129,193},{193,1... | collective-permute-start | bytes 786440 | tf_op jit(solution)/shard_map/ppermute | solution.py:28
  111.6 12.6 %copy-start.3 = (bf16[2,1024,1024]{2,1,0:T(8,128)(2,1)S(1)}, bf16[2,1024,1024]{2,1,0:T(8,128)(2,1)}, u32[]{:S(2)}) copy-start(bf16[2,1024,1024]{2,1,0:T(8,128)(2,1)} %weight_ref.7) | copy-start | bytes 12582916
  113.0 0.7 copy-start.8
  113.8 12.8 %copy-start.11 = (bf16[256,128]{1,0:T(8,128)(2,1)S(1)}, bf16[256,128]{1,0:T(8,128)(2,1)}, u32[]{:S(2)}) copy-start(bf16[256,128]{1,0:T(8,128)(2,1)} %copy-done.10) | copy-start | bytes 196612
  126.0 6.9 %collective-permute-start.29 = (bf16[64,1024]{1,0:T(8,128)(2,1)S(1)}, bf16[64,1024]{1,0:T(8,128)(2,1)S(1)}, u32[]{:S(2)}, u32[]{:S(2)}) collective-permute-start(bf16[64,1024]{1,0:T(8,128)(2,1)S(1)} %get-tuple-element.72), channel_id=1, source_target_pairs={{0,1},{1,2},{2,3},{3,4},{4,5},{5,6},{6,7},{7,0},{8,9},{9,10},{10,1... | collective-permute-start | bytes 393224 | tf_op jit(solution)/shard_map/ppermute | solution.py:28
  126.1 9.0 %collective-permute-start.30 = (bf16[64,1024]{1,0:T(8,128)(2,1)S(1)}, bf16[64,1024]{1,0:T(8,128)(2,1)S(1)}, u32[]{:S(2)}, u32[]{:S(2)}) collective-permute-start(bf16[64,1024]{1,0:T(8,128)(2,1)S(1)} %get-tuple-element.73), channel_id=1, source_target_pairs={{0,2},{1,3},{2,4},{3,5},{4,6},{5,7},{6,0},{7,1},{8,10},{9,11},{10,... | collective-permute-start | bytes 393224 | tf_op jit(solution)/shard_map/ppermute | solution.py:28
  128.0 9.3 %collective-permute-start.31 = (bf16[64,1024]{1,0:T(8,128)(2,1)S(1)}, bf16[64,1024]{1,0:T(8,128)(2,1)S(1)}, u32[]{:S(2)}, u32[]{:S(2)}) collective-permute-start(bf16[64,1024]{1,0:T(8,128)(2,1)S(1)} %get-tuple-element.74), channel_id=1, source_target_pairs={{0,3},{1,4},{2,5},{3,6},{4,7},{5,0},{6,1},{7,2},{8,11},{9,12},{10,... | collective-permute-start | bytes 393224 | tf_op jit(solution)/shard_map/ppermute | solution.py:28
  129.9 9.6 %collective-permute-start.32 = (bf16[64,1024]{1,0:T(8,128)(2,1)S(1)}, bf16[64,1024]{1,0:T(8,128)(2,1)S(1)}, u32[]{:S(2)}, u32[]{:S(2)}) collective-permute-start(bf16[64,1024]{1,0:T(8,128)(2,1)S(1)} %get-tuple-element.75), channel_id=1, source_target_pairs={{0,4},{1,5},{2,6},{3,7},{4,0},{5,1},{6,2},{7,3},{8,12},{9,13},{10,... | collective-permute-start | bytes 393224 | tf_op jit(solution)/shard_map/ppermute | solution.py:28
  131.5 9.5 %collective-permute-start.33 = (bf16[64,1024]{1,0:T(8,128)(2,1)S(1)}, bf16[64,1024]{1,0:T(8,128)(2,1)S(1)}, u32[]{:S(2)}, u32[]{:S(2)}) collective-permute-start(bf16[64,1024]{1,0:T(8,128)(2,1)S(1)} %get-tuple-element.76), channel_id=1, source_target_pairs={{0,5},{1,6},{2,7},{3,0},{4,1},{5,2},{6,3},{7,4},{8,13},{9,14},{10,... | collective-permute-start | bytes 393224 | tf_op jit(solution)/shard_map/ppermute | solution.py:28
  132.9 12.1 %collective-permute-start.34 = (bf16[64,1024]{1,0:T(8,128)(2,1)S(1)}, bf16[64,1024]{1,0:T(8,128)(2,1)S(1)}, u32[]{:S(2)}, u32[]{:S(2)}) collective-permute-start(bf16[64,1024]{1,0:T(8,128)(2,1)S(1)} %get-tuple-element.77), channel_id=1, source_target_pairs={{0,6},{1,7},{2,0},{3,1},{4,2},{5,3},{6,4},{7,5},{8,14},{9,15},{10,... | collective-permute-start | bytes 393224 | tf_op jit(solution)/shard_map/ppermute | solution.py:28
  135.0 10.0 %collective-permute-start.35 = (bf16[64,1024]{1,0:T(8,128)(2,1)S(1)}, bf16[64,1024]{1,0:T(8,128)(2,1)S(1)}, u32[]{:S(2)}, u32[]{:S(2)}) collective-permute-start(bf16[64,1024]{1,0:T(8,128)(2,1)S(1)} %get-tuple-element.78), channel_id=1, source_target_pairs={{0,7},{1,0},{2,1},{3,2},{4,3},{5,4},{6,5},{7,6},{8,15},{9,8},{10,9... | collective-permute-start | bytes 393224 | tf_op jit(solution)/shard_map/ppermute | solution.py:28
  135.0 1.0 copy-start.9
  137.2 12.0 %collective-permute-start.16 = (bf16[64,1024]{1,0:T(8,128)(2,1)S(1)}, bf16[64,1024]{1,0:T(8,128)(2,1)S(1)}, u32[]{:S(2)}, u32[]{:S(2)}) collective-permute-start(bf16[64,1024]{1,0:T(8,128)(2,1)S(1)} %get-tuple-element.60), channel_id=1, source_target_pairs={{0,56},{8,0},{16,8},{24,16},{32,24},{40,32},{48,40},{56,48},{1,57}... | collective-permute-start | bytes 393224 | tf_op jit(solution)/shard_map/ppermute | solution.py:28
  139.5 11.0 %collective-permute-start.17 = (bf16[64,1024]{1,0:T(8,128)(2,1)S(1)}, bf16[64,1024]{1,0:T(8,128)(2,1)S(1)}, u32[]{:S(2)}, u32[]{:S(2)}) collective-permute-start(bf16[64,1024]{1,0:T(8,128)(2,1)S(1)} %get-tuple-element.61), channel_id=1, source_target_pairs={{0,8},{8,16},{16,24},{24,32},{32,40},{40,48},{48,56},{56,0},{1,9},... | collective-permute-start | bytes 393224 | tf_op jit(solution)/shard_map/ppermute | solution.py:28
  141.0 12.0 %collective-permute-start.18 = (bf16[64,1024]{1,0:T(8,128)(2,1)S(1)}, bf16[64,1024]{1,0:T(8,128)(2,1)S(1)}, u32[]{:S(2)}, u32[]{:S(2)}) collective-permute-start(bf16[64,1024]{1,0:T(8,128)(2,1)S(1)} %get-tuple-element.62), channel_id=1, source_target_pairs={{0,32},{8,40},{16,48},{24,56},{32,0},{40,8},{48,16},{56,24},{1,33}... | collective-permute-start | bytes 393224 | tf_op jit(solution)/shard_map/ppermute | solution.py:28
  146.2 13.4 %collective-permute-start.36 = (bf16[64,1024]{1,0:T(8,128)(2,1)S(1)}, bf16[64,1024]{1,0:T(8,128)(2,1)S(1)}, u32[]{:S(2)}, u32[]{:S(2)}) collective-permute-start(bf16[64,1024]{1,0:T(8,128)(2,1)S(1)} %get-tuple-element.79), channel_id=1, source_target_pairs={{0,48},{8,56},{16,0},{24,8},{32,16},{40,24},{48,32},{56,40},{1,49}... | collective-permute-start | bytes 393224 | tf_op jit(solution)/shard_map/ppermute | solution.py:28
  146.3 13.3 %collective-permute-start.37 = (bf16[64,1024]{1,0:T(8,128)(2,1)S(1)}, bf16[64,1024]{1,0:T(8,128)(2,1)S(1)}, u32[]{:S(2)}, u32[]{:S(2)}) collective-permute-start(bf16[64,1024]{1,0:T(8,128)(2,1)S(1)} %get-tuple-element.80), channel_id=1, source_target_pairs={{0,16},{8,24},{16,32},{24,40},{32,48},{40,56},{48,0},{56,8},{1,17}... | collective-permute-start | bytes 393224 | tf_op jit(solution)/shard_map/ppermute | solution.py:28
  149.2 16.5 %collective-permute-start.38 = (bf16[64,1024]{1,0:T(8,128)(2,1)S(1)}, bf16[64,1024]{1,0:T(8,128)(2,1)S(1)}, u32[]{:S(2)}, u32[]{:S(2)}) collective-permute-start(bf16[64,1024]{1,0:T(8,128)(2,1)S(1)} %get-tuple-element.81), channel_id=1, source_target_pairs={{0,40},{8,48},{16,56},{24,0},{32,8},{40,16},{48,24},{56,32},{1,41}... | collective-permute-start | bytes 393224 | tf_op jit(solution)/shard_map/ppermute | solution.py:28
  150.4 15.3 %collective-permute-start.39 = (bf16[64,1024]{1,0:T(8,128)(2,1)S(1)}, bf16[64,1024]{1,0:T(8,128)(2,1)S(1)}, u32[]{:S(2)}, u32[]{:S(2)}) collective-permute-start(bf16[64,1024]{1,0:T(8,128)(2,1)S(1)} %get-tuple-element.82), channel_id=1, source_target_pairs={{0,24},{8,32},{16,40},{24,48},{32,56},{40,0},{48,8},{56,16},{1,25}... | collective-permute-start | bytes 393224 | tf_op jit(solution)/shard_map/ppermute | solution.py:28
